TPU v7x, 32 devices: a whole 2x2x4 slice. The times are simulated.
32 devices in a mesh: dp: 4 (over z), expert: 8 (over y, x, core).
Axes of the slice: x: 2, y: 2, z: 4, core: 2. Of those that a mesh axis runs over, the one named last changes fastest.
Arguments:
- inputs: bfloat16 [8, 1024, 1024], P('expert', 'dp'), may hold values from -6 to 6
- cotangent: bfloat16 [8, 1024, 1024], P('expert', 'dp'), may hold values from -6 to 6
- gain_attn: bfloat16 [1024], P(('dp', 'expert')), may hold values from 0.5 to 1.5
- w_query: bfloat16 [1024, 1024], P(('dp', 'expert')), may hold values from -0.1875 to 0.1875
- w_key: bfloat16 [1024, 1024], P(('dp', 'expert')), may hold values from -0.1875 to 0.1875
- w_value: bfloat16 [1024, 1024], P(('dp', 'expert')), may hold values from -0.1875 to 0.1875
- w_out: bfloat16 [1024, 1024], P(('dp', 'expert')), may hold values from -3 to 3
- position_bias: bfloat16 [512], P(('dp', 'expert')), may hold values from -4 to 4
- gain_moe: bfloat16 [1024], P(('dp', 'expert')), may hold values from 0.5 to 1.5
- w_gate: bfloat16 [8, 1024, 2816], P('expert', 'dp'), may hold values from -0.1875 to 0.1875
- w_up: bfloat16 [8, 1024, 2816], P('expert', 'dp'), may hold values from -0.1875 to 0.1875
- w_down: bfloat16 [8, 2816, 1024], P('expert', 'dp'), may hold values from -0.21875 to 0.21875
- routes: int32 [8, 1024, 2], P('expert', 'dp'), may hold values from 0 to 7, all different within a row
- gate_fixed: int32 [8, 1024], P('expert', 'dp'), may hold values from 13107 to 52428
Outputs:
- block_out: bfloat16 [8, 1024, 1024], P('expert', 'dp')
- grad_inputs: bfloat16 [8, 1024, 1024], P('expert', 'dp')
- grad_gain_attn: float32 [1024], P(('dp', 'expert'))
- grad_w_query: float32 [1024, 1024], P(('dp', 'expert'))
- grad_w_key: float32 [1024, 1024], P(('dp', 'expert'))
- grad_w_value: float32 [1024, 1024], P(('dp', 'expert'))
- grad_w_out: float32 [1024, 1024], P(('dp', 'expert'))
- grad_position_bias: float32 [512], P(('dp', 'expert'))
- grad_gain_moe: float32 [1024], P(('dp', 'expert'))
- grad_w_gate: float32 [8, 1024, 2816], P('expert', 'dp')
- grad_w_up: float32 [8, 1024, 2816], P('expert', 'dp')
- grad_w_down: float32 [8, 2816, 1024], P('expert', 'dp')
Inputs may be any that keep to these rules, and one draw needn't show every extreme that they name: `routes`: each token names two different experts.
All inputs are finite; a program needn't handle non-finite values.
Results may differ from a plain program's by a relative error of at most 0.03.
Values may be sent and summed in bfloat16 or wider, within the bound.
A program may use at most 256 MiB of HBM per device.

v0:
```python
import jax
import jax.numpy as jnp
from jax import lax
from jax.sharding import PartitionSpec as P

HEADS = 16
HEAD_DIM = 64
BUCKETS = 32


THRESHOLDS = (12, 16, 23, 32, 46, 64, 91)
EPSILON = 1e-06
HIGHEST = lax.Precision.HIGHEST


def bucket_table(query_pos, key_pos):
    offset = key_pos[None, :] - query_pos[:, None]
    distance = jnp.abs(offset)
    banded = jnp.full(distance.shape, 8, jnp.int32)
    for cutoff in THRESHOLDS:
        banded = banded + (distance >= cutoff).astype(jnp.int32)
    nearby = jnp.where(distance < 8, distance, banded)
    return nearby + jnp.where(offset > 0, 16, 0).astype(jnp.int32)


def gelu_tanh(values):
    return jax.nn.gelu(values, approximate=True)


def norm_forward(values, gain):
    inverse = lax.rsqrt(jnp.mean(values * values, axis=-1, keepdims=True) + EPSILON)
    return (inverse, (values * inverse * gain).astype(jnp.bfloat16))


def norm_backward(values, inverse, gain, grad_normed):
    scaled = gain * grad_normed
    grad_gain = jnp.sum(grad_normed * values * inverse, axis=0)
    grad_values = inverse * scaled - values * inverse**3 * jnp.mean(
        scaled * values, axis=-1, keepdims=True
    )
    return (grad_gain, grad_values)


def expert_forward(slots_in, gate_full, up_full):
    gate_pre = jnp.einsum("esd,edf->esf", slots_in, gate_full, preferred_element_type=jnp.float32)
    up_pre = jnp.einsum("esd,edf->esf", slots_in, up_full, preferred_element_type=jnp.float32)
    return (gate_pre, up_pre)


def hidden_forward(slots_in, gate_full, up_full):
    gate_pre, up_pre = expert_forward(slots_in, gate_full, up_full)
    activated, gelu_back = jax.vjp(gelu_tanh, gate_pre)
    hidden_low = (activated * up_pre).astype(jnp.bfloat16)
    return (up_pre, activated, gelu_back, hidden_low)


def to_sources(per_expert, sources, capacity):
    local_n, _, width = per_expert.shape
    return jnp.swapaxes(per_expert.reshape(local_n, sources, capacity, width), 0, 1).reshape(
        sources * local_n, capacity, width
    )


def from_sources(received, local_n):
    sources_n, capacity, width = received.shape
    sources = sources_n // local_n
    return jnp.swapaxes(received.reshape(sources, local_n, capacity, width), 0, 1).reshape(
        local_n, sources * capacity, width
    )


def local(
    inputs,
    cotangent,
    gain_attn,
    w_query,
    w_key,
    w_value,
    w_out,
    position_bias,
    gain_moe,
    w_gate,
    w_up,
    w_down,
    routes,
    gate_fixed,
):
    gathered = (
        lax.all_gather(gain_attn, ("dp", "expert"), axis=0, tiled=True),
        lax.all_gather(w_query, ("dp", "expert"), axis=0, tiled=True),
        lax.all_gather(w_key, ("dp", "expert"), axis=0, tiled=True),
        lax.all_gather(w_value, ("dp", "expert"), axis=0, tiled=True),
        lax.all_gather(w_out, ("dp", "expert"), axis=0, tiled=True),
        lax.all_gather(position_bias, ("dp", "expert"), axis=0, tiled=True),
        lax.all_gather(gain_moe, ("dp", "expert"), axis=0, tiled=True),
    )
    gain_one = gathered[0].astype(jnp.float32)
    query_w, key_w, value_w, out_w = (gathered[1], gathered[2], gathered[3], gathered[4])
    table = gathered[5].reshape(BUCKETS, HEADS)
    gain_two = gathered[6].astype(jnp.float32)
    gate_cols, up_cols = (
        lax.all_to_all(w_gate, "dp", split_axis=2, concat_axis=1, tiled=True),
        lax.all_to_all(w_up, "dp", split_axis=2, concat_axis=1, tiled=True),
    )
    tok_dev = inputs.shape[1]
    width = inputs.shape[2]
    scale = HEAD_DIM ** (-0.5)
    tokens = inputs[0].astype(jnp.float32)
    inverse_one, normed = norm_forward(tokens, gain_one)
    queries = jnp.dot(normed, query_w, preferred_element_type=jnp.float32).astype(jnp.bfloat16)
    keys_own = jnp.dot(normed, key_w, preferred_element_type=jnp.float32).astype(jnp.bfloat16)
    values_own = jnp.dot(normed, value_w, preferred_element_type=jnp.float32).astype(jnp.bfloat16)
    keys_all, values_all = (
        lax.all_gather(keys_own, "dp", axis=0, tiled=True),
        lax.all_gather(values_own, "dp", axis=0, tiled=True),
    )
    length = keys_all.shape[0]
    query_pos = lax.axis_index("dp") * tok_dev + jnp.arange(tok_dev, dtype=jnp.int32)
    key_pos = jnp.arange(length, dtype=jnp.int32)
    bucket_ids = bucket_table(query_pos, key_pos)
    bucket_onehot = (bucket_ids[:, :, None] == jnp.arange(BUCKETS, dtype=jnp.int32)).astype(
        jnp.bfloat16
    )
    bias_full = jnp.einsum("qkb,bh->hqk", bucket_onehot, table, preferred_element_type=jnp.float32)
    queries_h = queries.reshape(tok_dev, HEADS, HEAD_DIM)
    keys_h = keys_all.reshape(length, HEADS, HEAD_DIM)
    values_h = values_all.reshape(length, HEADS, HEAD_DIM)
    logits = (
        jnp.einsum("qhd,khd->hqk", queries_h, keys_h, preferred_element_type=jnp.float32) * scale
        + bias_full
    )
    row_max = jnp.max(logits, axis=-1, keepdims=True)
    exponent = jnp.exp(logits - row_max)
    row_total = jnp.sum(exponent, axis=-1, keepdims=True)
    log_total = row_max + jnp.log(row_total)
    probs_low = (exponent / row_total).astype(jnp.bfloat16)
    mixed_out = (
        jnp.einsum("hqk,khd->qhd", probs_low, values_h, preferred_element_type=jnp.float32)
        .reshape(tok_dev, -1)
        .astype(jnp.bfloat16)
    )
    resid = tokens + jnp.dot(mixed_out, out_w, preferred_element_type=jnp.float32)
    inverse_two, normed_two = norm_forward(resid, gain_two)
    local_n = w_gate.shape[0]
    sources = lax.axis_size("expert")
    experts_n = local_n * sources
    capacity = 5 * tok_dev // (2 * experts_n)
    pair_expert = routes[0]
    onehot = (pair_expert.reshape(-1)[:, None] == jnp.arange(experts_n, dtype=jnp.int32)).astype(
        jnp.int32
    )
    earlier = jnp.cumsum(onehot, axis=0) - onehot
    slot_idx = jnp.sum(earlier * onehot, axis=1).reshape(tok_dev, 2)
    dest = jnp.where(slot_idx < capacity, pair_expert * capacity + slot_idx, -1)
    slot_ids = jnp.arange(experts_n * capacity, dtype=jnp.int32)
    select = (jnp.transpose(dest)[:, :, None] == slot_ids).astype(jnp.bfloat16)
    dispatch_map = select[0] + select[1]
    send_rows = jnp.einsum(
        "ts,td->sd", dispatch_map, normed_two, preferred_element_type=jnp.float32
    ).astype(jnp.bfloat16)
    received = lax.all_to_all(
        send_rows.reshape(experts_n, capacity, width),
        "expert",
        split_axis=0,
        concat_axis=0,
        tiled=True,
    )
    slots_in = from_sources(received, local_n)
    slots_all = lax.all_gather(slots_in, "dp", axis=1, tiled=True)
    up_pre, activated, gelu_back, hidden_low = hidden_forward(slots_all, gate_cols, up_cols)
    partial_out = jnp.einsum("esf,efd->esd", hidden_low, w_down, preferred_element_type=jnp.float32)
    expert_out = lax.psum_scatter(
        partial_out.astype(jnp.bfloat16), "dp", scatter_dimension=1, tiled=True
    )
    returned = lax.all_to_all(
        to_sources(expert_out, sources, capacity), "expert", split_axis=0, concat_axis=0, tiled=True
    )
    picked = jnp.einsum(
        "kts,sd->ktd",
        select,
        returned.reshape(experts_n * capacity, width),
        preferred_element_type=jnp.float32,
    )
    first_gate = gate_fixed[0].astype(jnp.float32) / 65536.0
    gate_pair = jnp.stack([first_gate, 1.0 - first_gate], axis=0)
    block_out = (resid + jnp.sum(picked * gate_pair[:, :, None], axis=0)).astype(jnp.bfloat16)
    grad_top = cotangent[0].astype(jnp.float32)
    weighted = gate_pair[:, :, None] * grad_top[None]
    grad_send = jnp.einsum(
        "kts,ktd->sd", select.astype(jnp.float32), weighted, precision=HIGHEST
    ).astype(jnp.bfloat16)
    grad_recv = lax.all_to_all(
        grad_send.reshape(experts_n, capacity, width),
        "expert",
        split_axis=0,
        concat_axis=0,
        tiled=True,
    )
    grad_expert_out = from_sources(grad_recv, local_n)
    grad_all = lax.all_gather(grad_expert_out, "dp", axis=1, tiled=True)
    up_pre, activated, gelu_back, hidden_low = hidden_forward(slots_all, gate_cols, up_cols)
    grad_w_down = jnp.einsum(
        "esf,esd->efd", hidden_low, grad_all, preferred_element_type=jnp.float32
    )
    grad_hidden = jnp.einsum("esd,efd->esf", grad_all, w_down, preferred_element_type=jnp.float32)
    grad_gate_low = gelu_back(grad_hidden * up_pre)[0].astype(jnp.bfloat16)
    grad_up_low = (grad_hidden * activated).astype(jnp.bfloat16)
    gate_grad_cols = jnp.einsum(
        "esd,esf->edf", slots_all, grad_gate_low, preferred_element_type=jnp.float32
    )
    up_grad_cols = jnp.einsum(
        "esd,esf->edf", slots_all, grad_up_low, preferred_element_type=jnp.float32
    )
    slot_terms = jnp.einsum(
        "esf,edf->esd", grad_gate_low, gate_cols, preferred_element_type=jnp.float32
    )
    slot_terms = slot_terms + jnp.einsum(
        "esf,edf->esd", grad_up_low, up_cols, preferred_element_type=jnp.float32
    )
    grad_slots = lax.psum_scatter(
        slot_terms.astype(jnp.bfloat16), "dp", scatter_dimension=1, tiled=True
    )
    grad_w_gate, grad_w_up = (
        lax.all_to_all(
            gate_grad_cols.astype(jnp.bfloat16), "dp", split_axis=1, concat_axis=2, tiled=True
        ).astype(gate_grad_cols.dtype),
        lax.all_to_all(
            up_grad_cols.astype(jnp.bfloat16), "dp", split_axis=1, concat_axis=2, tiled=True
        ).astype(up_grad_cols.dtype),
    )
    grad_back = lax.all_to_all(
        to_sources(grad_slots, sources, capacity), "expert", split_axis=0, concat_axis=0, tiled=True
    )
    grad_normed_two = jnp.dot(
        dispatch_map,
        grad_back.reshape(experts_n * capacity, width),
        preferred_element_type=jnp.float32,
    )
    grad_gain_two, grad_resid_norm = norm_backward(resid, inverse_two, gain_two, grad_normed_two)
    grad_resid = grad_top + grad_resid_norm
    grad_attn_low = grad_resid.astype(jnp.bfloat16)
    grad_w_out = jnp.einsum(
        "ti,to->io", mixed_out, grad_attn_low, preferred_element_type=jnp.float32
    )
    grad_mixed = (
        jnp.einsum("to,io->ti", grad_attn_low, out_w, preferred_element_type=jnp.float32)
        .astype(jnp.bfloat16)
        .reshape(tok_dev, HEADS, HEAD_DIM)
    )
    logits = (
        jnp.einsum("qhd,khd->hqk", queries_h, keys_h, preferred_element_type=jnp.float32) * scale
        + bias_full
    )
    attn_probs = jnp.exp(logits - log_total)
    probs_low = attn_probs.astype(jnp.bfloat16)
    grad_probs = jnp.einsum(
        "qhd,khd->hqk", grad_mixed, values_h, preferred_element_type=jnp.float32
    )
    grad_logits = (
        attn_probs * (grad_probs - jnp.sum(grad_probs * attn_probs, axis=-1, keepdims=True))
    ).astype(jnp.bfloat16)
    grad_table = jnp.einsum(
        "hqk,qkb->bh", grad_logits, bucket_onehot, preferred_element_type=jnp.float32
    )
    grad_queries = (
        (
            jnp.einsum("hqk,khd->qhd", grad_logits, keys_h, preferred_element_type=jnp.float32)
            * scale
        )
        .astype(jnp.bfloat16)
        .reshape(tok_dev, -1)
    )
    grad_keys_part = (
        jnp.einsum("hqk,qhd->khd", grad_logits, queries_h, preferred_element_type=jnp.float32)
        * scale
    )
    grad_values_part = jnp.einsum(
        "hqk,qhd->khd", probs_low, grad_mixed, preferred_element_type=jnp.float32
    )
    grad_keys, grad_values = (
        lax.psum_scatter(
            grad_keys_part.reshape(length, -1).astype(jnp.bfloat16),
            "dp",
            scatter_dimension=0,
            tiled=True,
        ).astype(jnp.float32),
        lax.psum_scatter(
            grad_values_part.reshape(length, -1).astype(jnp.bfloat16),
            "dp",
            scatter_dimension=0,
            tiled=True,
        ).astype(jnp.float32),
    )
    grad_keys = grad_keys.astype(jnp.bfloat16)
    grad_values = grad_values.astype(jnp.bfloat16)
    grad_w_query = jnp.einsum("ti,to->io", normed, grad_queries, preferred_element_type=jnp.float32)
    grad_w_key = jnp.einsum("ti,to->io", normed, grad_keys, preferred_element_type=jnp.float32)
    grad_w_value = jnp.einsum("ti,to->io", normed, grad_values, preferred_element_type=jnp.float32)
    grad_normed = jnp.einsum("to,io->ti", grad_queries, query_w, preferred_element_type=jnp.float32)
    grad_normed = grad_normed + jnp.einsum(
        "to,io->ti", grad_keys, key_w, preferred_element_type=jnp.float32
    )
    grad_normed = grad_normed + jnp.einsum(
        "to,io->ti", grad_values, value_w, preferred_element_type=jnp.float32
    )
    grad_gain_one, grad_tok_norm = norm_backward(tokens, inverse_one, gain_one, grad_normed)
    grad_inputs = (grad_resid + grad_tok_norm).astype(jnp.bfloat16)
    attn_grads = (
        lax.psum_scatter(grad_gain_one, ("dp", "expert"), scatter_dimension=0, tiled=True),
        lax.psum_scatter(grad_w_query, ("dp", "expert"), scatter_dimension=0, tiled=True),
        lax.psum_scatter(grad_w_key, ("dp", "expert"), scatter_dimension=0, tiled=True),
        lax.psum_scatter(grad_w_value, ("dp", "expert"), scatter_dimension=0, tiled=True),
        lax.psum_scatter(grad_w_out, ("dp", "expert"), scatter_dimension=0, tiled=True),
        lax.psum_scatter(grad_table.reshape(-1), ("dp", "expert"), scatter_dimension=0, tiled=True),
        lax.psum_scatter(grad_gain_two, ("dp", "expert"), scatter_dimension=0, tiled=True),
    )
    return (
        block_out[None],
        grad_inputs[None],
        attn_grads[0],
        attn_grads[1],
        attn_grads[2],
        attn_grads[3],
        attn_grads[4],
        attn_grads[5],
        attn_grads[6],
        grad_w_gate,
        grad_w_up,
        grad_w_down,
    )


def solution(mesh):
    placed = (
        P("expert", "dp", None),
        P("expert", "dp", None),
        P(("dp", "expert")),
        P(("dp", "expert"), None),
        P(("dp", "expert"), None),
        P(("dp", "expert"), None),
        P(("dp", "expert"), None),
        P(("dp", "expert")),
        P(("dp", "expert")),
        P("expert", "dp", None),
        P("expert", "dp", None),
        P("expert", "dp", None),
        P("expert", "dp", None),
        P("expert", "dp"),
    )
    return jax.shard_map(
        local,
        mesh=mesh,
        in_specs=placed,
        out_specs=(
            P("expert", "dp", None),
            P("expert", "dp", None),
            P(("dp", "expert")),
            P(("dp", "expert"), None),
            P(("dp", "expert"), None),
            P(("dp", "expert"), None),
            P(("dp", "expert"), None),
            P(("dp", "expert")),
            P(("dp", "expert")),
            P("expert", "dp", None),
            P("expert", "dp", None),
            P("expert", "dp", None),
        ),
        check_vma=False,
    )
```

profile of v0, /device:TPU:0, one launch (start us, length us, event | category | flops | bytes accessed | tf_op | source)
XLA Modules:
  0.0 1528.4 jit_solution(5917689199385693043)
XLA Ops:
  12.0 42.2 %all-reduce.7 = (bf16[1024]{0:T(1024)(128)(2,1)S(1)}, bf16[512]{0:T(512)(128)(2,1)S(1)}, bf16[1024]{0:T(1024)(128)(2,1)S(1)}) all-reduce(bf16[1024]{0:T(1024)(128)(2,1)S(1)} %dynamic-update-slice, bf16[512]{0:T(512)(128)(2,1)S(1)} %dynamic-update-slice.1, ...), channel_id=1, replica_groups=mesh['dp'=4,'expert'=8] {'dp','expert'}, use_global_device_ids=true, to_apply=%add | all-reduce | flops 2560 | bytes 10240
  56.2 13.9 all-gather.15.cloned.1.call-done
  73.5 54.7 %all-gather.9.cloned.1.call-done = bf16[1024,1024]{1,0:T(8,128)(2,1)} async-done(((bf16[32,1024]{1,0:T(8,128)(2,1)}), bf16[1024,1024]{1,0:T(8,128)(2,1)}) %all-gather.9.cloned.1.call-update) | async-done | bytes 2097168 | tf_op jit(solution)/shard_map/all_gather | solution.py:92
  146.0 45.9 %copy.114 = pred[256,1024,32]{1,2,0:T(32,128)(4,1)S(1)} copy(pred[256,1024,32]{0,2,1:T(32,128)(4,1)} %iota_compare_fusion) | data formatting | bytes 16777216 | tf_op jit(solution)/shard_map/eq | solution.py:121
  203.1 30.1 %all-gather.17.cloned.1.call-done = bf16[1024,1024]{1,0:T(8,128)(2,1)} async-done(((bf16[256,1024]{1,0:T(8,128)(2,1)}), bf16[1024,1024]{1,0:T(8,128)(2,1)}) %all-gather.17.cloned.1.call-update) | async-done | bytes 2097168 | tf_op jit(solution)/shard_map/all_gather | solution.py:114
  236.0 43.8 %all-gather.11.cloned.1.call-done = bf16[1024,1024]{1,0:T(8,128)(2,1)} async-done(((bf16[256,1024]{1,0:T(8,128)(2,1)}), bf16[1024,1024]{1,0:T(8,128)(2,1)}) %all-gather.11.cloned.1.call-update) | async-done | bytes 2097168 | tf_op jit(solution)/shard_map/all_gather | solution.py:115
  283.7 21.2 %fusion.115 = (f32[16,256]{1,0:T(8,128)S(1)}, f32[16,256,1024]{2,1,0:T(8,128)}) fusion(f32[16,256,1024]{2,0,1:T(8,128)} %fusion.106, bf16[256,16,64]{0,2,1:T(8,128)(2,1)} %bitcast.238, bf16[1024,16,64]{0,2,1:T(8,128)(2,1)S(1)} %bitcast.223), kind=kOutput, calls=%fused_computation.148 | convolution fusion | flops 549449728 | bytes 36192256 | tf_op jit(solution)/shard_map/qhd,khd->hqk/dot_general | solution.py:129
  320.2 17.5 %all-gather.19.cloned.1.call-done = bf16[1024,1024]{1,0:T(8,128)(2,1)} async-done(((bf16[32,1024]{1,0:T(8,128)(2,1)}), bf16[1024,1024]{1,0:T(8,128)(2,1)}) %all-gather.19.cloned.1.call-update) | async-done | bytes 2097168 | tf_op jit(solution)/shard_map/all_gather | solution.py:93
  341.3 21.3 %all_to_all.68 = bf16[8,80,1024]{2,1,0:T(8,128)(2,1)} all-to-all(bf16[8,80,1024]{2,1,0:T(8,128)(2,1)S(1)} %bitcast.249), channel_id=1, replica_groups=mesh['dp'=4,'expert'=8] {'expert'}, dimensions={0} | all-to-all | bytes 2621440 | tf_op jit(solution)/shard_map/all_to_all | solution.py:161
  366.9 21.3 %all_to_all.69 = bf16[8,80,1024]{2,1,0:T(8,128)(2,1)} all-to-all(bf16[8,80,1024]{2,1,0:T(8,128)(2,1)S(1)} %bitcast.262), channel_id=1, replica_groups=mesh['dp'=4,'expert'=8] {'expert'}, dimensions={0} | all-to-all | bytes 2621440 | tf_op jit(solution)/shard_map/all_to_all | solution.py:192
  396.1 17.4 %reduce.2 = bf16[2816,256]{1,0:T(8,128)(2,1)} reduce(bf16[2816,1,256]{2,1,0:T(2,128)(2,1)} %bitcast.230, bf16[]{:T(256)} %broadcast.249), dimensions={1}, to_apply=%bitcast.169.reduce_sub_computation | reduce | bytes 2883586
  429.0 17.4 %reduce.3 = bf16[2816,256]{1,0:T(8,128)(2,1)} reduce(bf16[2816,1,256]{2,1,0:T(2,128)(2,1)} %bitcast.237, bf16[]{:T(256)} %broadcast.249), dimensions={1}, to_apply=%bitcast.171.reduce_sub_computation | reduce | bytes 2883586
  450.1 37.4 %all-to-all-done.1 = bf16[4,2,90112]{2,1,0:T(2,128)(2,1)} async-done(((bf16[4,2,90112]{2,1,0:T(2,128)(2,1)}), bf16[4,2,90112]{2,1,0:T(2,128)(2,1)}, u32[]{:S(2)}, u32[]{:S(2)}) %all-to-all-start.1) | async-done | bytes 1441824 | tf_op jit(solution)/shard_map/all_to_all | solution.py:102
  501.5 65.1 %all-to-all-done.2 = bf16[4,2,90112]{2,1,0:T(2,128)(2,1)} async-done(((bf16[4,2,90112]{2,1,0:T(2,128)(2,1)}), bf16[4,2,90112]{2,1,0:T(2,128)(2,1)}, u32[]{:S(2)}, u32[]{:S(2)}) %all-to-all-start.2) | async-done | bytes 1441824 | tf_op jit(solution)/shard_map/all_to_all | solution.py:103
  591.6 19.7 %all-gather.23.cloned.1.call-done = bf16[1,2560,1024]{2,1,0:T(8,128)(2,1)} async-done(((bf16[1,640,1024]{2,1,0:T(8,128)(2,1)}), bf16[1,2560,1024]{2,1,0:T(8,128)(2,1)}) %all-gather.23.cloned.1.call-update) | async-done | bytes 5242896 | tf_op jit(solution)/shard_map/all_gather | solution.py:200
  611.3 15.2 multiply_convert_fusion.1
  649.0 78.3 %reduce-scatter.9.cloned.1.call-done = bf16[1,640,1024]{2,1,0:T(8,128)(2,1)} async-done(((bf16[1,2560,1024]{2,1,0:T(8,128)(2,1)}), bf16[1,640,1024]{2,1,0:T(8,128)(2,1)}) %reduce-scatter.9.cloned.1.call-update) | async-done | bytes 1310736 | tf_op jit(solution)/shard_map/reduce_scatter | solution.py:172
  731.6 92.1 %reduce-scatter.11.cloned.1.call-done = bf16[1,640,1024]{2,1,0:T(8,128)(2,1)} async-done(((bf16[1,2560,1024]{2,1,0:T(8,128)(2,1)}), bf16[1,640,1024]{2,1,0:T(8,128)(2,1)}) %reduce-scatter.11.cloned.1.call-update) | async-done | bytes 1310736 | tf_op jit(solution)/shard_map/reduce_scatter | solution.py:220
  831.7 14.5 all-to-all-done.5
  909.0 42.1 %reduce-scatter.13.cloned.1.call-done = bf16[256,1024]{0,1:T(8,128)(2,1)} async-done(((bf16[1024,1024]{0,1:T(8,128)(2,1)}), bf16[256,1024]{0,1:T(8,128)(2,1)}) %reduce-scatter.13.cloned.1.call-update) | async-done | bytes 524304 | tf_op jit(solution)/shard_map/reduce_scatter | solution.py:281
  1111.4 42.7 %all-reduce.6 = (f32[1024]{0:T(1024)S(1)}, f32[512]{0:T(512)S(1)}, f32[1024]{0:T(1024)S(1)}) all-reduce(f32[1024]{0:T(1024)S(1)} %get-tuple-element.62, f32[512]{0:T(512)S(1)} %reshape.334, f32[1024]{0:T(1024)S(1)} %get-tuple-element.60), channel_id=6, replica_groups=mesh['dp'=4,'expert'=8] {'dp','expert'}, use_global_device_ids=true, to_apply=%region_16.17.clone | all-reduce | flops 2560 | bytes 20480
  1158.2 83.8 %reduce-scatter.17.cloned.1.call-done = f32[32,1024]{1,0:T(8,128)} async-done(((f32[1024,1024]{1,0:T(8,128)}), f32[32,1024]{1,0:T(8,128)}) %reduce-scatter.17.cloned.1.call-update) | async-done | bytes 131088 | tf_op jit(solution)/shard_map/reduce_scatter | solution.py:310
  1242.0 139.7 %reduce-scatter.21.cloned.1.call-done = f32[32,1024]{1,0:T(8,128)} async-done(((f32[1024,1024]{1,0:T(8,128)}), f32[32,1024]{1,0:T(8,128)}) %reduce-scatter.21.cloned.1.call-update) | async-done | bytes 131088 | tf_op jit(solution)/shard_map/reduce_scatter | solution.py:312
  1381.7 139.7 %reduce-scatter.19.cloned.1.call-done = f32[32,1024]{1,0:T(8,128)} async-done(((f32[1024,1024]{1,0:T(8,128)}), f32[32,1024]{1,0:T(8,128)}) %reduce-scatter.19.cloned.1.call-update) | async-done | bytes 131088 | tf_op jit(solution)/shard_map/reduce_scatter | solution.py:311
  (252 shorter events, 396.5 us)
Async XLA Ops:
  7.2 604.1 %copy-start = (bf16[1,704,1024]{2,1,0:T(8,128)(2,1)S(1)}, bf16[1,704,1024]{2,1,0:T(8,128)(2,1)}, u32[]{:S(2)}) copy-start(bf16[1,704,1024]{2,1,0:T(8,128)(2,1)} %param.25) | copy-start | bytes 4325380
  7.2 62.9 %all-gather.15.cloned.1.call-start = ((), (), s32[]{:S(2)}) async-start(), calls=%async_computation.19 | async-start | bytes 2162688 | tf_op jit(solution)/shard_map/all_gather | solution.py:91
  7.9 120.2 %all-gather.9.cloned.1.call-start = ((), (), s32[]{:S(2)}) async-start(), calls=%async_computation.16 | async-start | bytes 2162688 | tf_op jit(solution)/shard_map/all_gather | solution.py:92
  8.7 191.0 %all-gather.13.cloned.1.call-start = ((), (), s32[]{:S(2)}) async-start(), calls=%async_computation.18 | async-start | bytes 2162688 | tf_op jit(solution)/shard_map/all_gather | solution.py:90
  9.4 223.7 %all-gather.17.cloned.1.call-start = ((), (), s32[]{:S(2)}) async-start(), calls=%async_computation.20 | async-start | bytes 2621440 | tf_op jit(solution)/shard_map/all_gather | solution.py:114
  73.4 206.4 %all-gather.11.cloned.1.call-start = ((), (), s32[]{:S(2)}) async-start(), calls=%async_computation.17 | async-start | bytes 2621440 | tf_op jit(solution)/shard_map/all_gather | solution.py:115
  131.3 206.3 %all-gather.19.cloned.1.call-start = ((), (), s32[]{:S(2)}) async-start(), calls=%async_computation.21 | async-start | bytes 2162688 | tf_op jit(solution)/shard_map/all_gather | solution.py:93
  131.9 443.6 %all-gather.21.cloned.1.call-start = ((), (), s32[]{:S(2)}) async-start(), calls=%async_computation.22 | async-start | bytes 6553600 | tf_op jit(solution)/shard_map/all_gather | solution.py:169
  362.7 248.6 %all-gather.23.cloned.1.call-start = ((), (), s32[]{:S(2)}) async-start(), calls=%async_computation.24 | async-start | bytes 6553600 | tf_op jit(solution)/shard_map/all_gather | solution.py:200
  417.2 70.2 %all-to-all-start.1 = ((bf16[4,2,90112]{2,1,0:T(2,128)(2,1)}), bf16[4,2,90112]{2,1,0:T(2,128)(2,1)}, u32[]{:S(2)}, u32[]{:S(2)}) async-start(bf16[4,2,90112]{2,1,0:T(2,128)(2,1)} %reshape.352), calls=%async_computation.1 | async-start | bytes 2883584 | tf_op jit(solution)/shard_map/all_to_all | solution.py:102
  487.4 79.2 %all-to-all-start.2 = ((bf16[4,2,90112]{2,1,0:T(2,128)(2,1)}), bf16[4,2,90112]{2,1,0:T(2,128)(2,1)}, u32[]{:S(2)}, u32[]{:S(2)}) async-start(bf16[4,2,90112]{2,1,0:T(2,128)(2,1)} %reshape.354), calls=%async_computation.2 | async-start | bytes 2883584 | tf_op jit(solution)/shard_map/all_to_all | solution.py:103
  491.8 235.6 %reduce-scatter.9.cloned.1.call-start = ((), (), s32[]{:S(2)}) async-start(), calls=%async_computation.23 | async-start | bytes 6553600 | tf_op jit(solution)/shard_map/reduce_scatter | solution.py:172
  634.7 189.1 %reduce-scatter.11.cloned.1.call-start = ((), (), s32[]{:S(2)}) async-start(), calls=%async_computation.25 | async-start | bytes 6553600 | tf_op jit(solution)/shard_map/reduce_scatter | solution.py:220
  727.3 96.4 %all-to-all-start.3 = ((bf16[8,80,1024]{2,1,0:T(8,128)(2,1)}), bf16[8,80,1024]{2,1,0:T(8,128)(2,1)}, u32[]{:S(2)}, u32[]{:S(2)}) async-start(bf16[8,80,1024]{2,1,0:T(8,128)(2,1)} %bitcast.261), calls=%async_computation.4 | async-start | bytes 2621440 | tf_op jit(solution)/shard_map/all_to_all | solution.py:175
  823.8 22.5 %all-to-all-start.5 = ((bf16[8,80,1024]{2,1,0:T(8,128)(2,1)}), bf16[8,80,1024]{2,1,0:T(8,128)(2,1)}, u32[]{:S(2)}, u32[]{:S(2)}) async-start(bf16[8,80,1024]{2,1,0:T(8,128)(2,1)} %bitcast.260), calls=%async_computation.7 | async-start | bytes 2621440 | tf_op jit(solution)/shard_map/all_to_all | solution.py:231
  828.0 77.0 %reduce-scatter.15.cloned.1.call-start = ((), (), s32[]{:S(2)}) async-start(), calls=%async_computation.27 | async-start | bytes 2621440 | tf_op jit(solution)/shard_map/reduce_scatter | solution.py:287
  862.3 88.8 %reduce-scatter.13.cloned.1.call-start = ((), (), s32[]{:S(2)}) async-start(), calls=%async_computation.26 | async-start | bytes 2621440 | tf_op jit(solution)/shard_map/reduce_scatter | solution.py:281
  890.6 267.6 %reduce-scatter.23.cloned.1.call-start = ((), (), s32[]{:S(2)}) async-start(), calls=%async_computation.31 | async-start | bytes 4325376 | tf_op jit(solution)/shard_map/reduce_scatter | solution.py:313
  894.6 347.4 %reduce-scatter.17.cloned.1.call-start = ((), (), s32[]{:S(2)}) async-start(), calls=%async_computation.28 | async-start | bytes 4325376 | tf_op jit(solution)/shard_map/reduce_scatter | solution.py:310
  904.1 477.6 %reduce-scatter.21.cloned.1.call-start = ((), (), s32[]{:S(2)}) async-start(), calls=%async_computation.30 | async-start | bytes 4325376 | tf_op jit(solution)/shard_map/reduce_scatter | solution.py:312
  908.9 612.5 %reduce-scatter.19.cloned.1.call-start = ((), (), s32[]{:S(2)}) async-start(), calls=%async_computation.29 | async-start | bytes 4325376 | tf_op jit(solution)/shard_map/reduce_scatter | solution.py:311
  983.0 41.6 %all-to-all-start.6 = ((bf16[4,2,90112]{2,1,0:T(2,128)(2,1)}), bf16[4,2,90112]{2,1,0:T(2,128)(2,1)S(1)}, u32[]{:S(2)}, u32[]{:S(2)}) async-start(bf16[4,2,90112]{2,1,0:T(2,128)(2,1)} %reshape.356), calls=%async_computation.14 | async-start | bytes 2883584 | tf_op jit(solution)/shard_map/all_to_all | solution.py:224
  1024.6 41.5 %all-to-all-start.7 = ((bf16[4,2,90112]{2,1,0:T(2,128)(2,1)}), bf16[4,2,90112]{2,1,0:T(2,128)(2,1)S(1)}, u32[]{:S(2)}, u32[]{:S(2)}) async-start(bf16[4,2,90112]{2,1,0:T(2,128)(2,1)} %reshape.358), calls=%async_computation.15 | async-start | bytes 2883584 | tf_op jit(solution)/shard_map/all_to_all | solution.py:227
  1108.6 412.7 %copy-start.1 = (bf16[1,704,1024]{2,1,0:T(8,128)(2,1)S(1)}, bf16[1,704,1024]{2,1,0:T(8,128)(2,1)}, u32[]{:S(2)}) copy-start(bf16[1,704,1024]{2,1,0:T(8,128)(2,1)} %param.25) | copy-start | bytes 4325380
  (48 other events, 1698.5 us)
Sparse Core Ops, SparseCore 0:
  10.9 59.1 all-gather.14
  72.9 55.2 all-gather.8
  131.0 55.2 all-gather.12
  188.3 44.7 all-gather.16
  235.1 44.6 all-gather.10
  282.5 55.0 all-gather.18
  362.8 126.7 all-gather.20
  491.1 120.1 all-gather.22
  634.8 92.4 reduce-scatter.8
  729.5 94.2 reduce-scatter.10
  862.4 42.5 reduce-scatter.14
  907.8 43.1 reduce-scatter.12
  953.9 145.4 reduce-scatter.22
  1102.1 139.8 reduce-scatter.16
  1244.7 136.9 reduce-scatter.20
  1384.4 136.9 reduce-scatter.18
where the time goes:
time: 1530 us
  waiting for transfers between devices  893 us (58%)
  matrix products  188 us (12%)
  local copies, waits for them, and re-layouts  180 us (12%)
  blocking collectives  127 us (8%)
  other arithmetic  96.8 us (6%)
  starting transfers between devices  27.8 us (2%)
    reduce_scatter x1, waiting for transfers between devices, local(): lax.psum_scatter(grad_w_key, ('dp', 'expert'), scatter_dimension=0, tiled...  140 us
    reduce_scatter x1, waiting for transfers between devices, local(): lax.psum_scatter(grad_w_value, ('dp', 'expert'), scatter_dimension=0, til...  140 us
    reduce_scatter x1, waiting for transfers between devices, local(): lax.psum_scatter(slot_terms.astype(jnp.bfloat16), 'dp', scatter_dimension...  92.1 us
    unnamed x2, blocking collectives  84.9 us
    reduce_scatter x1, waiting for transfers between devices, local(): lax.psum_scatter(grad_w_query, ('dp', 'expert'), scatter_dimension=0, til...  83.8 us
    reduce_scatter x1, waiting for transfers between devices, local(): lax.psum_scatter(partial_out.astype(jnp.bfloat16), 'dp', scatter_dimensio...  78.3 us
    unnamed x127, local copies, waits for them, and re-layouts  71.3 us
    all_to_all x1, waiting for transfers between devices, local(): lax.all_to_all(w_up, 'dp', split_axis=2, concat_axis=1, tiled=True)  65.1 us
  transfers between devices with their start and end apart: 22, of which 18 were waited for; matrix products, arithmetic and copies ran while one was open for 27% of the time, Pallas kernels for 0%

commit v1 on v0

v1 whole, which is shorter than its diff:
```python
import functools

import jax
import jax.numpy as jnp
from jax import lax
from jax.experimental import pallas as pl
from jax.experimental.pallas import tpu as pltpu
from jax.sharding import PartitionSpec as P

HEADS = 16
HEAD_DIM = 64
BUCKETS = 32
THRESHOLDS = (12, 16, 23, 32, 46, 64, 91)
EPSILON = 1e-06
SCALE = HEAD_DIM ** (-0.5)
BF16 = jnp.bfloat16
F32 = jnp.float32
GELU_C = 0.7978845608028654
GELU_A = 0.044715
VMEM_LIMIT = 56 * 1024 * 1024

NT = (((1,), (1,)), ((), ()))
TN = (((0,), (0,)), ((), ()))
NN = (((1,), (0,)), ((), ()))


def mm(a, b, dims=NN):
    return lax.dot_general(a, b, dims, preferred_element_type=F32)


def bucket_of(offset):
    distance = jnp.abs(offset)
    banded = jnp.full(distance.shape, 8, jnp.int32)
    for cutoff in THRESHOLDS:
        banded = banded + (distance >= cutoff).astype(jnp.int32)
    nearby = jnp.where(distance < 8, distance, banded)
    return nearby + jnp.where(offset > 0, 16, 0).astype(jnp.int32)


def norm_forward(values, gain):
    inverse = lax.rsqrt(jnp.mean(values * values, axis=-1, keepdims=True) + EPSILON)
    return (inverse, (values * inverse * gain).astype(BF16))


def norm_backward(values, inverse, gain, grad_normed):
    scaled = gain * grad_normed
    grad_gain = jnp.sum(grad_normed * values * inverse, axis=0)
    grad_values = inverse * scaled - values * inverse**3 * jnp.mean(
        scaled * values, axis=-1, keepdims=True
    )
    return (grad_gain, grad_values)


def bias_tile(vec_ref, head, tile_ref):
    block, wide = tile_ref.shape
    row = jnp.broadcast_to(vec_ref[pl.ds(head, 1), :], (block, wide))
    tile_ref[...] = pltpu.roll(row, wide - block, 1, stride=1, stride_axis=0)


def tile_offset(dp, n, block, query_block, key_block):
    query_abs = lax.rem(dp - query_block + n, n)
    key_abs = lax.rem(dp - key_block + n, n)
    return pl.multiple_of((key_abs - query_abs + n - 1) * block, 128)


def head_logits(n, block, dp, query_block, q_pair, k_pair, mask, tile_ref):
    masked = jnp.where(mask, q_pair, jnp.zeros_like(q_pair))
    raw = mm(masked, k_pair, NT) * SCALE
    bias = jnp.concatenate(
        [
            tile_ref[:, pl.ds(tile_offset(dp, n, block, query_block, j), block)]
            for j in range(n)
        ],
        axis=1,
    )
    return raw + bias


def attention_forward_kernel(n, block, dp_ref, q_ref, k_ref, v_ref, vec_ref, out_ref, lse_ref, tiles):
    dp = dp_ref[0]
    pair, query_block = pl.program_id(0), pl.program_id(1)

    @pl.when(query_block == 0)
    def _():
        for side in range(2):
            bias_tile(vec_ref, 2 * pair + side, tiles.at[side])

    q_pair, k_pair, v_pair = q_ref[...], k_ref[...], v_ref[...]
    lane = lax.broadcasted_iota(jnp.int32, (block, 128), 1)
    outs, lses = [], []
    for side in range(2):
        mask = (lane >= HEAD_DIM) if side else (lane < HEAD_DIM)
        logits = head_logits(n, block, dp, query_block, q_pair, k_pair, mask, tiles.at[side])
        row_max = jnp.max(logits, axis=-1, keepdims=True)
        exponent = jnp.exp(logits - row_max)
        total = jnp.sum(exponent, axis=-1, keepdims=True)
        low = (exponent * (1.0 / total)).astype(BF16)
        outs.append(mm(low, v_pair))
        lses.append(jnp.broadcast_to(row_max + jnp.log(total), (block, 128)))
    first = lane < HEAD_DIM
    out_ref[...] = jnp.where(first, outs[0], outs[1]).astype(BF16)
    lse_ref[...] = jnp.where(first, lses[0], lses[1])


def attention_forward(dp, n, qkv, vectors):
    rows, triple = qkv.shape
    own = triple // 3
    block = rows // n
    pairs = own // 128
    wide = vectors.shape[1]
    return pl.pallas_call(
        functools.partial(attention_forward_kernel, n, block),
        grid=(pairs, n),
        in_specs=[
            pl.BlockSpec(memory_space=pltpu.SMEM),
            pl.BlockSpec((block, 128), lambda p, i: (i, p)),
            pl.BlockSpec((rows, 128), lambda p, i: (0, pairs + p)),
            pl.BlockSpec((rows, 128), lambda p, i: (0, 2 * pairs + p)),
            pl.BlockSpec((2 * pairs, wide), lambda p, i: (0, 0)),
        ],
        out_specs=[
            pl.BlockSpec((block, 128), lambda p, i: (i, p)),
            pl.BlockSpec((block, 128), lambda p, i: (i, p)),
        ],
        out_shape=[
            jax.ShapeDtypeStruct((rows, own), BF16),
            jax.ShapeDtypeStruct((rows, own), F32),
        ],
        scratch_shapes=[pltpu.VMEM((2, block, wide), F32)],
        compiler_params=pltpu.CompilerParams(vmem_limit_bytes=VMEM_LIMIT),
        cost_estimate=pl.CostEstimate(
            flops=16 * rows * rows * own, bytes_accessed=6 * rows * own, transcendentals=rows * rows * own // 64
        ),
        name="attention_forward",
    )(dp, qkv, qkv, qkv, vectors)


def diagonal_sum(tile):
    rows, wide = tile.shape
    while rows > 1:
        half = rows // 2
        tile = tile[:half] + pltpu.roll(tile[half:], wide - half, 1)
        rows = half
    return tile


def attention_backward_kernel(
    n, block, dp_ref, q_ref, k_ref, v_ref, lse_ref, dm_ref, vec_ref,
    dq_ref, dk_ref, dv_ref, diag_ref, tiles, sums, dk_acc, dv_acc,
):
    dp = dp_ref[0]
    pair, query_block = pl.program_id(0), pl.program_id(1)

    @pl.when(query_block == 0)
    def _():
        for side in range(2):
            bias_tile(vec_ref, 2 * pair + side, tiles.at[side])
        sums[...] = jnp.zeros_like(sums)
        dk_acc[...] = jnp.zeros_like(dk_acc)
        dv_acc[...] = jnp.zeros_like(dv_acc)

    q_pair, k_pair, v_pair, dm_pair = q_ref[...], k_ref[...], v_ref[...], dm_ref[...]
    rows = k_pair.shape[0]
    lane = lax.broadcasted_iota(jnp.int32, (block, 128), 1)
    dqs, dks, dvs = [], [], []
    for side in range(2):
        mask = (lane >= HEAD_DIM) if side else (lane < HEAD_DIM)
        logits = head_logits(n, block, dp, query_block, q_pair, k_pair, mask, tiles.at[side])
        probs = jnp.exp(logits - lse_ref[:, side * HEAD_DIM : side * HEAD_DIM + 1])
        masked = jnp.where(mask, dm_pair, jnp.zeros_like(dm_pair))
        d_probs = mm(masked, v_pair, NT)
        inner = jnp.sum(probs * d_probs, axis=-1, keepdims=True)
        d_logits = (probs * (d_probs - inner)).astype(BF16)
        dvs.append(mm(probs.astype(BF16), dm_pair, TN))
        dqs.append(mm(d_logits, k_pair))
        dks.append(mm(d_logits, q_pair, TN))
        wide = d_logits.astype(F32)
        for j in range(n):
            here = pl.ds(tile_offset(dp, n, block, query_block, j), block)
            sums[side, :, here] += wide[:, j * block : (j + 1) * block]
    dq_ref[...] = (jnp.where(lane < HEAD_DIM, dqs[0], dqs[1]) * SCALE).astype(BF16)
    key_lane = lax.broadcasted_iota(jnp.int32, (rows, 128), 1)
    dk_acc[...] += jnp.where(key_lane < HEAD_DIM, dks[0], dks[1])
    dv_acc[...] += jnp.where(key_lane < HEAD_DIM, dvs[0], dvs[1])

    @pl.when(query_block == n - 1)
    def _():
        dk_ref[...] = (dk_acc[...] * SCALE).astype(BF16)
        dv_ref[...] = dv_acc[...].astype(BF16)
        for side in range(2):
            diag_ref[0, pl.ds(side, 1), :] = diagonal_sum(sums[side])


def attention_backward(dp, n, qkv, lse, d_mixed, vectors):
    rows, triple = qkv.shape
    own = triple // 3
    block = rows // n
    pairs = own // 128
    wide = vectors.shape[1]
    return pl.pallas_call(
        functools.partial(attention_backward_kernel, n, block),
        grid=(pairs, n),
        in_specs=[
            pl.BlockSpec(memory_space=pltpu.SMEM),
            pl.BlockSpec((block, 128), lambda p, i: (i, p)),
            pl.BlockSpec((rows, 128), lambda p, i: (0, pairs + p)),
            pl.BlockSpec((rows, 128), lambda p, i: (0, 2 * pairs + p)),
            pl.BlockSpec((block, 128), lambda p, i: (i, p)),
            pl.BlockSpec((block, 128), lambda p, i: (i, p)),
            pl.BlockSpec((2 * pairs, wide), lambda p, i: (0, 0)),
        ],
        out_specs=[
            pl.BlockSpec((block, 128), lambda p, i: (i, p)),
            pl.BlockSpec((rows, 128), lambda p, i: (0, p)),
            pl.BlockSpec((rows, 128), lambda p, i: (0, p)),
            pl.BlockSpec((1, 2, wide), lambda p, i: (p, 0, 0)),
        ],
        out_shape=[
            jax.ShapeDtypeStruct((rows, own), BF16),
            jax.ShapeDtypeStruct((rows, own), BF16),
            jax.ShapeDtypeStruct((rows, own), BF16),
            jax.ShapeDtypeStruct((pairs, 2, wide), F32),
        ],
        scratch_shapes=[
            pltpu.VMEM((2, block, wide), F32),
            pltpu.VMEM((2, block, wide), F32),
            pltpu.VMEM((rows, 128), F32),
            pltpu.VMEM((rows, 128), F32),
        ],
        compiler_params=pltpu.CompilerParams(vmem_limit_bytes=VMEM_LIMIT),
        cost_estimate=pl.CostEstimate(
            flops=40 * rows * rows * own, bytes_accessed=14 * rows * own, transcendentals=rows * rows * own // 64
        ),
        name="attention_backward",
    )(dp, qkv, qkv, qkv, lse, d_mixed, vectors)


def gelu_pair(v):
    square = v * v
    t = jnp.tanh(GELU_C * (v + GELU_A * v * square))
    half = 0.5 * (1.0 + t)
    slope = half + (0.5 * GELU_C) * v * (1.0 - t * t) * (1.0 + (3.0 * GELU_A) * square)
    return v * half, slope


def expert_kernel(
    main, slots_a, slots_b, dout_a, dout_b, wgu_ref, wd_ref,
    out_ref, dslot_ref, gwgu_ref, gwd_ref, gwgu_acc, gwd_acc,
):
    step = pl.program_id(0)

    @pl.when(step == 0)
    def _():
        gwgu_acc[...] = jnp.zeros_like(gwgu_acc)
        gwd_acc[...] = jnp.zeros_like(gwd_acc)

    slots = jnp.concatenate([slots_a[0], slots_b[0]], axis=0)
    d_out = jnp.concatenate([dout_a[0], dout_b[0]], axis=0)
    rows = slots.shape[0]
    wgu, wd = wgu_ref[...], wd_ref[...]
    pre = mm(slots, wgu)
    d_hidden = mm(d_out, wd, NT)
    low_lane = lax.broadcasted_iota(jnp.int32, (rows, 128), 1) < 64
    gate, up = pre[:, :main], pre[:, main : 2 * main]
    tail = pre[:, 2 * main :]
    tail_up = pltpu.roll(tail, 64, 1)
    act, slope = gelu_pair(gate)
    act_t, slope_t = gelu_pair(tail)
    hidden_t = jnp.where(low_lane, act_t * tail_up, 0.0)
    hidden = jnp.concatenate([(act * up).astype(BF16), hidden_t.astype(BF16)], axis=1)
    out_ref[0] = mm(hidden, wd).astype(BF16)
    gwd_acc[...] += mm(hidden, d_out, TN)
    dh, dh_t = d_hidden[:, :main], d_hidden[:, main:]
    d_gate = dh * up * slope
    d_up = dh * act
    d_tail = jnp.where(low_lane, dh_t * tail_up * slope_t, pltpu.roll(dh_t * act_t, 64, 1))
    d_pre = jnp.concatenate([d_gate.astype(BF16), d_up.astype(BF16), d_tail.astype(BF16)], axis=1)
    dslot_ref[0] = mm(d_pre, wgu, NT).astype(BF16)
    gwgu_acc[...] += mm(slots, d_pre, TN)

    @pl.when(step == pl.num_programs(0) - 1)
    def _():
        gwgu_ref[...] = gwgu_acc[...].astype(BF16)
        gwd_ref[...] = gwd_acc[...]


def experts(slots, d_outs, wgu, wd, steps):
    width, columns = wgu.shape
    deep = wd.shape[0]
    main = (columns - 128) // 2
    slots = [s.reshape(steps, -1, width) for s in slots]
    d_outs = [s.reshape(steps, -1, width) for s in d_outs]
    half = slots[0].shape[1]
    rows = 2 * half * steps
    part = pl.BlockSpec((1, half, width), lambda i: (i, 0, 0))
    whole = pl.BlockSpec((1, 2 * half, width), lambda i: (i, 0, 0))
    return pl.pallas_call(
        functools.partial(expert_kernel, main),
        grid=(steps,),
        in_specs=[
            part, part, part, part,
            pl.BlockSpec((width, columns), lambda i: (0, 0)),
            pl.BlockSpec((deep, width), lambda i: (0, 0)),
        ],
        out_specs=[
            whole, whole,
            pl.BlockSpec((width, columns), lambda i: (0, 0)),
            pl.BlockSpec((deep, width), lambda i: (0, 0)),
        ],
        out_shape=[
            jax.ShapeDtypeStruct((steps, 2 * half, width), BF16),
            jax.ShapeDtypeStruct((steps, 2 * half, width), BF16),
            jax.ShapeDtypeStruct((width, columns), BF16),
            jax.ShapeDtypeStruct((deep, width), F32),
        ],
        scratch_shapes=[
            pltpu.VMEM((width, columns), F32),
            pltpu.VMEM((deep, width), F32),
        ],
        compiler_params=pltpu.CompilerParams(vmem_limit_bytes=VMEM_LIMIT),
        cost_estimate=pl.CostEstimate(
            flops=6 * rows * width * (columns + deep),
            bytes_accessed=8 * rows * width + 8 * width * columns,
            transcendentals=rows * deep,
        ),
        name="experts",
    )(*slots, *d_outs, wgu, wd)


def pack_kernel(n, piece, gate_ref, up_ref, out_ref):
    main = piece // 128 * 128
    gate, up = gate_ref[...], up_ref[...]
    for j in range(n):
        g = gate[:, j * piece : (j + 1) * piece]
        u = up[:, j * piece : (j + 1) * piece]
        out_ref[j] = jnp.concatenate([g[:, :main], u[:, :main], g[:, main:], u[:, main:]], axis=1)


def pack_columns(n, gate, up):
    rows, total = gate.shape
    piece = total // n
    step = min(rows, 64)
    return pl.pallas_call(
        functools.partial(pack_kernel, n, piece),
        grid=(rows // step,),
        in_specs=[pl.BlockSpec((step, total), lambda i: (i, 0))] * 2,
        out_specs=pl.BlockSpec((n, step, 2 * piece), lambda i: (0, i, 0)),
        out_shape=jax.ShapeDtypeStruct((n, rows, 2 * piece), gate.dtype),
        compiler_params=pltpu.CompilerParams(vmem_limit_bytes=VMEM_LIMIT),
        cost_estimate=pl.CostEstimate(flops=0, bytes_accessed=8 * rows * total, transcendentals=0),
        name="pack_columns",
    )(gate, up)


def unpack_kernel(n, piece, in_ref, gate_ref, up_ref):
    main = piece // 128 * 128
    rest = piece - main
    gates, ups = [], []
    for j in range(n):
        block = in_ref[j].astype(F32)
        gates += [block[:, :main], block[:, 2 * main : 2 * main + rest]]
        ups += [block[:, main : 2 * main], block[:, 2 * main + rest :]]
    gate_ref[...] = jnp.concatenate(gates, axis=1)
    up_ref[...] = jnp.concatenate(ups, axis=1)


def unpack_columns(blocks):
    n, rows, both = blocks.shape
    piece = both // 2
    step = min(rows, 64)
    total = n * piece
    return pl.pallas_call(
        functools.partial(unpack_kernel, n, piece),
        grid=(rows // step,),
        in_specs=[pl.BlockSpec((n, step, both), lambda i: (0, i, 0))],
        out_specs=[pl.BlockSpec((step, total), lambda i: (i, 0))] * 2,
        out_shape=[jax.ShapeDtypeStruct((rows, total), F32)] * 2,
        compiler_params=pltpu.CompilerParams(vmem_limit_bytes=VMEM_LIMIT),
        cost_estimate=pl.CostEstimate(flops=0, bytes_accessed=12 * rows * total, transcendentals=0),
        name="unpack_columns",
    )(blocks)


def shift(value, distance, n):
    return lax.ppermute(value, "dp", [(i, (i + distance) % n) for i in range(n)])


def gather_dp(value, n):
    return [value] + [shift(value, d, n) for d in range(1, n)]


def pick(stacked, index):
    return lax.dynamic_index_in_dim(stacked, index, 0, keepdims=False)


def exchange(value):
    return lax.all_to_all(value, "expert", split_axis=0, concat_axis=0, tiled=True)


def local(
    inputs, cotangent, gain_attn, w_query, w_key, w_value, w_out, position_bias,
    gain_moe, w_gate, w_up, w_down, routes, gate_fixed,
):
    n = lax.axis_size("dp")
    experts_n = lax.axis_size("expert")
    dp = lax.axis_index("dp")
    ex = lax.axis_index("expert")
    tok, width = inputs.shape[1:]
    length = n * tok
    own = HEADS * HEAD_DIM // n
    heads_own = HEADS // n
    wrows = w_query.shape[0]
    capacity = 5 * tok // (2 * experts_n)
    slots_n = experts_n * capacity
    order = [lax.rem(dp - j + n, n) for j in range(n)]

    x_blocks = gather_dp(inputs[0], n)
    n_gain, n_bias = gain_attn.shape[0], position_bias.shape[0]
    extra = jnp.concatenate([gain_attn, gain_moe, position_bias])
    extra = jnp.zeros((16, own), BF16).at[0, : 2 * n_gain + n_bias].set(extra)
    columns = jnp.concatenate([w_query, w_key, w_value], axis=0).reshape(3 * wrows, n, own)
    columns = jnp.concatenate(
        [jnp.swapaxes(columns, 0, 1), jnp.broadcast_to(extra, (n, 16, own))], axis=1
    )
    shares = [pick(columns, dp)] + [
        shift(pick(columns, lax.rem(dp + d, n)), d, n) for d in range(1, n)
    ]
    plane = jnp.concatenate(shares, axis=1)
    plane_all = jnp.stack(
        [plane]
        + [
            lax.ppermute(plane, "expert", [(i, i ^ k) for i in range(experts_n)])
            for k in range(1, experts_n)
        ]
    )
    plane_all = jnp.stack([pick(plane_all, ex ^ j) for j in range(experts_n)])
    by_block = plane_all.reshape(experts_n, 3 * wrows + 16, n, own)
    by_block = jnp.stack([lax.dynamic_index_in_dim(by_block, order[j], 2, keepdims=False) for j in range(n)])
    wqkv = (
        by_block[:, :, : 3 * wrows]
        .reshape(n, experts_n, 3, wrows, own)
        .transpose(0, 1, 3, 2, 4)
        .reshape(width, 3 * own)
    )
    extras = by_block[:, :, 3 * wrows]
    gain_one = extras[:, :, :n_gain].reshape(-1).astype(F32)
    gain_two = extras[:, :, n_gain : 2 * n_gain].reshape(-1).astype(F32)
    table = extras[:, :, 2 * n_gain : 2 * n_gain + n_bias].reshape(BUCKETS, HEADS)
    table = lax.dynamic_slice_in_dim(table, dp * heads_own, heads_own, 1)

    outs = jnp.stack(gather_dp(w_out, n))
    outs_all = jnp.stack(
        [outs]
        + [
            lax.ppermute(outs, "expert", [(i, i ^ k) for i in range(experts_n)])
            for k in range(1, experts_n)
        ]
    )
    outs_all = jnp.stack([pick(outs_all, ex ^ j) for j in range(experts_n)])
    w_out_all = jnp.swapaxes(outs_all, 0, 1).reshape(width, width)

    meta = jnp.concatenate([routes[0].T, gate_fixed], axis=0)
    meta_all = jnp.stack(gather_dp(meta, n))
    cot_blocks = gather_dp(cotangent[0], n)

    packed = pack_columns(n, w_gate[0], w_up[0])
    halves = [pick(packed, dp)] + [
        shift(pick(packed, lax.rem(dp + d, n)), d, n) for d in range(1, n)
    ]
    halves = jnp.stack(halves)
    wgu = jnp.concatenate([pick(halves, order[j]) for j in range(n)], axis=0)
    deep = w_down.shape[1]
    padded = -(-deep // 128) * 128
    wd = jnp.pad(w_down[0], ((0, padded - deep), (0, 0)))

    x_all = jnp.concatenate(x_blocks, axis=0).astype(F32)
    _, normed = norm_forward(x_all, gain_one)
    qkv = mm(normed, wqkv).astype(BF16)
    wide = 2 * length
    offsets = jnp.arange(wide, dtype=jnp.int32) - length
    in_bucket = (bucket_of(offsets)[:, None] == jnp.arange(BUCKETS, dtype=jnp.int32)).astype(BF16)
    in_bucket = jnp.where(jnp.abs(offsets)[:, None] < length, in_bucket, jnp.zeros_like(in_bucket))
    vectors = mm(table, in_bucket, (((0,), (1,)), ((), ())))
    place = jnp.reshape(dp, (1,)).astype(jnp.int32)
    mixed_heads, lse = attention_forward(place, n, qkv, vectors)
    mixed_blocks = [mixed_heads[:tok]] + [None] * (n - 1)
    for d in range(1, n):
        mixed_blocks[n - d] = shift(mixed_heads[d * tok : (d + 1) * tok], n - d, n)
    mixed = jnp.concatenate(mixed_blocks, axis=1)
    tokens = inputs[0].astype(F32)
    resid = tokens + mm(mixed, w_out_all)
    inverse_two, normed_two = norm_forward(resid, gain_two)
    normed_two_blocks = gather_dp(normed_two, n)

    ids = jnp.arange(experts_n, dtype=jnp.int32)
    pair = meta_all[:, :2]
    hot = (pair[..., None] == ids).astype(F32)
    earlier_tokens = jnp.tril(jnp.ones((tok, tok), BF16), -1)
    counts = jnp.einsum(
        "ts,gse->gte", earlier_tokens, jnp.sum(hot, axis=1).astype(BF16), preferred_element_type=F32
    )
    slot = jnp.sum(counts[:, None] * hot, axis=-1)
    slot = slot + jnp.stack([jnp.zeros_like(slot[:, 0]), (pair[:, 0] == pair[:, 1]).astype(F32)], axis=1)
    slot = slot.astype(jnp.int32)
    dest = jnp.where(slot < capacity, pair * capacity + slot, -1)
    select = (dest[..., None] == jnp.arange(slots_n, dtype=jnp.int32)).astype(BF16)
    both = select[:, 0] + select[:, 1]
    first_gate = meta_all[:, 2].astype(F32) / 65536.0
    gates = jnp.stack([first_gate, 1.0 - first_gate], axis=1)
    slot_gate = jnp.sum(select.astype(F32) * gates[..., None], axis=(1, 2))

    def to_experts(groups, rows):
        sent = jnp.swapaxes(rows.reshape(groups, experts_n, capacity, width), 0, 1)
        return exchange(sent.reshape(experts_n, groups * capacity, width))

    def dispatch(maps, blocks, factor):
        rows = jnp.einsum("gts,gtd->gsd", maps, blocks, preferred_element_type=F32)
        if factor is not None:
            rows = rows * factor[..., None]
        return to_experts(maps.shape[0], rows.astype(BF16))

    cut = n // 2
    cot_all = jnp.stack(cot_blocks)
    two_all = jnp.stack(normed_two_blocks)
    d_outs = [
        dispatch(both[:cut], cot_all[:cut], slot_gate[:cut]),
        dispatch(both[cut:], cot_all[cut:], slot_gate[cut:]),
    ]
    slots = [dispatch(both[:cut], two_all[:cut], None), dispatch(both[cut:], two_all[cut:], None)]

    steps = 8
    out_rows, dslot_rows, gwgu, gwd = experts(slots, d_outs, wgu, wd, steps)
    grad_w_down = gwd[:deep]

    def from_experts(rows):
        sides = []
        for side in range(2):
            part = rows.reshape(steps, 2, -1, width)[:, side].reshape(experts_n, cut * capacity, width)
            back = exchange(part).reshape(experts_n, cut, capacity, width)
            sides.append(jnp.swapaxes(back, 0, 1).reshape(cut, slots_n, width))
        return sides

    def to_owners(blocks):
        total = blocks[0].astype(F32)
        for d in range(1, n):
            total = total + shift(blocks[d].astype(BF16), n - d, n).astype(F32)
        return total

    dslot_back = from_experts(dslot_rows)
    partial = [
        jnp.einsum("gts,gsd->gtd", both[:cut], dslot_back[0], preferred_element_type=F32),
        jnp.einsum("gts,gsd->gtd", both[cut:], dslot_back[1], preferred_element_type=F32),
    ]
    grad_normed_two = to_owners([partial[d // cut][d % cut] for d in range(n)])
    grad_top = cotangent[0].astype(F32)
    grad_gain_two, grad_resid_norm = norm_backward(resid, inverse_two, gain_two, grad_normed_two)
    grad_resid = grad_top + grad_resid_norm
    grad_attn_low = grad_resid.astype(BF16)
    d_mixed = mm(grad_attn_low, w_out_all, NT).astype(BF16)
    d_mixed_heads = jnp.concatenate(
        [d_mixed[:, :own]]
        + [None] * 0
        + [
            part
            for _, part in sorted(
                (n - d, shift(d_mixed[:, d * own : (d + 1) * own], n - d, n)) for d in range(1, n)
            )
        ],
        axis=0,
    )
    grad_w_out_part = mm(mixed, grad_attn_low, TN)

    dq, dk, dv, diagonals = attention_backward(place, n, qkv, lse, d_mixed_heads, vectors)
    d_qkv = jnp.concatenate([dq, dk, dv], axis=1)
    d_normed_part = mm(d_qkv, wqkv, NT)
    grad_normed = to_owners([d_normed_part[d * tok : (d + 1) * tok] for d in range(n)])
    grad_wqkv_part = mm(normed, d_qkv, TN)
    inverse_one = lax.rsqrt(jnp.mean(tokens * tokens, axis=-1, keepdims=True) + EPSILON)
    grad_gain_one, grad_tok_norm = norm_backward(tokens, inverse_one, gain_one, grad_normed)
    grad_inputs = (grad_resid + grad_tok_norm).astype(BF16)

    out_back = from_experts(out_rows)
    moe = []
    for side in range(2):
        part = select[side * cut : (side + 1) * cut]
        picked = jnp.einsum("gcts,gsd->gctd", part, out_back[side], preferred_element_type=F32)
        moe.append(jnp.sum(picked * gates[side * cut : (side + 1) * cut, :, :, None], axis=1))
    block_out = (resid + to_owners([moe[d // cut][d % cut] for d in range(n)])).astype(BF16)

    pieces = gwgu.reshape(n, tok * 0 + width // n, gwgu.shape[1])
    got = [pick(pieces, dp)] + [
        shift(pick(pieces, lax.rem(dp + d, n)), d, n) for d in range(1, n)
    ]
    got = jnp.stack(got)
    grad_w_gate, grad_w_up = unpack_columns(jnp.stack([pick(got, order[j]) for j in range(n)]))

    def plane_sum(parts):
        return jnp.sum(exchange(parts.astype(BF16)).astype(F32), axis=0)

    go = grad_w_out_part.reshape(n, experts_n, wrows, width)
    go = plane_sum(jnp.swapaxes(go, 0, 1))
    grad_w_out = to_owners([go[d] for d in range(n)])

    gq = grad_wqkv_part.reshape(n, experts_n, wrows, 3 * own)
    gq = plane_sum(jnp.swapaxes(gq, 0, 1)).astype(BF16)
    gq_parts = [pick(gq, dp)] + [shift(pick(gq, lax.rem(dp + d, n)), d, n) for d in range(1, n)]
    gq_parts = jnp.stack(gq_parts)
    gq_all = jnp.stack([pick(gq_parts, order[j]) for j in range(n)]).astype(F32)
    gq_all = gq_all.reshape(n, wrows, 3, own).transpose(2, 1, 0, 3).reshape(3, wrows, width)

    diag_rows = jnp.roll(diagonals.reshape(heads_own, wide), tok, axis=1)
    grad_table = lax.dot_general(
        in_bucket.astype(F32), diag_rows, (((0,), (1,)), ((), ())), precision=lax.Precision.HIGHEST,
        preferred_element_type=F32,
    )
    grad_table = lax.dynamic_update_slice_in_dim(
        jnp.zeros((BUCKETS, HEADS), F32), grad_table, dp * heads_own, 1
    )
    small = jnp.concatenate([grad_gain_one, grad_gain_two, grad_table.reshape(-1)]).reshape(-1, 128)
    step = 1
    while step < experts_n:
        small = small + lax.ppermute(small, "expert", [(i, i ^ step) for i in range(experts_n)])
        step *= 2
    small = sum(gather_dp(small, n)[1:], small).reshape(-1)
    me = dp * experts_n + ex
    grad_gain_attn = lax.dynamic_slice_in_dim(small, me * n_gain, n_gain)
    grad_gain_moe = lax.dynamic_slice_in_dim(small, width + me * n_gain, n_gain)
    grad_bias = lax.dynamic_slice_in_dim(small, 2 * width + me * n_bias, n_bias)

    return (
        block_out[None],
        grad_inputs[None],
        grad_gain_attn,
        gq_all[0],
        gq_all[1],
        gq_all[2],
        grad_w_out,
        grad_bias,
        grad_gain_moe,
        grad_w_gate[None],
        grad_w_up[None],
        grad_w_down[None],
    )


def solution(mesh):
    vector = P(("dp", "expert"))
    matrix = P(("dp", "expert"), None)
    split = P("expert", "dp", None)
    return jax.shard_map(
        local,
        mesh=mesh,
        in_specs=(
            split, split, vector, matrix, matrix, matrix, matrix, vector, vector,
            split, split, split, split, P("expert", "dp"),
        ),
        out_specs=(
            split, split, vector, matrix, matrix, matrix, matrix, vector, vector,
            split, split, split,
        ),
        check_vma=False,
    )
```

time: 1530 us -> 861 us (0.56)
  waiting for transfers between devices: 893 us -> 334 us
  starting transfers between devices: 27.8 us -> 223 us
  matrix products: 188 us -> 33.1 us
  Pallas kernels: 0 us -> 101 us
  local copies, waits for them, and re-layouts: 180 us -> 84.1 us
  blocking collectives: 127 us -> 36 us
  other arithmetic: 96.8 us -> 37.6 us
    reduce_scatter x8 -> x0, waiting for transfers between devices: 577 us -> none  [the longest x1 140 us: local(): lax.psum_scatter(grad_w_key, ('dp', 'expert'), scatter_dimension=0, tiled...]
    ppermute x0 -> x65, waiting for transfers between devices: none -> 273 us  [the longest x48 237 us: shift(): lax.ppermute(value, 'dp', [(i, (i + distance) % n) for i in range(n)])]
    ppermute x0 -> x65, starting transfers between devices: none -> 185 us  [the longest x48 164 us: shift(): lax.ppermute(value, 'dp', [(i, (i + distance) % n) for i in range(n)])]
    all_gather x8 -> x0, waiting for transfers between devices: 180 us -> none  [the longest x1 54.7 us: local(): lax.all_gather(w_value, ('dp', 'expert'), axis=0, tiled=True)]
    dot_general x33 -> x17, matrix products: 188 us -> 33.1 us  [the longest x7 19.9 us: mm(): return lax.dot_general(a, b, dims, preferred_element_type=F32)]
    pallas_call x0 -> x5, Pallas kernels: none -> 101 us  [the longest x1 53.6 us: experts(): pl.pallas_call(functools.partial(expert_kernel, main), grid=(steps,), in_...]
    unnamed x2 -> x0, blocking collectives: 84.9 us -> none
    all_to_all x6 -> x9, waiting for transfers between devices: 134 us -> 61.3 us  [exchange(): lax.all_to_all(value, 'expert', split_axis=0, concat_axis=0, tiled=True)]
  transfers between devices with their start and end apart: 22 -> 74, of which waited for: 18 -> 31; matrix products, arithmetic and copies ran while one was open for 27% -> 16% of each run, Pallas kernels for 0% -> 3%
where the time goes in v1:
time: 861 us; the launch traced here: 851 us
  waiting for transfers between devices  334 us (39%)
  starting transfers between devices  223 us (26%)
  Pallas kernels  101 us (12%)
  local copies, waits for them, and re-layouts  84.1 us (10%)
  other arithmetic  37.6 us (4%)
  blocking collectives  36 us (4%)
  matrix products  33.1 us (4%)
    ppermute x48, waiting for transfers between devices, shift(): lax.ppermute(value, 'dp', [(i, (i + distance) % n) for i in range(n)])  237 us
    ppermute x48, starting transfers between devices, shift(): lax.ppermute(value, 'dp', [(i, (i + distance) % n) for i in range(n)])  164 us
    all_to_all x9, waiting for transfers between devices, exchange(): lax.all_to_all(value, 'expert', split_axis=0, concat_axis=0, tiled=True)  61.3 us
    pallas_call x1, Pallas kernels, experts(): pl.pallas_call(functools.partial(expert_kernel, main), grid=(steps,), in_...  53.6 us
    all_to_all x9, starting transfers between devices, exchange(): lax.all_to_all(value, 'expert', split_axis=0, concat_axis=0, tiled=True)  38.5 us
    all_to_all x1, blocking collectives, exchange(): lax.all_to_all(value, 'expert', split_axis=0, concat_axis=0, tiled=True)  36 us
    pallas_call x1, Pallas kernels, attention_backward(): pl.pallas_call(functools.partial(attention_backward_kernel, n, block), gr...  23.4 us
    unnamed x97, local copies, waits for them, and re-layouts  21.5 us
  transfers between devices with their start and end apart: 74, of which 31 were waited for; matrix products, arithmetic and copies ran while one was open for 16% of the time, Pallas kernels for 3%

profile of v1, /device:TPU:0, one launch (start us, length us, event | category | flops | bytes accessed | tf_op | source)
XLA Modules:
  0.0 851.2 jit_solution(9411748992317835309)
XLA Ops:
  44.9 6.9 collective-permute-done.10
  122.1 13.0 %collective-permute-done.32 = bf16[256,1024]{1,0:T(8,128)(2,1)S(1)} collective-permute-done((bf16[256,1024]{1,0:T(8,128)(2,1)}, bf16[256,1024]{1,0:T(8,128)(2,1)S(1)}, u32[]{:S(2)}, u32[]{:S(2)}) %collective-permute-start.32) | collective-permute-done | bytes 524320 | tf_op jit(solution)/shard_map/ppermute | solution.py:385
  149.9 14.7 %attention_forward.1 = (bf16[1024,256]{1,0:T(8,128)(2,1)}, f32[1024,256]{1,0:T(8,128)}) custom-call(s32[1]{0:T(128)} %bitcast.1.dp_ref, bf16[1024,768]{1,0:T(8,128)(2,1)} %convolution_convert_fusion.4.q_ref.k_ref.v_ref, bf16[1024,768]{1,0:T(8,128)(2,1)} %convolution_convert_fusion.4.q_ref.k_ref.v_ref, ...), custom_call_target="tpu_custom_call" | custom-call | flops 4294967296 | bytes 1572864 | tf_op jit(solution)/shard_map/attention_forward/pallas_call | solution.py:111
  165.7 8.3 collective-permute-start.13
  194.9 21.3 %collective-permute-done.30 = bf16[256,1024]{1,0:T(8,128)(2,1)S(1)} collective-permute-done((bf16[256,1024]{1,0:T(8,128)(2,1)S(1)}, bf16[256,1024]{1,0:T(8,128)(2,1)S(1)}, u32[]{:S(2)}, u32[]{:S(2)}) %collective-permute-start.30) | collective-permute-done | bytes 524320 | tf_op jit(solution)/shard_map/ppermute | solution.py:385
  223.2 10.9 %collective-permute-start.29 = (bf16[256,1024]{1,0:T(8,128)(2,1)S(1)}, bf16[256,1024]{1,0:T(8,128)(2,1)S(1)}, u32[]{:S(2)}, u32[]{:S(2)}) collective-permute-start(bf16[256,1024]{1,0:T(8,128)(2,1)S(1)} %multiply_convert_fusion.2), channel_id=1, source_target_pairs={{0,8},{8,16},{16,24},{24,0},{1,9},{9,17},{17,25},{25,1},{2,10},{10... | collective-permute-start | bytes 1572872 | tf_op jit(solution)/shard_map/ppermute | solution.py:385
  234.3 14.9 %collective-permute-done.29 = bf16[256,1024]{1,0:T(8,128)(2,1)S(1)} collective-permute-done((bf16[256,1024]{1,0:T(8,128)(2,1)S(1)}, bf16[256,1024]{1,0:T(8,128)(2,1)S(1)}, u32[]{:S(2)}, u32[]{:S(2)}) %collective-permute-start.29) | collective-permute-done | bytes 524320 | tf_op jit(solution)/shard_map/ppermute | solution.py:385
  266.3 10.9 %collective-permute-start.35 = (bf16[256,1408]{1,0:T(8,128)(2,1)S(1)}, bf16[256,1408]{1,0:T(8,128)(2,1)S(1)}, u32[]{:S(2)}, u32[]{:S(2)}) collective-permute-start(bf16[256,1408]{1,0:T(8,128)(2,1)S(1)} %get-tuple-element.73), channel_id=1, source_target_pairs={{0,8},{8,16},{16,24},{24,0},{1,9},{9,17},{17,25},{25,1},{2,10},{10... | collective-permute-start | bytes 2162696 | tf_op jit(solution)/shard_map/ppermute | solution.py:385
  282.1 14.9 %collective-permute-done.35 = bf16[256,1408]{1,0:T(8,128)(2,1)S(1)} collective-permute-done((bf16[256,1408]{1,0:T(8,128)(2,1)S(1)}, bf16[256,1408]{1,0:T(8,128)(2,1)S(1)}, u32[]{:S(2)}, u32[]{:S(2)}) %collective-permute-start.35) | collective-permute-done | bytes 720928 | tf_op jit(solution)/shard_map/ppermute | solution.py:385
  297.0 30.5 %collective-permute-done.36 = bf16[256,1408]{1,0:T(8,128)(2,1)S(1)} collective-permute-done((bf16[256,1408]{1,0:T(8,128)(2,1)S(1)}, bf16[256,1408]{1,0:T(8,128)(2,1)S(1)}, u32[]{:S(2)}, u32[]{:S(2)}) %collective-permute-start.36) | collective-permute-done | bytes 720928 | tf_op jit(solution)/shard_map/ppermute | solution.py:385
  334.1 53.6 %experts.1 = (bf16[8,320,1024]{2,1,0:T(8,128)(2,1)}, bf16[8,320,1024]{2,1,0:T(8,128)(2,1)}, bf16[1024,1408]{1,0:T(8,128)(2,1)}, f32[768,1024]{1,0:T(8,128)}) custom-call(bf16[8,160,1024]{2,1,0:T(8,128)(2,1)} %all-to-all-done.slots_a, bf16[8,160,1024]{2,1,0:T(8,128)(2,1)} %all-to-all-done.1.slots_b, bf16[8,160,1024]{2,1,0:T(8,128)(2,1)} %all-to-all-done.2.dout_a, ...), custom_call_target="tpu_custom_call" | custom-call | flops 34225520640 | bytes 32505856 | tf_op jit(solution)/shard_map/experts/pallas_call | solution.py:297
  392.4 36.0 %all_to_all.50 = bf16[8,160,1024]{2,1,0:T(8,128)(2,1)} all-to-all(bf16[8,160,1024]{2,1,0:T(8,128)(2,1)S(1)} %get-tuple-element.54), channel_id=1, replica_groups=mesh['dp'=4,'expert'=8] {'expert'}, dimensions={0} | all-to-all | bytes 5242880 | tf_op jit(solution)/shard_map/all_to_all | solution.py:397
  438.6 26.5 %all-to-all-done.7 = bf16[8,160,1024]{2,1,0:T(8,128)(2,1)} async-done(((bf16[8,160,1024]{2,1,0:T(8,128)(2,1)}), bf16[8,160,1024]{2,1,0:T(8,128)(2,1)}, u32[]{:S(2)}, u32[]{:S(2)}) %all-to-all-start.7) | async-done | bytes 2621472 | tf_op jit(solution)/shard_map/all_to_all | solution.py:397
  470.8 31.0 %all-to-all-done.4 = bf16[8,160,1024]{2,1,0:T(8,128)(2,1)} async-done(((bf16[8,160,1024]{2,1,0:T(8,128)(2,1)}), bf16[8,160,1024]{2,1,0:T(8,128)(2,1)}, u32[]{:S(2)}, u32[]{:S(2)}) %all-to-all-start.4) | async-done | bytes 2621472 | tf_op jit(solution)/shard_map/all_to_all | solution.py:397
  512.6 15.9 %collective-permute-start.62 = (bf16[256,1408]{1,0:T(8,128)(2,1)}, bf16[256,1408]{1,0:T(8,128)(2,1)}, u32[]{:S(2)}, u32[]{:S(2)}) collective-permute-start(bf16[256,1408]{1,0:T(8,128)(2,1)} %get-tuple-element.65), channel_id=1, source_target_pairs={{0,8},{8,16},{16,24},{24,0},{1,9},{9,17},{17,25},{25,1},{2,10},{10... | collective-permute-start | bytes 2162696 | tf_op jit(solution)/shard_map/ppermute | solution.py:385
  553.1 19.0 %collective-permute-done.41 = bf16[256,1024]{1,0:T(8,128)(2,1)} collective-permute-done((bf16[256,1024]{1,0:T(8,128)(2,1)}, bf16[256,1024]{1,0:T(8,128)(2,1)}, u32[]{:S(2)}, u32[]{:S(2)}) %collective-permute-start.41) | collective-permute-done | bytes 524320 | tf_op jit(solution)/shard_map/ppermute | solution.py:385
  576.4 44.2 %collective-permute-done.42 = bf16[256,1024]{1,0:T(8,128)(2,1)S(1)} collective-permute-done((bf16[256,1024]{1,0:T(8,128)(2,1)}, bf16[256,1024]{1,0:T(8,128)(2,1)S(1)}, u32[]{:S(2)}, u32[]{:S(2)}) %collective-permute-start.42) | collective-permute-done | bytes 524320 | tf_op jit(solution)/shard_map/ppermute | solution.py:385
  620.6 23.1 %collective-permute-start.40 = (bf16[256,1024]{1,0:T(8,128)(2,1)S(1)}, bf16[256,1024]{1,0:T(8,128)(2,1)S(1)}, u32[]{:S(2)}, u32[]{:S(2)}) collective-permute-start(bf16[256,1024]{1,0:T(8,128)(2,1)S(1)} %get-tuple-element.88), channel_id=1, source_target_pairs={{0,8},{8,16},{16,24},{24,0},{1,9},{9,17},{17,25},{25,1},{2,10},{10... | collective-permute-start | bytes 1572872 | tf_op jit(solution)/shard_map/ppermute | solution.py:385
  645.3 20.2 %collective-permute-done.39 = bf16[256,1024]{1,0:T(8,128)(2,1)S(1)} collective-permute-done((bf16[256,1024]{1,0:T(8,128)(2,1)S(1)}, bf16[256,1024]{1,0:T(8,128)(2,1)S(1)}, u32[]{:S(2)}, u32[]{:S(2)}) %collective-permute-start.39) | collective-permute-done | bytes 524320 | tf_op jit(solution)/shard_map/ppermute | solution.py:385
  670.4 15.8 %collective-permute-start.44 = (bf16[256,256]{1,0:T(8,128)(2,1)S(1)}, bf16[256,256]{1,0:T(8,128)(2,1)S(1)}, u32[]{:S(2)}, u32[]{:S(2)}) collective-permute-start(bf16[256,256]{1,0:T(8,128)(2,1)S(1)} %get-tuple-element.95), channel_id=1, source_target_pairs={{0,8},{8,16},{16,24},{24,0},{1,9},{9,17},{17,25},{25,1},{2,10},{10... | collective-permute-start | bytes 393224 | tf_op jit(solution)/shard_map/ppermute | solution.py:385
  699.1 23.4 %attention_backward.1 = (bf16[1024,256]{1,0:T(8,128)(2,1)}, bf16[1024,256]{1,0:T(8,128)(2,1)}, bf16[1024,256]{1,0:T(8,128)(2,1)}, f32[2,2,2048]{2,1,0:T(2,128)}) custom-call(s32[1]{0:T(128)} %bitcast.1.dp_ref, bf16[1024,768]{1,0:T(8,128)(2,1)} %convolution_convert_fusion.4.q_ref.k_ref.v_ref, bf16[1024,768]{1,0:T(8,128)(2,1)} %convolution_convert_fusion.4.q_ref.k_ref.v_ref, ...), custom_call_target="tpu_custom_call" | custom-call | flops 10737418240 | bytes 3670016 | tf_op jit(solution)/shard_map/attention_backward/pallas_call | solution.py:200
  749.0 8.7 %collective-permute-done.47 = bf16[256,1024]{1,0:T(8,128)(2,1)} collective-permute-done((bf16[256,1024]{1,0:T(8,128)(2,1)}, bf16[256,1024]{1,0:T(8,128)(2,1)}, u32[]{:S(2)}, u32[]{:S(2)}) %collective-permute-start.47) | collective-permute-done | bytes 524320 | tf_op jit(solution)/shard_map/ppermute | solution.py:385
  757.6 34.3 %collective-permute-done.48 = bf16[256,1024]{1,0:T(8,128)(2,1)} collective-permute-done((bf16[256,1024]{1,0:T(8,128)(2,1)}, bf16[256,1024]{1,0:T(8,128)(2,1)}, u32[]{:S(2)}, u32[]{:S(2)}) %collective-permute-start.48) | collective-permute-done | bytes 524320 | tf_op jit(solution)/shard_map/ppermute | solution.py:385
  814.3 10.2 %collective-permute-done.52 = f32[20,128]{1,0:T(8,128)S(1)} collective-permute-done((f32[20,128]{1,0:T(8,128)S(1)}, f32[20,128]{1,0:T(8,128)S(1)}, u32[]{:S(2)}, u32[]{:S(2)}) %collective-permute-start.52) | collective-permute-done | bytes 10272 | tf_op jit(solution)/shard_map/ppermute | solution.py:622
  (363 shorter events, 340.9 us)
Async XLA Ops:
  22.4 78.3 %collective-permute-start.33 = (bf16[256,1024]{1,0:T(8,128)(2,1)}, bf16[256,1024]{1,0:T(8,128)(2,1)}, u32[]{:S(2)}, u32[]{:S(2)}) collective-permute-start(bf16[256,1024]{1,0:T(8,128)(2,1)} %bitcast.60), channel_id=1, source_target_pairs={{0,16},{8,24},{16,0},{24,8},{1,17},{9,25},{17,1},{25,9},{2,18},{10... | collective-permute-start | bytes 1572872 | tf_op jit(solution)/shard_map/ppermute | solution.py:385
  23.4 78.6 %collective-permute-start.34 = (bf16[256,1024]{1,0:T(8,128)(2,1)}, bf16[256,1024]{1,0:T(8,128)(2,1)}, u32[]{:S(2)}, u32[]{:S(2)}) collective-permute-start(bf16[256,1024]{1,0:T(8,128)(2,1)} %bitcast.60), channel_id=1, source_target_pairs={{0,24},{8,0},{16,8},{24,16},{1,25},{9,1},{17,9},{25,17},{2,26},{10... | collective-permute-start | bytes 1572872 | tf_op jit(solution)/shard_map/ppermute | solution.py:385
  26.9 111.9 %collective-permute-start = (bf16[256,1024]{1,0:T(8,128)(2,1)}, bf16[256,1024]{1,0:T(8,128)(2,1)}, u32[]{:S(2)}, u32[]{:S(2)}) collective-permute-start(bf16[256,1024]{1,0:T(8,128)(2,1)} %bitcast), channel_id=1, source_target_pairs={{0,8},{8,16},{16,24},{24,0},{1,9},{9,17},{17,25},{25,1},{2,10},{10... | collective-permute-start | bytes 1572872 | tf_op jit(solution)/shard_map/ppermute | solution.py:385
  90.6 48.1 %collective-permute-start.1 = (bf16[256,1024]{1,0:T(8,128)(2,1)}, bf16[256,1024]{1,0:T(8,128)(2,1)}, u32[]{:S(2)}, u32[]{:S(2)}) collective-permute-start(bf16[256,1024]{1,0:T(8,128)(2,1)} %bitcast), channel_id=1, source_target_pairs={{0,16},{8,24},{16,0},{24,8},{1,17},{9,25},{17,1},{25,9},{2,18},{10... | collective-permute-start | bytes 1572872 | tf_op jit(solution)/shard_map/ppermute | solution.py:385
  96.7 42.0 %collective-permute-start.2 = (bf16[256,1024]{1,0:T(8,128)(2,1)}, bf16[256,1024]{1,0:T(8,128)(2,1)}, u32[]{:S(2)}, u32[]{:S(2)}) collective-permute-start(bf16[256,1024]{1,0:T(8,128)(2,1)} %bitcast), channel_id=1, source_target_pairs={{0,24},{8,0},{16,8},{24,16},{1,25},{9,1},{17,9},{25,17},{2,26},{10... | collective-permute-start | bytes 1572872 | tf_op jit(solution)/shard_map/ppermute | solution.py:385
  106.3 39.2 %all-to-all-start.3 = ((bf16[8,160,1024]{2,1,0:T(8,128)(2,1)}), bf16[8,160,1024]{2,1,0:T(8,128)(2,1)}, u32[]{:S(2)}, u32[]{:S(2)}) async-start(bf16[8,160,1024]{2,1,0:T(8,128)(2,1)} %bitcast.312), calls=%async_computation.3 | async-start | bytes 5242880 | tf_op jit(solution)/shard_map/all_to_all | solution.py:397
  145.5 73.3 %all-to-all-start.2 = ((bf16[8,160,1024]{2,1,0:T(8,128)(2,1)}), bf16[8,160,1024]{2,1,0:T(8,128)(2,1)}, u32[]{:S(2)}, u32[]{:S(2)}) async-start(bf16[8,160,1024]{2,1,0:T(8,128)(2,1)} %bitcast.311), calls=%async_computation.2 | async-start | bytes 5242880 | tf_op jit(solution)/shard_map/all_to_all | solution.py:397
  255.5 78.7 %all-to-all-start = ((bf16[8,160,1024]{2,1,0:T(8,128)(2,1)}), bf16[8,160,1024]{2,1,0:T(8,128)(2,1)}, u32[]{:S(2)}, u32[]{:S(2)}) async-start(bf16[8,160,1024]{2,1,0:T(8,128)(2,1)} %bitcast.313), calls=%async_computation | async-start | bytes 5242880 | tf_op jit(solution)/shard_map/all_to_all | solution.py:397
  277.2 50.3 %collective-permute-start.36 = (bf16[256,1408]{1,0:T(8,128)(2,1)S(1)}, bf16[256,1408]{1,0:T(8,128)(2,1)S(1)}, u32[]{:S(2)}, u32[]{:S(2)}) collective-permute-start(bf16[256,1408]{1,0:T(8,128)(2,1)S(1)} %get-tuple-element.72), channel_id=1, source_target_pairs={{0,16},{8,24},{16,0},{24,8},{1,17},{9,25},{17,1},{25,9},{2,18},{10... | collective-permute-start | bytes 2162696 | tf_op jit(solution)/shard_map/ppermute | solution.py:385
  280.4 47.1 %collective-permute-start.37 = (bf16[256,1408]{1,0:T(8,128)(2,1)S(1)}, bf16[256,1408]{1,0:T(8,128)(2,1)S(1)}, u32[]{:S(2)}, u32[]{:S(2)}) collective-permute-start(bf16[256,1408]{1,0:T(8,128)(2,1)S(1)} %get-tuple-element.71), channel_id=1, source_target_pairs={{0,24},{8,0},{16,8},{24,16},{1,25},{9,1},{17,9},{25,17},{2,26},{10... | collective-permute-start | bytes 2162696 | tf_op jit(solution)/shard_map/ppermute | solution.py:385
  501.8 44.5 %all-to-all-start.5 = ((bf16[8,160,1024]{2,1,0:T(8,128)(2,1)}), bf16[8,160,1024]{2,1,0:T(8,128)(2,1)}, u32[]{:S(2)}, u32[]{:S(2)}) async-start(bf16[8,160,1024]{2,1,0:T(8,128)(2,1)} %get-tuple-element.57), calls=%async_computation.5 | async-start | bytes 5242880 | tf_op jit(solution)/shard_map/all_to_all | solution.py:397
  512.6 176.9 %collective-permute-start.62 = (bf16[256,1408]{1,0:T(8,128)(2,1)}, bf16[256,1408]{1,0:T(8,128)(2,1)}, u32[]{:S(2)}, u32[]{:S(2)}) collective-permute-start(bf16[256,1408]{1,0:T(8,128)(2,1)} %get-tuple-element.65), channel_id=1, source_target_pairs={{0,8},{8,16},{16,24},{24,0},{1,9},{9,17},{17,25},{25,1},{2,10},{10... | collective-permute-start | bytes 2162696 | tf_op jit(solution)/shard_map/ppermute | solution.py:385
  528.5 162.6 %collective-permute-start.63 = (bf16[256,1408]{1,0:T(8,128)(2,1)}, bf16[256,1408]{1,0:T(8,128)(2,1)}, u32[]{:S(2)}, u32[]{:S(2)}) collective-permute-start(bf16[256,1408]{1,0:T(8,128)(2,1)} %get-tuple-element.64), channel_id=1, source_target_pairs={{0,16},{8,24},{16,0},{24,8},{1,17},{9,25},{17,1},{25,9},{2,18},{10... | collective-permute-start | bytes 2162696 | tf_op jit(solution)/shard_map/ppermute | solution.py:385
  533.7 38.4 %collective-permute-start.41 = (bf16[256,1024]{1,0:T(8,128)(2,1)}, bf16[256,1024]{1,0:T(8,128)(2,1)}, u32[]{:S(2)}, u32[]{:S(2)}) collective-permute-start(bf16[256,1024]{1,0:T(8,128)(2,1)} %fusion.51), channel_id=1, source_target_pairs={{0,24},{8,0},{16,8},{24,16},{1,25},{9,1},{17,9},{25,17},{2,26},{10... | collective-permute-start | bytes 1572872 | tf_op jit(solution)/shard_map/ppermute | solution.py:385
  540.1 80.5 %collective-permute-start.42 = (bf16[256,1024]{1,0:T(8,128)(2,1)}, bf16[256,1024]{1,0:T(8,128)(2,1)S(1)}, u32[]{:S(2)}, u32[]{:S(2)}) collective-permute-start(bf16[256,1024]{1,0:T(8,128)(2,1)} %get-tuple-element.85), channel_id=1, source_target_pairs={{0,16},{8,24},{16,0},{24,8},{1,17},{9,25},{17,1},{25,9},{2,18},{10... | collective-permute-start | bytes 1572872 | tf_op jit(solution)/shard_map/ppermute | solution.py:385
  541.2 79.4 %collective-permute-start.43 = (bf16[256,1024]{1,0:T(8,128)(2,1)}, bf16[256,1024]{1,0:T(8,128)(2,1)S(1)}, u32[]{:S(2)}, u32[]{:S(2)}) collective-permute-start(bf16[256,1024]{1,0:T(8,128)(2,1)} %get-tuple-element.86), channel_id=1, source_target_pairs={{0,8},{8,16},{16,24},{24,0},{1,9},{9,17},{17,25},{25,1},{2,10},{10... | collective-permute-start | bytes 1572872 | tf_op jit(solution)/shard_map/ppermute | solution.py:385
  572.1 73.2 %collective-permute-start.38 = (bf16[256,1024]{1,0:T(8,128)(2,1)S(1)}, bf16[256,1024]{1,0:T(8,128)(2,1)S(1)}, u32[]{:S(2)}, u32[]{:S(2)}) collective-permute-start(bf16[256,1024]{1,0:T(8,128)(2,1)S(1)} %fusion.50), channel_id=1, source_target_pairs={{0,24},{8,0},{16,8},{24,16},{1,25},{9,1},{17,9},{25,17},{2,26},{10... | collective-permute-start | bytes 1572872 | tf_op jit(solution)/shard_map/ppermute | solution.py:385
  620.6 45.0 %collective-permute-start.39 = (bf16[256,1024]{1,0:T(8,128)(2,1)S(1)}, bf16[256,1024]{1,0:T(8,128)(2,1)S(1)}, u32[]{:S(2)}, u32[]{:S(2)}) collective-permute-start(bf16[256,1024]{1,0:T(8,128)(2,1)S(1)} %get-tuple-element.87), channel_id=1, source_target_pairs={{0,16},{8,24},{16,0},{24,8},{1,17},{9,25},{17,1},{25,9},{2,18},{10... | collective-permute-start | bytes 1572872 | tf_op jit(solution)/shard_map/ppermute | solution.py:385
  620.6 45.0 %collective-permute-start.40 = (bf16[256,1024]{1,0:T(8,128)(2,1)S(1)}, bf16[256,1024]{1,0:T(8,128)(2,1)S(1)}, u32[]{:S(2)}, u32[]{:S(2)}) collective-permute-start(bf16[256,1024]{1,0:T(8,128)(2,1)S(1)} %get-tuple-element.88), channel_id=1, source_target_pairs={{0,8},{8,16},{16,24},{24,0},{1,9},{9,17},{17,25},{25,1},{2,10},{10... | collective-permute-start | bytes 1572872 | tf_op jit(solution)/shard_map/ppermute | solution.py:385
  645.3 45.9 %collective-permute-start.64 = (bf16[256,1408]{1,0:T(8,128)(2,1)S(1)}, bf16[256,1408]{1,0:T(8,128)(2,1)S(1)}, u32[]{:S(2)}, u32[]{:S(2)}) collective-permute-start(bf16[256,1408]{1,0:T(8,128)(2,1)S(1)} %copy-done.12), channel_id=1, source_target_pairs={{0,24},{8,0},{16,8},{24,16},{1,25},{9,1},{17,9},{25,17},{2,26},{10... | collective-permute-start | bytes 2162696 | tf_op jit(solution)/shard_map/ppermute | solution.py:385
  734.3 65.1 %all-to-all-start.8 = ((bf16[8,4,32,768]{3,2,1,0:T(8,128)(2,1)}), bf16[8,4,32,768]{3,2,1,0:T(8,128)(2,1)S(1)}, u32[]{:S(2)}, u32[]{:S(2)}) async-start(bf16[8,4,32,768]{3,2,1,0:T(8,128)(2,1)} %bitcast.322), calls=%async_computation.8 | async-start | bytes 3145728 | tf_op jit(solution)/shard_map/all_to_all | solution.py:397
  745.0 46.9 %collective-permute-start.48 = (bf16[256,1024]{1,0:T(8,128)(2,1)}, bf16[256,1024]{1,0:T(8,128)(2,1)}, u32[]{:S(2)}, u32[]{:S(2)}) collective-permute-start(bf16[256,1024]{1,0:T(8,128)(2,1)} %get-tuple-element.76), channel_id=1, source_target_pairs={{0,16},{8,24},{16,0},{24,8},{1,17},{9,25},{17,1},{25,9},{2,18},{10... | collective-permute-start | bytes 1572872 | tf_op jit(solution)/shard_map/ppermute | solution.py:385
  745.6 46.3 %collective-permute-start.49 = (bf16[256,1024]{1,0:T(8,128)(2,1)S(1)}, bf16[256,1024]{1,0:T(8,128)(2,1)}, u32[]{:S(2)}, u32[]{:S(2)}) collective-permute-start(bf16[256,1024]{1,0:T(8,128)(2,1)S(1)} %get-tuple-element.75), channel_id=1, source_target_pairs={{0,8},{8,16},{16,24},{24,0},{1,9},{9,17},{17,25},{25,1},{2,10},{10... | collective-permute-start | bytes 1572872 | tf_op jit(solution)/shard_map/ppermute | solution.py:385
  800.6 41.0 %all-to-all-start.9 = ((bf16[8,4,32,1024]{3,2,1,0:T(8,128)(2,1)}), bf16[8,4,32,1024]{3,2,1,0:T(8,128)(2,1)S(1)}, u32[]{:S(2)}, u32[]{:S(2)}) async-start(bf16[8,4,32,1024]{3,2,1,0:T(8,128)(2,1)} %bitcast.321), calls=%async_computation.9 | async-start | bytes 4194304 | tf_op jit(solution)/shard_map/all_to_all | solution.py:397
  (80 other events, 1049.1 us)

commit v2 on v1

v2 whole, which is shorter than its diff:
```python
import functools

import jax
import jax.numpy as jnp
from jax import lax
from jax.experimental import pallas as pl
from jax.experimental.pallas import tpu as pltpu
from jax.sharding import PartitionSpec as P

HEADS = 16
HEAD_DIM = 64
BUCKETS = 32
THRESHOLDS = (12, 16, 23, 32, 46, 64, 91)
EPSILON = 1e-06
SCALE = HEAD_DIM ** (-0.5)
BF16 = jnp.bfloat16
F32 = jnp.float32
GELU_C = 0.7978845608028654
GELU_A = 0.044715
VMEM_LIMIT = 56 * 1024 * 1024

NT = (((1,), (1,)), ((), ()))
TN = (((0,), (0,)), ((), ()))
NN = (((1,), (0,)), ((), ()))


def mm(a, b, dims=NN):
    return lax.dot_general(a, b, dims, preferred_element_type=F32)


def bucket_of(offset):
    distance = jnp.abs(offset)
    banded = jnp.full(distance.shape, 8, jnp.int32)
    for cutoff in THRESHOLDS:
        banded = banded + (distance >= cutoff).astype(jnp.int32)
    nearby = jnp.where(distance < 8, distance, banded)
    return nearby + jnp.where(offset > 0, 16, 0).astype(jnp.int32)


def norm_forward(values, gain):
    inverse = lax.rsqrt(jnp.mean(values * values, axis=-1, keepdims=True) + EPSILON)
    return (inverse, (values * inverse * gain).astype(BF16))


def norm_backward(values, inverse, gain, grad_normed):
    scaled = gain * grad_normed
    grad_gain = jnp.sum(grad_normed * values * inverse, axis=0)
    grad_values = inverse * scaled - values * inverse**3 * jnp.mean(
        scaled * values, axis=-1, keepdims=True
    )
    return (grad_gain, grad_values)


def bias_tile(vec_ref, head, tile_ref):
    block, wide = tile_ref.shape
    row = jnp.broadcast_to(vec_ref[pl.ds(head, 1), :], (block, wide))
    tile_ref[...] = pltpu.roll(row, wide - block, 1, stride=1, stride_axis=0)


def tile_offset(n, block, query_block, key_block):
    return pl.multiple_of((key_block - query_block + n - 1) * block, 128)


def logits_of(n, block, query_block, q_pair, k_pair, mask, tile_ref):
    masked = jnp.where(mask, q_pair, jnp.zeros_like(q_pair))
    raw = mm(masked, k_pair, NT) * SCALE
    bias = jnp.concatenate(
        [tile_ref[:, pl.ds(tile_offset(n, block, query_block, j), block)] for j in range(n)], axis=1
    )
    return raw + bias


def diagonal_sum(tile):
    rows, wide = tile.shape
    while rows > 1:
        half = rows // 2
        tile = tile[:half] + pltpu.roll(tile[half:], wide - half, 1)
        rows = half
    return tile


def attention_backward_kernel(
    n, block, q_ref, k_ref, v_ref, lse_ref, dm_ref, vec_ref,
    dq_ref, dk_ref, dv_ref, diag_ref, tiles, sums, dk_acc, dv_acc,
):
    pair, query_block = pl.program_id(0), pl.program_id(1)

    @pl.when(query_block == 0)
    def _():
        for side in range(2):
            bias_tile(vec_ref, 2 * pair + side, tiles.at[side])
        sums[...] = jnp.zeros_like(sums)
        dk_acc[...] = jnp.zeros_like(dk_acc)
        dv_acc[...] = jnp.zeros_like(dv_acc)

    q_pair, k_pair, v_pair, dm_pair = q_ref[...], k_ref[...], v_ref[...], dm_ref[...]
    rows = k_pair.shape[0]
    lane = lax.broadcasted_iota(jnp.int32, (block, 128), 1)
    dqs, dks, dvs = [], [], []
    for side in range(2):
        mask = (lane >= HEAD_DIM) if side else (lane < HEAD_DIM)
        logits = logits_of(n, block, query_block, q_pair, k_pair, mask, tiles.at[side])
        probs = jnp.exp(logits - lse_ref[:, side * HEAD_DIM : side * HEAD_DIM + 1])
        masked = jnp.where(mask, dm_pair, jnp.zeros_like(dm_pair))
        d_probs = mm(masked, v_pair, NT)
        inner = jnp.sum(probs * d_probs, axis=-1, keepdims=True)
        d_logits = (probs * (d_probs - inner)).astype(BF16)
        dvs.append(mm(probs.astype(BF16), dm_pair, TN))
        dqs.append(mm(d_logits, k_pair))
        dks.append(mm(d_logits, q_pair, TN))
        wide = d_logits.astype(F32)
        for j in range(n):
            here = pl.ds(tile_offset(n, block, query_block, j), block)
            sums[side, :, here] += wide[:, j * block : (j + 1) * block]
    dq_ref[...] = (jnp.where(lane < HEAD_DIM, dqs[0], dqs[1]) * SCALE).astype(BF16)
    key_lane = lax.broadcasted_iota(jnp.int32, (rows, 128), 1)
    dk_acc[...] += jnp.where(key_lane < HEAD_DIM, dks[0], dks[1])
    dv_acc[...] += jnp.where(key_lane < HEAD_DIM, dvs[0], dvs[1])

    @pl.when(query_block == n - 1)
    def _():
        dk_ref[...] = (dk_acc[...] * SCALE).astype(BF16)
        dv_ref[...] = dv_acc[...].astype(BF16)
        for side in range(2):
            diag_ref[0, pl.ds(side, 1), :] = diagonal_sum(sums[side])


def attention_backward(n, qkv, lse, d_mixed, vectors):
    rows, triple = qkv.shape
    own = triple // 3
    block = rows // n
    pairs = own // 128
    wide = vectors.shape[1]
    return pl.pallas_call(
        functools.partial(attention_backward_kernel, n, block),
        grid=(pairs, n),
        in_specs=[
            pl.BlockSpec((block, 128), lambda p, i: (i, p)),
            pl.BlockSpec((rows, 128), lambda p, i: (0, pairs + p)),
            pl.BlockSpec((rows, 128), lambda p, i: (0, 2 * pairs + p)),
            pl.BlockSpec((block, 128), lambda p, i: (i, p)),
            pl.BlockSpec((block, 128), lambda p, i: (i, p)),
            pl.BlockSpec((2 * pairs, wide), lambda p, i: (0, 0)),
        ],
        out_specs=[
            pl.BlockSpec((block, 128), lambda p, i: (i, p)),
            pl.BlockSpec((rows, 128), lambda p, i: (0, p)),
            pl.BlockSpec((rows, 128), lambda p, i: (0, p)),
            pl.BlockSpec((1, 2, wide), lambda p, i: (p, 0, 0)),
        ],
        out_shape=[
            jax.ShapeDtypeStruct((rows, own), BF16),
            jax.ShapeDtypeStruct((rows, own), BF16),
            jax.ShapeDtypeStruct((rows, own), BF16),
            jax.ShapeDtypeStruct((pairs, 2, wide), F32),
        ],
        scratch_shapes=[
            pltpu.VMEM((2, block, wide), F32),
            pltpu.VMEM((2, block, wide), F32),
            pltpu.VMEM((rows, 128), F32),
            pltpu.VMEM((rows, 128), F32),
        ],
        compiler_params=pltpu.CompilerParams(vmem_limit_bytes=VMEM_LIMIT),
        cost_estimate=pl.CostEstimate(
            flops=40 * rows * rows * own, bytes_accessed=14 * rows * own, transcendentals=rows * rows * own // 64
        ),
        name="attention_backward",
    )(qkv, qkv, qkv, lse, d_mixed, vectors)


def gelu_pair(v):
    square = v * v
    t = jnp.tanh(GELU_C * (v + GELU_A * v * square))
    half = 0.5 * (1.0 + t)
    slope = half + (0.5 * GELU_C) * v * (1.0 - t * t) * (1.0 + (3.0 * GELU_A) * square)
    return v * half, slope


def expert_kernel(
    main, slots_ref, dout_ref, wgu_ref, wd_ref,
    out_ref, dslot_ref, gwgu_ref, gwd_ref, gwgu_acc, gwd_acc,
):
    step = pl.program_id(0)

    @pl.when(step == 0)
    def _():
        gwgu_acc[...] = jnp.zeros_like(gwgu_acc)
        gwd_acc[...] = jnp.zeros_like(gwd_acc)

    slots, d_out = slots_ref[0], dout_ref[0]
    rows = slots.shape[0]
    wgu, wd = wgu_ref[...], wd_ref[...]
    pre = mm(slots, wgu)
    d_hidden = mm(d_out, wd, NT)
    low_lane = lax.broadcasted_iota(jnp.int32, (rows, 128), 1) < 64
    gate, up = pre[:, :main], pre[:, main : 2 * main]
    tail = pre[:, 2 * main :]
    tail_up = pltpu.roll(tail, 64, 1)
    act, slope = gelu_pair(gate)
    act_t, slope_t = gelu_pair(tail)
    hidden_t = jnp.where(low_lane, act_t * tail_up, 0.0)
    hidden = jnp.concatenate([(act * up).astype(BF16), hidden_t.astype(BF16)], axis=1)
    out_ref[0] = mm(hidden, wd).astype(BF16)
    gwd_acc[...] += mm(hidden, d_out, TN)
    dh, dh_t = d_hidden[:, :main], d_hidden[:, main:]
    d_gate = dh * up * slope
    d_up = dh * act
    d_tail = jnp.where(low_lane, dh_t * tail_up * slope_t, pltpu.roll(dh_t * act_t, 64, 1))
    d_pre = jnp.concatenate([d_gate.astype(BF16), d_up.astype(BF16), d_tail.astype(BF16)], axis=1)
    dslot_ref[0] = mm(d_pre, wgu, NT).astype(BF16)
    gwgu_acc[...] += mm(slots, d_pre, TN)

    @pl.when(step == pl.num_programs(0) - 1)
    def _():
        gwgu_ref[...] = gwgu_acc[...].astype(BF16)
        gwd_ref[...] = gwd_acc[...]


def experts(slots, d_outs, wgu, wd, steps):
    width, columns = wgu.shape
    deep = wd.shape[0]
    main = (columns - 128) // 2
    slots = slots.reshape(steps, -1, width)
    d_outs = d_outs.reshape(steps, -1, width)
    half = slots.shape[1]
    rows = half * steps
    part = pl.BlockSpec((1, half, width), lambda i: (i, 0, 0))
    return pl.pallas_call(
        functools.partial(expert_kernel, main),
        grid=(steps,),
        in_specs=[
            part, part,
            pl.BlockSpec((width, columns), lambda i: (0, 0)),
            pl.BlockSpec((deep, width), lambda i: (0, 0)),
        ],
        out_specs=[
            part, part,
            pl.BlockSpec((width, columns), lambda i: (0, 0)),
            pl.BlockSpec((deep, width), lambda i: (0, 0)),
        ],
        out_shape=[
            jax.ShapeDtypeStruct((steps, half, width), BF16),
            jax.ShapeDtypeStruct((steps, half, width), BF16),
            jax.ShapeDtypeStruct((width, columns), BF16),
            jax.ShapeDtypeStruct((deep, width), F32),
        ],
        scratch_shapes=[
            pltpu.VMEM((width, columns), F32),
            pltpu.VMEM((deep, width), F32),
        ],
        compiler_params=pltpu.CompilerParams(vmem_limit_bytes=VMEM_LIMIT),
        cost_estimate=pl.CostEstimate(
            flops=6 * rows * width * (columns + deep),
            bytes_accessed=8 * rows * width + 8 * width * columns,
            transcendentals=rows * deep,
        ),
        name="experts",
    )(slots, d_outs, wgu, wd)


def unpack_kernel(n, piece, in_ref, gate_ref, up_ref):
    main = piece // 128 * 128
    rest = piece - main
    gates, ups = [], []
    for j in range(n):
        block = in_ref[j].astype(F32)
        gates += [block[:, :main], block[:, 2 * main : 2 * main + rest]]
        ups += [block[:, main : 2 * main], block[:, 2 * main + rest :]]
    gate_ref[...] = jnp.concatenate(gates, axis=1)
    up_ref[...] = jnp.concatenate(ups, axis=1)


def unpack_columns(blocks):
    n, rows, both = blocks.shape
    piece = both // 2
    step = min(rows, 64)
    total = n * piece
    return pl.pallas_call(
        functools.partial(unpack_kernel, n, piece),
        grid=(rows // step,),
        in_specs=[pl.BlockSpec((n, step, both), lambda i: (0, i, 0))],
        out_specs=[pl.BlockSpec((step, total), lambda i: (i, 0))] * 2,
        out_shape=[jax.ShapeDtypeStruct((rows, total), F32)] * 2,
        compiler_params=pltpu.CompilerParams(vmem_limit_bytes=VMEM_LIMIT),
        cost_estimate=pl.CostEstimate(flops=0, bytes_accessed=12 * rows * total, transcendentals=0),
        name="unpack_columns",
    )(blocks)


MESH = pl.DeviceIdType.MESH


def remote(src, dst, send, recv, target):
    return pltpu.make_async_remote_copy(
        src_ref=src, dst_ref=dst, send_sem=send, recv_sem=recv, device_id=target, device_id_type=MESH
    )


def greet(n, ne, dp, ex):
    barrier = pltpu.get_barrier_semaphore()
    for d in range(1, n):
        pl.semaphore_signal(barrier, inc=1, device_id=(lax.rem(dp + d, n), ex), device_id_type=MESH)
    for k in range(1, ne):
        pl.semaphore_signal(barrier, inc=1, device_id=(dp, lax.rem(ex + k, ne)), device_id_type=MESH)
    pl.semaphore_wait(barrier, n + ne - 2)


class Chain:
    def __init__(self, n, dp, ex, own, buffer, send, recv):
        self.n, self.dp, self.ex, self.own = n, dp, ex, own
        self.buffer, self.send_sem, self.recv_sem = buffer, send, recv

    def block(self, hop, side):
        return lax.rem(self.dp + self.n + hop * (2 * side - 1), self.n)

    def copy(self, hop, side, first=False):
        at = self.block(hop, side)
        target = lax.rem(self.dp + self.n + 1 - 2 * side, self.n)
        return remote(
            self.own if first else self.buffer.at[at], self.buffer.at[at],
            self.send_sem.at[hop, side], self.recv_sem.at[hop, side], (target, self.ex),
        )

    def has_next(self, side):
        return (self.dp + 1 < self.n) if side == 0 else (self.dp > 0)

    def start(self):
        for side in range(2):
            @pl.when(self.has_next(side))
            def _():
                self.copy(0, side, True).start()

    def held(self, hop, side):
        return (self.dp > hop) if side == 0 else (self.dp + 1 + hop < self.n)

    def arrive(self, hop, side):
        at = self.block(hop + 1, side)
        remote(
            self.buffer.at[at], self.buffer.at[at], self.send_sem.at[hop, side], self.recv_sem.at[hop, side],
            (self.dp, self.ex),
        ).wait_recv()

        @pl.when(self.has_next(side))
        def _():
            self.copy(hop + 1, side).start()

        return at

    def finish(self):
        for hop in range(self.n - 1):
            for side in range(2):
                mine = self.has_next(side)
                if hop:
                    mine = mine & self.held(hop - 1, side)

                @pl.when(mine)
                def _():
                    self.copy(hop, side, hop == 0).wait_send()


def start_kernel(
    n, ne, cap, cap_pad, piece,
    x, wq, wk, wv, extra, wo, meta_in, wg, wu,
    x_all, lq, lk, lv, lext, lwo, meta_all, packed,
    sq, sk, sv, sext, swo, smeta,
    line_send, line_recv, plane_send, plane_recv, core_send, core_recv, chain_send, chain_recv, own_sem,
):
    dp, ex = lax.axis_index("dp"), lax.axis_index("expert")
    own = sq.shape[2]
    greet(n, ne, dp, ex)
    chain = Chain(n, dp, ex, x, x_all, chain_send, chain_recv)

    def column(ref, t):
        return ref.at[:, pl.ds(pl.multiple_of(t * own, 128), own)]

    def line(kind, d):
        t = lax.rem(dp + d, n)
        src, dst = [
            (column(wq, t), sq.at[dp]), (column(wk, t), sk.at[dp]), (column(wv, t), sv.at[dp]),
            (extra, sext.at[dp]), (wo, swo.at[dp]), (smeta, meta_all.at[dp]),
        ][kind]
        return remote(src, dst, line_send.at[kind, d], line_recv.at[kind, d], (t, ex))

    for d in range(1, n):
        for kind in range(4):
            line(kind, d).start()
    chain.start()
    for d in range(1, n):
        line(4, d).start()
    keep = pltpu.make_async_copy(x, x_all.at[dp], own_sem.at[0])
    keep.start()
    sq[dp] = wq[:, pl.ds(pl.multiple_of(dp * own, 128), own)]
    sk[dp] = wk[:, pl.ds(pl.multiple_of(dp * own, 128), own)]
    sv[dp] = wv[:, pl.ds(pl.multiple_of(dp * own, 128), own)]
    sext[dp] = extra[...]
    swo[dp] = wo[...]

    tok = meta_in.shape[1]
    routes = meta_in[...]
    ids = lax.broadcasted_iota(jnp.int32, (ne, tok), 0)
    first = (ids == routes[0:1, :]).astype(F32)
    second = (ids == routes[1:2, :]).astype(F32)
    before = (
        lax.broadcasted_iota(jnp.int32, (tok, tok), 0) < lax.broadcasted_iota(jnp.int32, (tok, tok), 1)
    ).astype(BF16)
    counts = mm((first + second).astype(BF16), before)
    slot_a = jnp.sum(counts * first, axis=0, keepdims=True)
    slot_b = jnp.sum((counts + first) * second, axis=0, keepdims=True)
    wide = routes.astype(F32)
    dest_a = jnp.where(slot_a < cap, wide[0:1, :] * cap_pad + slot_a, -1.0)
    dest_b = jnp.where(slot_b < cap, wide[1:2, :] * cap_pad + slot_b, -1.0)
    gate = wide[2:3, :] * (1.0 / 65536.0)
    smeta[...] = jnp.concatenate([dest_a, dest_b, gate, jnp.zeros((5, tok), F32)], axis=0)
    for d in range(1, n):
        line(5, d).start()
    keep_meta = pltpu.make_async_copy(smeta, meta_all.at[dp], own_sem.at[1])
    keep_meta.start()

    pairs = [(sq, lq), (sk, lk), (sv, lv), (sext, lext), (swo, lwo)]
    partner = ex + 1 - 2 * lax.rem(ex, 2)

    def plane(kind, k):
        src, dst = pairs[kind]
        return remote(
            src, dst.at[:, ex], plane_send.at[kind, k], plane_recv.at[kind, k],
            (dp, lax.rem(ex + 2 * k, ne)),
        )

    def core(kind, k):
        src, dst = pairs[kind]
        at = lax.rem(ex + ne - 2 * k, ne)
        return remote(
            src if k == 0 else dst.at[:, at], dst.at[:, at],
            core_send.at[kind, k], core_recv.at[kind, k], (dp, partner),
        )

    def spread(kind):
        for d in range(1, n):
            line(kind, d).wait_recv()
        for k in range(1, ne // 2):
            plane(kind, k).start()
        core(kind, 0).start()
        pltpu.make_async_copy(pairs[kind][0], pairs[kind][1].at[:, ex], own_sem.at[2 + kind]).start()

    for kind in range(4):
        spread(kind)

    main = piece // 128 * 128
    step = min(wg.shape[0], 64)

    @pl.loop(0, wg.shape[0] // step)
    def _(i):
        rows = pl.ds(pl.multiple_of(i * step, step), step)
        gate_w, up_w = wg[rows, :], wu[rows, :]
        for j in range(n):
            g = gate_w[:, j * piece : (j + 1) * piece]
            u = up_w[:, j * piece : (j + 1) * piece]
            packed[j, rows, :] = jnp.concatenate([g[:, :main], u[:, :main], g[:, main:], u[:, main:]], axis=1)

    spread(4)

    def pass_on(kind):
        for k in range(1, ne // 2):
            plane(kind, k).wait_recv()
            core(kind, k).start()

    def hop(h):
        for side in range(2):
            @pl.when(chain.held(h, side))
            def _():
                chain.arrive(h, side)

    hop(0)
    for kind in range(4):
        pass_on(kind)
    for h in range(1, n - 1):
        hop(h)
        if h == 1:
            pass_on(4)
    if n < 3:
        pass_on(4)
    for kind in range(5):
        for k in range(ne // 2):
            core(kind, k).wait()
        for k in range(1, ne // 2):
            plane(kind, k).wait_send()
        pltpu.make_async_copy(pairs[kind][0], pairs[kind][1].at[:, ex], own_sem.at[2 + kind]).wait()
    for d in range(1, n):
        for kind in range(6):
            line(kind, d).wait_send()
        line(5, d).wait_recv()
    chain.finish()
    keep.wait()
    keep_meta.wait()


def whole(array):
    return pl.BlockSpec(memory_space=pltpu.VMEM)


ANY = pl.BlockSpec(memory_space=pl.ANY)
VM = pl.BlockSpec(memory_space=pltpu.VMEM)


def start(n, ne, cap, cap_pad, x, wq, wk, wv, extra, wo, meta_in, wg, wu):
    tok, width = x.shape
    wrows = wq.shape[0]
    own = width // n
    piece = wg.shape[1] // n
    return pl.pallas_call(
        functools.partial(start_kernel, n, ne, cap, cap_pad, piece),
        in_specs=[VM] * 9,
        out_specs=[ANY] * 7 + [VM],
        out_shape=[
            jax.ShapeDtypeStruct((n, tok, width), BF16),
            jax.ShapeDtypeStruct((n, ne, wrows, own), BF16),
            jax.ShapeDtypeStruct((n, ne, wrows, own), BF16),
            jax.ShapeDtypeStruct((n, ne, wrows, own), BF16),
            jax.ShapeDtypeStruct((n, ne, 16, own), BF16),
            jax.ShapeDtypeStruct((n, ne, wrows, width), BF16),
            jax.ShapeDtypeStruct((n, 8, tok), F32),
            jax.ShapeDtypeStruct((n, tok, 2 * piece), BF16),
        ],
        scratch_shapes=[
            pltpu.VMEM((n, wrows, own), BF16),
            pltpu.VMEM((n, wrows, own), BF16),
            pltpu.VMEM((n, wrows, own), BF16),
            pltpu.VMEM((n, 16, own), BF16),
            pltpu.VMEM((n, wrows, width), BF16),
            pltpu.VMEM((8, tok), F32),
            pltpu.SemaphoreType.DMA((6, n)),
            pltpu.SemaphoreType.DMA((6, n)),
            pltpu.SemaphoreType.DMA((5, ne // 2)),
            pltpu.SemaphoreType.DMA((5, ne // 2)),
            pltpu.SemaphoreType.DMA((5, ne // 2)),
            pltpu.SemaphoreType.DMA((5, ne // 2)),
            pltpu.SemaphoreType.DMA((n, 2)),
            pltpu.SemaphoreType.DMA((n, 2)),
            pltpu.SemaphoreType.DMA((7,)),
        ],
        compiler_params=pltpu.CompilerParams(
            collective_id=1, has_side_effects=True, vmem_limit_bytes=VMEM_LIMIT
        ),
        name="start",
    )(x, wq, wk, wv, extra, wo, meta_in, wg, wu)


def forward_kernel(
    n, ne, cap_pad,
    x_all, wq, wk, wv, wo, gain_one, gain_two, vectors, cot, meta_all, packed,
    normed, qkv, lse, mixed, resid, slots, d_outs, wgu,
    heads, mixed_in, tiles, cot_all, two_all, two_own, two_rows, cot_rows,
    w_send, w_recv, m_send, m_recv, c_send, c_recv, t_send, t_recv,
    pc_send, pc_recv, pt_send, pt_recv, own_sem,
):
    dp, ex = lax.axis_index("dp"), lax.axis_index("expert")
    block, width = cot.shape
    own = heads.shape[1]
    pairs_n = own // 128
    slots_n = ne * cap_pad
    greet(n, ne, dp, ex)

    def weights(d):
        t = lax.rem(dp + d, n)
        return remote(packed.at[t], wgu.at[dp], w_send.at[d], w_recv.at[d], (t, ex))

    cots = Chain(n, dp, ex, cot, cot_all, c_send, c_recv)
    twos = Chain(n, dp, ex, two_own, two_all, t_send, t_recv)
    cots.start()
    keep_w = pltpu.make_async_copy(packed.at[dp], wgu.at[dp], own_sem.at[0])
    keep_w.start()

    def to_plane(rows, land, send, recv, group, k):
        peer = lax.rem(ex + k, ne)
        return remote(
            rows.at[group, pl.ds(pl.multiple_of(peer * cap_pad, 16), cap_pad)], land.at[group, ex],
            send.at[group, k], recv.at[group, k], (dp, peer),
        )

    def kept(rows, land, group, sem):
        return pltpu.make_async_copy(
            rows.at[group, pl.ds(pl.multiple_of(ex * cap_pad, 16), cap_pad)], land.at[group, ex], sem.at[group, 0]
        )

    def dispatch(group, tokens, rows, land, send, recv, weigh):
        meta = meta_all[group]
        ids = lax.broadcasted_iota(jnp.int32, (slots_n, block), 0).astype(F32)
        hit_a, hit_b = ids == meta[0:1, :], ids == meta[1:2, :]
        chosen = jnp.where(hit_a | hit_b, 1.0, 0.0).astype(BF16)
        found = mm(chosen, tokens)
        if weigh:
            gate = meta[2:3, :]
            factor = jnp.sum(
                jnp.where(hit_a, gate, 0.0) + jnp.where(hit_b, 1.0 - gate, 0.0), axis=1, keepdims=True
            )
            found = found * factor
        rows[group] = found.astype(BF16)
        for k in range(1, ne):
            to_plane(rows, land, send, recv, group, k).start()
        kept(rows, land, group, send).start()

    @pl.loop(0, n)
    def _(j):
        at = pl.ds(pl.multiple_of(j * block, block), block)
        xf = x_all[j].astype(F32)
        inverse = lax.rsqrt(jnp.mean(xf * xf, axis=-1, keepdims=True) + EPSILON)
        low = (xf * inverse * gain_one[...]).astype(BF16)
        normed[at, :] = low
        for w, ref in enumerate((wq, wk, wv)):
            qkv[at, w * own : (w + 1) * own] = mm(low, ref[...]).astype(BF16)

    def attend(pair):
        for side in range(2):
            bias_tile(vectors, 2 * pair + side, tiles.at[side])
        lane = lax.broadcasted_iota(jnp.int32, (block, 128), 1)
        low_half = lane < HEAD_DIM
        k_pair = qkv[:, own + pair * 128 : own + (pair + 1) * 128]
        v_pair = qkv[:, 2 * own + pair * 128 : 2 * own + (pair + 1) * 128]

        @pl.loop(0, n)
        def _(i):
            at = pl.ds(pl.multiple_of(i * block, block), block)
            q_pair = qkv[at, pair * 128 : (pair + 1) * 128]
            outs, logs = [], []
            for side in range(2):
                mask = low_half if side == 0 else jnp.logical_not(low_half)
                logits = logits_of(n, block, i, q_pair, k_pair, mask, tiles.at[side])
                row_max = jnp.max(logits, axis=-1, keepdims=True)
                exponent = jnp.exp(logits - row_max)
                total = jnp.sum(exponent, axis=-1, keepdims=True)
                probs_low = (exponent * (1.0 / total)).astype(BF16)
                outs.append(mm(probs_low, v_pair))
                logs.append(jnp.broadcast_to(row_max + jnp.log(total), (block, 128)))
            heads[at, pair * 128 : (pair + 1) * 128] = jnp.where(low_half, outs[0], outs[1]).astype(BF16)
            lse[at, pair * 128 : (pair + 1) * 128] = jnp.where(low_half, logs[0], logs[1])

    def hop(chain, h, then):
        for side in range(2):
            @pl.when(chain.held(h, side))
            def _():
                then(chain.arrive(h, side))

    attend(0)
    hop(cots, 0, lambda at: None)
    for d in range(1, n):
        weights(d).start()
    for pair in range(1, pairs_n):
        attend(pair)

    def give(d):
        t = lax.rem(dp + d, n)
        return remote(
            heads.at[pl.ds(pl.multiple_of(t * block, block), block)], mixed_in.at[dp], m_send.at[d], m_recv.at[d],
            (t, ex),
        )

    for d in range(1, n):
        give(d).start()
    mixed_in[dp] = heads[pl.ds(pl.multiple_of(dp * block, block), block), :]
    dispatch(dp, cot[...], cot_rows, d_outs, pc_send, pc_recv, True)
    for h in range(1, n - 1):
        hop(cots, h, lambda at: None)
    cots.finish()
    for d in range(1, n):
        give(d).wait()
    mixed[...] = jnp.concatenate([mixed_in[j] for j in range(n)], axis=1)
    total = x_all[dp].astype(F32) + mm(mixed[...], wo[...])
    resid[...] = total
    inverse = lax.rsqrt(jnp.mean(total * total, axis=-1, keepdims=True) + EPSILON)
    two_own[...] = (total * inverse * gain_two[...]).astype(BF16)
    twos.start()

    def send_two(group, tokens):
        dispatch(group, tokens, two_rows, slots, pt_send, pt_recv, False)

    send_two(dp, two_own[...])
    for j in range(1, n):
        at = lax.rem(dp + j, n)
        dispatch(at, cot_all[at], cot_rows, d_outs, pc_send, pc_recv, True)
        hop(twos, j - 1, lambda group: send_two(group, two_all[group]))
    twos.finish()
    keep_w.wait()
    for d in range(1, n):
        weights(d).wait()
    for rows, land, send, recv in (
        (two_rows, slots, pt_send, pt_recv), (cot_rows, d_outs, pc_send, pc_recv),
    ):
        @pl.loop(0, n)
        def _(group):
            kept(rows, land, group, send).wait()
            for k in range(1, ne):
                to_plane(rows, land, send, recv, group, k).wait()


def forward(n, ne, cap_pad, x_all, wq, wk, wv, wo, gain_one, gain_two, vectors, cot, meta_all, packed):
    tok, width = cot.shape
    own = wq.shape[1]
    wide = vectors.shape[1]
    both = packed.shape[2]
    slots_n = ne * cap_pad
    sem = pltpu.SemaphoreType.DMA
    return pl.pallas_call(
        functools.partial(forward_kernel, n, ne, cap_pad),
        in_specs=[VM] * 10 + [ANY],
        out_specs=[VM] * 5 + [ANY] * 3,
        out_shape=[
            jax.ShapeDtypeStruct((n * tok, width), BF16),
            jax.ShapeDtypeStruct((n * tok, 3 * own), BF16),
            jax.ShapeDtypeStruct((n * tok, own), F32),
            jax.ShapeDtypeStruct((tok, width), BF16),
            jax.ShapeDtypeStruct((tok, width), F32),
            jax.ShapeDtypeStruct((n, ne, cap_pad, width), BF16),
            jax.ShapeDtypeStruct((n, ne, cap_pad, width), BF16),
            jax.ShapeDtypeStruct((n, tok, both), BF16),
        ],
        scratch_shapes=[
            pltpu.VMEM((n * tok, own), BF16),
            pltpu.VMEM((n, tok, own), BF16),
            pltpu.VMEM((2, tok, wide), F32),
            pltpu.VMEM((n, tok, width), BF16),
            pltpu.VMEM((n, tok, width), BF16),
            pltpu.VMEM((tok, width), BF16),
            pltpu.VMEM((n, slots_n, width), BF16),
            pltpu.VMEM((n, slots_n, width), BF16),
            sem((n,)), sem((n,)), sem((n,)), sem((n,)),
            sem((n, 2)), sem((n, 2)), sem((n, 2)), sem((n, 2)),
            sem((n, ne)), sem((n, ne)), sem((n, ne)), sem((n, ne)),
            sem((1,)),
        ],
        compiler_params=pltpu.CompilerParams(
            collective_id=2, has_side_effects=True, vmem_limit_bytes=VMEM_LIMIT
        ),
        name="forward",
    )(x_all, wq, wk, wv, wo, gain_one, gain_two, vectors, cot, meta_all, packed)


def shift(value, distance, n):
    return lax.ppermute(value, "dp", [(i, (i + distance) % n) for i in range(n)])


def pick(stacked, index):
    return lax.dynamic_index_in_dim(stacked, index, 0, keepdims=False)


def exchange(value):
    return lax.all_to_all(value, "expert", split_axis=0, concat_axis=0, tiled=True)


def trade(blocks, n, dp):
    got = jnp.stack([pick(blocks, dp)] + [shift(pick(blocks, lax.rem(dp + d, n)), d, n) for d in range(1, n)])
    return jnp.stack([pick(got, lax.rem(dp - j + n, n)) for j in range(n)])


def to_owners(blocks, n, dp):
    total = pick(blocks, dp).astype(F32)
    for d in range(1, n):
        total = total + shift(pick(blocks, lax.rem(dp + d, n)).astype(BF16), d, n).astype(F32)
    return total


def local(
    inputs, cotangent, gain_attn, w_query, w_key, w_value, w_out, position_bias,
    gain_moe, w_gate, w_up, w_down, routes, gate_fixed,
):
    n = lax.axis_size("dp")
    experts_n = lax.axis_size("expert")
    dp = lax.axis_index("dp")
    ex = lax.axis_index("expert")
    tok, width = inputs.shape[1:]
    length = n * tok
    own = HEADS * HEAD_DIM // n
    heads_own = HEADS // n
    wrows = w_query.shape[0]
    capacity = 5 * tok // (2 * experts_n)
    cap_pad = -(-capacity // 16) * 16
    slots_n = experts_n * cap_pad

    n_gain, n_bias = gain_attn.shape[0], position_bias.shape[0]
    extra = jnp.concatenate([gain_attn, gain_moe, position_bias])
    extra = jnp.zeros((16, own), BF16).at[0, : 2 * n_gain + n_bias].set(extra)
    meta_in = jnp.concatenate([routes[0].T, gate_fixed], axis=0)
    x_all, wq, wk, wv, extras, wo, meta_all, packed = start(
        n, experts_n, capacity, cap_pad,
        inputs[0], w_query, w_key, w_value, extra, w_out, meta_in, w_gate[0], w_up[0],
    )
    wq, wk, wv = (w.reshape(width, own) for w in (wq, wk, wv))
    wo = wo.reshape(width, width)
    extras = extras[:, :, 0]
    gain_one = extras[:, :, :n_gain].reshape(1, -1).astype(F32)
    gain_two = extras[:, :, n_gain : 2 * n_gain].reshape(1, -1).astype(F32)
    table = extras[:, :, 2 * n_gain : 2 * n_gain + n_bias].reshape(BUCKETS, HEADS)
    table = lax.dynamic_slice_in_dim(table, dp * heads_own, heads_own, 1)
    wide = 2 * length
    offsets = jnp.arange(wide, dtype=jnp.int32) - length
    in_bucket = (bucket_of(offsets)[:, None] == jnp.arange(BUCKETS, dtype=jnp.int32)).astype(BF16)
    in_bucket = jnp.where(jnp.abs(offsets)[:, None] < length, in_bucket, jnp.zeros_like(in_bucket))
    vectors = mm(table, in_bucket, (((0,), (1,)), ((), ())))

    normed, qkv, lse, mixed, resid, slots, d_outs, wgu = forward(
        n, experts_n, cap_pad, x_all, wq, wk, wv, wo, gain_one, gain_two, vectors, cotangent[0], meta_all, packed
    )
    wgu = wgu.reshape(width, -1)
    deep = w_down.shape[1]
    padded = -(-deep // 128) * 128
    wd = jnp.pad(w_down[0], ((0, padded - deep), (0, 0)))
    steps = 2 * n
    out_rows, dslot_rows, gwgu, gwd = experts(slots, d_outs, wgu, wd, steps)
    grad_w_down = gwd[:deep]

    dest = meta_all[:, :2].astype(jnp.int32)
    select = (dest[..., None] == jnp.arange(slots_n, dtype=jnp.int32)).astype(BF16)
    both = select[:, 0] + select[:, 1]
    first_gate = meta_all[:, 2]
    gates = jnp.stack([first_gate, 1.0 - first_gate], axis=1)

    def from_experts(rows):
        rows = jnp.swapaxes(rows.reshape(n, experts_n, cap_pad, width), 0, 1)
        return jnp.swapaxes(exchange(rows), 0, 1).reshape(n, slots_n, width)

    got = trade(gwgu.reshape(n, width // n, gwgu.shape[1]), n, dp)
    dslot_back = from_experts(dslot_rows)
    dslot_back, got, out_rows = lax.optimization_barrier((dslot_back, got, out_rows))
    partial = jnp.einsum("gts,gsd->gtd", both, dslot_back, preferred_element_type=F32)
    grad_normed_two = to_owners(partial, n, dp)
    gain_one, gain_two = gain_one[0], gain_two[0]
    grad_top = cotangent[0].astype(F32)
    inverse_two = lax.rsqrt(jnp.mean(resid * resid, axis=-1, keepdims=True) + EPSILON)
    grad_gain_two, grad_resid_norm = norm_backward(resid, inverse_two, gain_two, grad_normed_two)
    grad_resid = grad_top + grad_resid_norm
    grad_attn_low = grad_resid.astype(BF16)
    d_mixed = mm(grad_attn_low, wo, NT).astype(BF16)
    d_mixed_heads = trade(jnp.swapaxes(d_mixed.reshape(tok, n, own), 0, 1), n, dp).reshape(length, own)
    grad_w_out_part = mm(mixed, grad_attn_low, TN)

    out_back = from_experts(out_rows)
    out_back, d_mixed_heads = lax.optimization_barrier((out_back, d_mixed_heads))
    picked = jnp.einsum("gcts,gsd->gctd", select, out_back, preferred_element_type=F32)
    moe_sum = to_owners(jnp.sum(picked * gates[..., None], axis=1), n, dp)

    dq, dk, dv, diagonals = attention_backward(n, qkv, lse, d_mixed_heads, vectors)
    d_normed_part = mm(dq, wq, NT) + mm(dk, wk, NT) + mm(dv, wv, NT)
    d_normed_part, moe_sum = lax.optimization_barrier((d_normed_part, moe_sum))
    grad_normed = to_owners(d_normed_part.reshape(n, tok, width), n, dp)
    d_qkv = jnp.concatenate([dq, dk, dv], axis=1)
    grad_wqkv_part = mm(normed, d_qkv, TN)
    tokens = inputs[0].astype(F32)
    inverse_one = lax.rsqrt(jnp.mean(tokens * tokens, axis=-1, keepdims=True) + EPSILON)
    grad_gain_one, grad_tok_norm = norm_backward(tokens, inverse_one, gain_one, grad_normed)
    grad_inputs = (grad_resid + grad_tok_norm).astype(BF16)
    block_out = (resid + moe_sum).astype(BF16)

    grad_w_gate, grad_w_up = unpack_columns(got)

    def plane_sum(parts):
        return jnp.sum(exchange(parts.astype(BF16)).astype(F32), axis=0)

    go = grad_w_out_part.reshape(n, experts_n, wrows, width)
    go = plane_sum(jnp.swapaxes(go, 0, 1))
    grad_w_out = to_owners(go, n, dp)

    gq = grad_wqkv_part.reshape(n, experts_n, wrows, 3 * own)
    gq = plane_sum(jnp.swapaxes(gq, 0, 1)).astype(BF16)
    gq_all = trade(gq, n, dp).astype(F32)
    gq_all = gq_all.reshape(n, wrows, 3, own).transpose(2, 1, 0, 3).reshape(3, wrows, width)

    diag_rows = jnp.roll(diagonals.reshape(heads_own, wide), tok, axis=1)
    grad_table = lax.dot_general(
        in_bucket.astype(F32), diag_rows, (((0,), (1,)), ((), ())), precision=lax.Precision.HIGHEST,
        preferred_element_type=F32,
    )
    grad_table = lax.dynamic_update_slice_in_dim(
        jnp.zeros((BUCKETS, HEADS), F32), grad_table, dp * heads_own, 1
    )
    small = jnp.concatenate([grad_gain_one, grad_gain_two, grad_table.reshape(-1)]).reshape(-1, 128)
    step = 1
    while step < experts_n:
        small = small + lax.ppermute(small, "expert", [(i, i ^ step) for i in range(experts_n)])
        step *= 2
    small = (small + sum(shift(small, d, n) for d in range(1, n))).reshape(-1)
    me = dp * experts_n + ex
    grad_gain_attn = lax.dynamic_slice_in_dim(small, me * n_gain, n_gain)
    grad_gain_moe = lax.dynamic_slice_in_dim(small, width + me * n_gain, n_gain)
    grad_bias = lax.dynamic_slice_in_dim(small, 2 * width + me * n_bias, n_bias)

    return (
        block_out[None],
        grad_inputs[None],
        grad_gain_attn,
        gq_all[0],
        gq_all[1],
        gq_all[2],
        grad_w_out,
        grad_bias,
        grad_gain_moe,
        grad_w_gate[None],
        grad_w_up[None],
        grad_w_down[None],
    )


def solution(mesh):
    vector = P(("dp", "expert"))
    matrix = P(("dp", "expert"), None)
    split = P("expert", "dp", None)
    return jax.shard_map(
        local,
        mesh=mesh,
        in_specs=(
            split, split, vector, matrix, matrix, matrix, matrix, vector, vector,
            split, split, split, split, P("expert", "dp"),
        ),
        out_specs=(
            split, split, vector, matrix, matrix, matrix, matrix, vector, vector,
            split, split, split,
        ),
        check_vma=False,
    )
```

time: 861 us -> 737 us (0.86)
  Pallas kernels: 101 us -> 344 us
  waiting for transfers between devices: 334 us -> 180 us
  starting transfers between devices: 223 us -> 114 us
  local copies, waits for them, and re-layouts: 84.1 us -> 45.6 us
  blocking collectives: 36 us -> 0 us
  matrix products: 33.1 us -> 17.7 us
  other arithmetic: 37.6 us -> 25 us
    pallas_call x2, Pallas kernels: 19 us -> 262 us  [the longest x1 204 us: forward(): pl.pallas_call(functools.partial(forward_kernel, n, ne, cap_pad), in_spec...]
    ppermute x48 -> x24, waiting for transfers between devices: 237 us -> 115 us  [shift(): lax.ppermute(value, 'dp', [(i, (i + distance) % n) for i in range(n)])]
    ppermute x48 -> x24, starting transfers between devices: 164 us -> 90.6 us  [shift(): lax.ppermute(value, 'dp', [(i, (i + distance) % n) for i in range(n)])]
    all_to_all x1 -> x0, blocking collectives: 36 us -> none  [exchange(): lax.all_to_all(value, 'expert', split_axis=0, concat_axis=0, tiled=True)]
    ppermute x14 -> x0, waiting for transfers between devices: 25.5 us -> none  [the longest x7 19.4 us: local(): lax.ppermute(plane, 'expert', [(i, i ^ k) for i in range(experts_n)])]
    all_to_all x9 -> x4, starting transfers between devices: 38.5 us -> 20.1 us  [exchange(): lax.all_to_all(value, 'expert', split_axis=0, concat_axis=0, tiled=True)]
    ppermute x14 -> x0, starting transfers between devices: 17.1 us -> none  [the longest x7 10.6 us: local(): lax.ppermute(plane, 'expert', [(i, i ^ k) for i in range(experts_n)])]
    unnamed x97 -> x52, local copies, waits for them, and re-layouts: 21.5 us -> 5.31 us
  transfers between devices with their start and end apart: 74 -> 31, of which waited for: 31 -> 19; matrix products, arithmetic and copies ran while one was open for 16% -> 7% of each run, Pallas kernels for 3% -> 4%
where the time goes in v2:
time: 737 us; the launch traced here: 728 us
  Pallas kernels  344 us (47%)
  waiting for transfers between devices  180 us (24%)
  starting transfers between devices  114 us (15%)
  local copies, waits for them, and re-layouts  45.6 us (6%)
  other arithmetic  25 us (3%)
  matrix products  17.7 us (2%)
    pallas_call x1, Pallas kernels, forward(): pl.pallas_call(functools.partial(forward_kernel, n, ne, cap_pad), in_spec...  204 us
    ppermute x24, waiting for transfers between devices, shift(): lax.ppermute(value, 'dp', [(i, (i + distance) % n) for i in range(n)])  115 us
    ppermute x24, starting transfers between devices, shift(): lax.ppermute(value, 'dp', [(i, (i + distance) % n) for i in range(n)])  90.6 us
    pallas_call x1, Pallas kernels, start(): pl.pallas_call(functools.partial(start_kernel, n, ne, cap, cap_pad, piece...  58.6 us
    pallas_call x1, Pallas kernels, experts(): pl.pallas_call(functools.partial(expert_kernel, main), grid=(steps,), in_...  53.4 us
    all_to_all x4, waiting for transfers between devices, exchange(): lax.all_to_all(value, 'expert', split_axis=0, concat_axis=0, tiled=True)  45.7 us
    pallas_call x1, Pallas kernels, attention_backward(): pl.pallas_call(functools.partial(attention_backward_kernel, n, block), gr...  23.4 us
    all_to_all x4, starting transfers between devices, exchange(): lax.all_to_all(value, 'expert', split_axis=0, concat_axis=0, tiled=True)  20.1 us
  transfers between devices with their start and end apart: 31, of which 19 were waited for; matrix products, arithmetic and copies ran while one was open for 7% of the time, Pallas kernels for 4%

profile of v2, /device:TPU:0, one launch (start us, length us, event | category | flops | bytes accessed | tf_op | source)
XLA Modules:
  0.0 727.7 jit_solution(1408997597461041604)
XLA Ops:
  3.5 58.6 %start.1 = (bf16[4,256,1024]{2,1,0:T(8,128)(2,1)}, bf16[4,8,32,256]{3,2,1,0:T(8,128)(2,1)}, bf16[4,8,32,256]{3,2,1,0:T(8,128)(2,1)}, bf16[4,8,32,256]{3,2,1,0:T(...) custom-call(bf16[256,1024]{1,0:T(8,128)(2,1)} %bitcast.191, ...), custom_call_target="tpu_custom_call" | custom-call | tf_op jit(solution)/shard_map/start/pallas_call | solution.py:510
  67.4 203.7 %forward.1 = (bf16[1024,1024]{1,0:T(8,128)(2,1)}, bf16[1024,768]{1,0:T(8,128)(2,1)}, f32[1024,256]{1,0:T(8,128)}, bf16[256,1024]{1,0:T(8,128)(2,1)}, f32[256,102...) custom-call(bf16[4,256,1024]{2,1,0:T(8,128)(2,1)} %get-tuple-element, ...), custom_call_target="tpu_custom_call" | custom-call | tf_op jit(solution)/shard_map/forward/pallas_call | solution.py:702
  271.1 53.4 %experts.1 = (bf16[8,320,1024]{2,1,0:T(8,128)(2,1)}, bf16[8,320,1024]{2,1,0:T(8,128)(2,1)}, bf16[1024,1408]{1,0:T(8,128)(2,1)}, f32[768,1024]{1,0:T(8,128)}) custom-call(bf16[8,320,1024]{2,1,0:T(8,128)(2,1)} %bitcast.228, bf16[8,320,1024]{2,1,0:T(8,128)(2,1)} %bitcast.229, bf16[1024,1408]{1,0:T(8,128)(2,1)} %bitcast.232, bf16[768,1024]{1,0:T(8,128)(2,1)} %pad.9.wd_ref), custom_call_target="tpu_custom_call" | custom-call | flops 34225520640 | bytes 32505856 | tf_op jit(solution)/shard_map/experts/pallas_call | solution.py:228
  324.5 5.8 copy.85
  330.4 5.2 all-to-all-start
  345.1 12.0 %collective-permute-done = bf16[256,1408]{1,0:T(8,128)(2,1)} collective-permute-done((bf16[256,1408]{1,0:T(8,128)(2,1)}, bf16[256,1408]{1,0:T(8,128)(2,1)}, u32[]{:S(2)}, u32[]{:S(2)}) %collective-permute-start) | collective-permute-done | bytes 720928 | tf_op jit(solution)/shard_map/ppermute | solution.py:738
  357.1 32.1 %collective-permute-done.1 = bf16[256,1408]{1,0:T(8,128)(2,1)} collective-permute-done((bf16[256,1408]{1,0:T(8,128)(2,1)}, bf16[256,1408]{1,0:T(8,128)(2,1)}, u32[]{:S(2)}, u32[]{:S(2)}) %collective-permute-start.1) | collective-permute-done | bytes 720928 | tf_op jit(solution)/shard_map/ppermute | solution.py:738
  404.6 13.1 %collective-permute-start.3 = (bf16[256,1024]{1,0:T(8,128)(2,1)}, bf16[256,1024]{1,0:T(8,128)(2,1)S(1)}, u32[]{:S(2)}, u32[]{:S(2)}) collective-permute-start(bf16[256,1024]{1,0:T(8,128)(2,1)} %get-tuple-element.102), channel_id=1, source_target_pairs={{0,8},{8,16},{16,24},{24,0},{1,9},{9,17},{17,25},{25,1},{2,10},{10... | collective-permute-start | bytes 1572872 | tf_op jit(solution)/shard_map/ppermute | solution.py:738
  420.4 9.9 %collective-permute-done.3 = bf16[256,1024]{1,0:T(8,128)(2,1)S(1)} collective-permute-done((bf16[256,1024]{1,0:T(8,128)(2,1)}, bf16[256,1024]{1,0:T(8,128)(2,1)S(1)}, u32[]{:S(2)}, u32[]{:S(2)}) %collective-permute-start.3) | collective-permute-done | bytes 524320 | tf_op jit(solution)/shard_map/ppermute | solution.py:738
  430.3 22.7 %collective-permute-done.4 = bf16[256,1024]{1,0:T(8,128)(2,1)S(1)} collective-permute-done((bf16[256,1024]{1,0:T(8,128)(2,1)}, bf16[256,1024]{1,0:T(8,128)(2,1)S(1)}, u32[]{:S(2)}, u32[]{:S(2)}) %collective-permute-start.4) | collective-permute-done | bytes 524320 | tf_op jit(solution)/shard_map/ppermute | solution.py:738
  458.0 5.2 all-to-all-start.3
  463.1 5.8 copy.84
  468.9 20.9 %all-to-all-done.3 = bf16[8,4,32,1024]{3,2,1,0:T(8,128)(2,1)} async-done(((bf16[8,4,32,1024]{3,2,1,0:T(8,128)(2,1)}), bf16[8,4,32,1024]{3,2,1,0:T(8,128)(2,1)}, u32[]{:S(2)}, u32[]{:S(2)}) %all-to-all-start.3) | async-done | bytes 2097184 | tf_op jit(solution)/shard_map/all_to_all | solution.py:746
  502.7 11.8 %collective-permute-start.6 = (bf16[256,256]{1,0:T(8,128)(2,1)S(1)}, bf16[256,256]{1,0:T(8,128)(2,1)S(1)}, u32[]{:S(2)}, u32[]{:S(2)}) collective-permute-start(bf16[256,256]{1,0:T(8,128)(2,1)S(1)} %bitcast.213), channel_id=1, source_target_pairs={{0,8},{8,16},{16,24},{24,0},{1,9},{9,17},{17,25},{25,1},{2,10},{10... | collective-permute-start | bytes 393224 | tf_op jit(solution)/shard_map/ppermute | solution.py:738
  519.5 5.3 collective-permute-done.7
  533.5 21.4 %all-to-all-done.1 = bf16[8,4,80,1024]{3,2,1,0:T(8,128)(2,1)} async-done(((bf16[8,4,80,1024]{3,2,1,0:T(8,128)(2,1)}), bf16[8,4,80,1024]{3,2,1,0:T(8,128)(2,1)}, u32[]{:S(2)}, u32[]{:S(2)}) %all-to-all-start.1) | async-done | bytes 5242912 | tf_op jit(solution)/shard_map/all_to_all | solution.py:746
  563.5 10.7 %collective-permute-start.10 = (bf16[256,1024]{1,0:T(8,128)(2,1)}, bf16[256,1024]{1,0:T(8,128)(2,1)}, u32[]{:S(2)}, u32[]{:S(2)}) collective-permute-start(bf16[256,1024]{1,0:T(8,128)(2,1)} %get-tuple-element.101), channel_id=1, source_target_pairs={{0,16},{8,24},{16,0},{24,8},{1,17},{9,25},{17,1},{25,9},{2,18},{10... | collective-permute-start | bytes 1572872 | tf_op jit(solution)/shard_map/ppermute | solution.py:738
  577.7 23.4 %attention_backward.1 = (bf16[1024,256]{1,0:T(8,128)(2,1)}, bf16[1024,256]{1,0:T(8,128)(2,1)}, bf16[1024,256]{1,0:T(8,128)(2,1)}, f32[2,2,2048]{2,1,0:T(2,128)}) custom-call(bf16[1024,768]{1,0:T(8,128)(2,1)} %get-tuple-element.66.q_ref.k_ref.v_ref, bf16[1024,768]{1,0:T(8,128)(2,1)} %get-tuple-element.66.q_ref.k_ref.v_ref, ...), custom_call_target="tpu_custom_call" | custom-call | flops 10737418240 | bytes 3670016 | tf_op jit(solution)/shard_map/attention_backward/pallas_call | solution.py:134
  613.5 9.7 %collective-permute-start.12 = (bf16[256,1024]{1,0:T(8,128)(2,1)}, bf16[256,1024]{1,0:T(8,128)(2,1)}, u32[]{:S(2)}, u32[]{:S(2)}) collective-permute-start(bf16[256,1024]{1,0:T(8,128)(2,1)} %get-tuple-element.96), channel_id=1, source_target_pairs={{0,8},{8,16},{16,24},{24,0},{1,9},{9,17},{17,25},{25,1},{2,10},{10... | collective-permute-start | bytes 1572872 | tf_op jit(solution)/shard_map/ppermute | solution.py:738
  628.2 4.9 unpack_columns.1
  635.8 16.9 %collective-permute-done.13 = bf16[256,1024]{1,0:T(8,128)(2,1)} collective-permute-done((bf16[256,1024]{1,0:T(8,128)(2,1)}, bf16[256,1024]{1,0:T(8,128)(2,1)}, u32[]{:S(2)}, u32[]{:S(2)}) %collective-permute-start.13) | collective-permute-done | bytes 524320 | tf_op jit(solution)/shard_map/ppermute | solution.py:738
  665.1 5.1 all-to-all-start.2
  675.3 16.4 %collective-permute-done.16 = f32[20,128]{1,0:T(8,128)S(1)} collective-permute-done((f32[20,128]{1,0:T(8,128)S(1)}, f32[20,128]{1,0:T(8,128)S(1)}, u32[]{:S(2)}, u32[]{:S(2)}) %collective-permute-start.16) | collective-permute-done | bytes 10272 | tf_op jit(solution)/shard_map/ppermute | solution.py:877
  695.4 13.7 %collective-permute-start.18 = (f32[20,128]{1,0:T(8,128)S(1)}, f32[20,128]{1,0:T(8,128)S(1)}, u32[]{:S(2)}, u32[]{:S(2)}) collective-permute-start(f32[20,128]{1,0:T(8,128)S(1)} %add.336), channel_id=1, source_target_pairs={{0,8},{8,16},{16,24},{24,0},{1,9},{9,17},{17,25},{25,1},{2,10},{10... | collective-permute-start | bytes 30728 | tf_op jit(solution)/shard_map/ppermute | solution.py:738
  (181 shorter events, 138.6 us)
Async XLA Ops:
  330.4 66.0 %all-to-all-start = ((bf16[8,4,80,1024]{3,2,1,0:T(8,128)(2,1)}), bf16[8,4,80,1024]{3,2,1,0:T(8,128)(2,1)}, u32[]{:S(2)}, u32[]{:S(2)}) async-start(bf16[8,4,80,1024]{3,2,1,0:T(8,128)(2,1)} %bitcast.182), calls=%async_computation | async-start | bytes 10485760 | tf_op jit(solution)/shard_map/all_to_all | solution.py:746
  337.2 19.9 %collective-permute-start = (bf16[256,1408]{1,0:T(8,128)(2,1)}, bf16[256,1408]{1,0:T(8,128)(2,1)}, u32[]{:S(2)}, u32[]{:S(2)}) collective-permute-start(bf16[256,1408]{1,0:T(8,128)(2,1)} %get-tuple-element.112), channel_id=1, source_target_pairs={{0,8},{8,16},{16,24},{24,0},{1,9},{9,17},{17,25},{25,1},{2,10},{10... | collective-permute-start | bytes 2162696 | tf_op jit(solution)/shard_map/ppermute | solution.py:738
  340.6 48.6 %collective-permute-start.1 = (bf16[256,1408]{1,0:T(8,128)(2,1)}, bf16[256,1408]{1,0:T(8,128)(2,1)}, u32[]{:S(2)}, u32[]{:S(2)}) collective-permute-start(bf16[256,1408]{1,0:T(8,128)(2,1)} %get-tuple-element.111), channel_id=1, source_target_pairs={{0,16},{8,24},{16,0},{24,8},{1,17},{9,25},{17,1},{25,9},{2,18},{10... | collective-permute-start | bytes 2162696 | tf_op jit(solution)/shard_map/ppermute | solution.py:738
  340.8 48.4 %collective-permute-start.2 = (bf16[256,1408]{1,0:T(8,128)(2,1)}, bf16[256,1408]{1,0:T(8,128)(2,1)}, u32[]{:S(2)}, u32[]{:S(2)}) collective-permute-start(bf16[256,1408]{1,0:T(8,128)(2,1)} %get-tuple-element.110), channel_id=1, source_target_pairs={{0,24},{8,0},{16,8},{24,16},{1,25},{9,1},{17,9},{25,17},{2,26},{10... | collective-permute-start | bytes 2162696 | tf_op jit(solution)/shard_map/ppermute | solution.py:738
  404.6 25.7 %collective-permute-start.3 = (bf16[256,1024]{1,0:T(8,128)(2,1)}, bf16[256,1024]{1,0:T(8,128)(2,1)S(1)}, u32[]{:S(2)}, u32[]{:S(2)}) collective-permute-start(bf16[256,1024]{1,0:T(8,128)(2,1)} %get-tuple-element.102), channel_id=1, source_target_pairs={{0,8},{8,16},{16,24},{24,0},{1,9},{9,17},{17,25},{25,1},{2,10},{10... | collective-permute-start | bytes 1572872 | tf_op jit(solution)/shard_map/ppermute | solution.py:738
  417.7 35.3 %collective-permute-start.4 = (bf16[256,1024]{1,0:T(8,128)(2,1)}, bf16[256,1024]{1,0:T(8,128)(2,1)S(1)}, u32[]{:S(2)}, u32[]{:S(2)}) collective-permute-start(bf16[256,1024]{1,0:T(8,128)(2,1)} %get-tuple-element.104), channel_id=1, source_target_pairs={{0,16},{8,24},{16,0},{24,8},{1,17},{9,25},{17,1},{25,9},{2,18},{10... | collective-permute-start | bytes 1572872 | tf_op jit(solution)/shard_map/ppermute | solution.py:738
  417.9 35.0 %collective-permute-start.5 = (bf16[256,1024]{1,0:T(8,128)(2,1)S(1)}, bf16[256,1024]{1,0:T(8,128)(2,1)S(1)}, u32[]{:S(2)}, u32[]{:S(2)}) collective-permute-start(bf16[256,1024]{1,0:T(8,128)(2,1)S(1)} %get-tuple-element.103), channel_id=1, source_target_pairs={{0,24},{8,0},{16,8},{24,16},{1,25},{9,1},{17,9},{25,17},{2,26},{10... | collective-permute-start | bytes 1572872 | tf_op jit(solution)/shard_map/ppermute | solution.py:738
  458.0 31.9 %all-to-all-start.3 = ((bf16[8,4,32,1024]{3,2,1,0:T(8,128)(2,1)}), bf16[8,4,32,1024]{3,2,1,0:T(8,128)(2,1)}, u32[]{:S(2)}, u32[]{:S(2)}) async-start(bf16[8,4,32,1024]{3,2,1,0:T(8,128)(2,1)} %bitcast.190), calls=%async_computation.3 | async-start | bytes 4194304 | tf_op jit(solution)/shard_map/all_to_all | solution.py:746
  489.9 65.0 %all-to-all-start.1 = ((bf16[8,4,80,1024]{3,2,1,0:T(8,128)(2,1)}), bf16[8,4,80,1024]{3,2,1,0:T(8,128)(2,1)}, u32[]{:S(2)}, u32[]{:S(2)}) async-start(bf16[8,4,80,1024]{3,2,1,0:T(8,128)(2,1)} %bitcast.183), calls=%async_computation.1 | async-start | bytes 10485760 | tf_op jit(solution)/shard_map/all_to_all | solution.py:746
  502.7 16.8 %collective-permute-start.6 = (bf16[256,256]{1,0:T(8,128)(2,1)S(1)}, bf16[256,256]{1,0:T(8,128)(2,1)S(1)}, u32[]{:S(2)}, u32[]{:S(2)}) collective-permute-start(bf16[256,256]{1,0:T(8,128)(2,1)S(1)} %bitcast.213), channel_id=1, source_target_pairs={{0,8},{8,16},{16,24},{24,0},{1,9},{9,17},{17,25},{25,1},{2,10},{10... | collective-permute-start | bytes 393224 | tf_op jit(solution)/shard_map/ppermute | solution.py:738
  514.5 10.3 %collective-permute-start.7 = (bf16[256,256]{1,0:T(8,128)(2,1)S(1)}, bf16[256,256]{1,0:T(8,128)(2,1)S(1)}, u32[]{:S(2)}, u32[]{:S(2)}) collective-permute-start(bf16[256,256]{1,0:T(8,128)(2,1)S(1)} %bitcast.214), channel_id=1, source_target_pairs={{0,16},{8,24},{16,0},{24,8},{1,17},{9,25},{17,1},{25,9},{2,18},{10... | collective-permute-start | bytes 393224 | tf_op jit(solution)/shard_map/ppermute | solution.py:738
  528.5 96.7 %collective-permute-start.24 = (bf16[32,1024]{1,0:T(8,128)(2,1)}, bf16[32,1024]{1,0:T(8,128)(2,1)S(1)}, u32[]{:S(2)}, u32[]{:S(2)}) collective-permute-start(bf16[32,1024]{1,0:T(8,128)(2,1)} %get-tuple-element.113), channel_id=1, source_target_pairs={{0,8},{8,16},{16,24},{24,0},{1,9},{9,17},{17,25},{25,1},{2,10},{10... | collective-permute-start | bytes 196616 | tf_op jit(solution)/shard_map/ppermute | solution.py:738
  531.7 101.3 %collective-permute-start.25 = (bf16[32,1024]{1,0:T(8,128)(2,1)S(1)}, bf16[32,1024]{1,0:T(8,128)(2,1)S(1)}, u32[]{:S(2)}, u32[]{:S(2)}) collective-permute-start(bf16[32,1024]{1,0:T(8,128)(2,1)S(1)} %get-tuple-element.115), channel_id=1, source_target_pairs={{0,16},{8,24},{16,0},{24,8},{1,17},{9,25},{17,1},{25,9},{2,18},{10... | collective-permute-start | bytes 196616 | tf_op jit(solution)/shard_map/ppermute | solution.py:738
  563.5 45.8 %collective-permute-start.10 = (bf16[256,1024]{1,0:T(8,128)(2,1)}, bf16[256,1024]{1,0:T(8,128)(2,1)}, u32[]{:S(2)}, u32[]{:S(2)}) collective-permute-start(bf16[256,1024]{1,0:T(8,128)(2,1)} %get-tuple-element.101), channel_id=1, source_target_pairs={{0,16},{8,24},{16,0},{24,8},{1,17},{9,25},{17,1},{25,9},{2,18},{10... | collective-permute-start | bytes 1572872 | tf_op jit(solution)/shard_map/ppermute | solution.py:738
  574.2 35.4 %collective-permute-start.11 = (bf16[256,1024]{1,0:T(8,128)(2,1)}, bf16[256,1024]{1,0:T(8,128)(2,1)}, u32[]{:S(2)}, u32[]{:S(2)}) collective-permute-start(bf16[256,1024]{1,0:T(8,128)(2,1)} %get-tuple-element.100), channel_id=1, source_target_pairs={{0,24},{8,0},{16,8},{24,16},{1,25},{9,1},{17,9},{25,17},{2,26},{10... | collective-permute-start | bytes 1572872 | tf_op jit(solution)/shard_map/ppermute | solution.py:738
  577.6 32.0 %collective-permute-start.9 = (bf16[256,1024]{1,0:T(8,128)(2,1)}, bf16[256,1024]{1,0:T(8,128)(2,1)}, u32[]{:S(2)}, u32[]{:S(2)}) collective-permute-start(bf16[256,1024]{1,0:T(8,128)(2,1)} %get-tuple-element.99), channel_id=1, source_target_pairs={{0,8},{8,16},{16,24},{24,0},{1,9},{9,17},{17,25},{25,1},{2,10},{10... | collective-permute-start | bytes 1572872 | tf_op jit(solution)/shard_map/ppermute | solution.py:738
  609.3 23.8 %collective-permute-start.26 = (bf16[32,1024]{1,0:T(8,128)(2,1)S(1)}, bf16[32,1024]{1,0:T(8,128)(2,1)S(1)}, u32[]{:S(2)}, u32[]{:S(2)}) collective-permute-start(bf16[32,1024]{1,0:T(8,128)(2,1)S(1)} %get-tuple-element.114), channel_id=1, source_target_pairs={{0,24},{8,0},{16,8},{24,16},{1,25},{9,1},{17,9},{25,17},{2,26},{10... | collective-permute-start | bytes 196616 | tf_op jit(solution)/shard_map/ppermute | solution.py:738
  613.5 22.3 %collective-permute-start.12 = (bf16[256,1024]{1,0:T(8,128)(2,1)}, bf16[256,1024]{1,0:T(8,128)(2,1)}, u32[]{:S(2)}, u32[]{:S(2)}) collective-permute-start(bf16[256,1024]{1,0:T(8,128)(2,1)} %get-tuple-element.96), channel_id=1, source_target_pairs={{0,8},{8,16},{16,24},{24,0},{1,9},{9,17},{17,25},{25,1},{2,10},{10... | collective-permute-start | bytes 1572872 | tf_op jit(solution)/shard_map/ppermute | solution.py:738
  623.2 29.6 %collective-permute-start.13 = (bf16[256,1024]{1,0:T(8,128)(2,1)}, bf16[256,1024]{1,0:T(8,128)(2,1)}, u32[]{:S(2)}, u32[]{:S(2)}) collective-permute-start(bf16[256,1024]{1,0:T(8,128)(2,1)} %get-tuple-element.98), channel_id=1, source_target_pairs={{0,16},{8,24},{16,0},{24,8},{1,17},{9,25},{17,1},{25,9},{2,18},{10... | collective-permute-start | bytes 1572872 | tf_op jit(solution)/shard_map/ppermute | solution.py:738
  625.2 32.3 %collective-permute-start.14 = (bf16[256,1024]{1,0:T(8,128)(2,1)}, bf16[256,1024]{1,0:T(8,128)(2,1)}, u32[]{:S(2)}, u32[]{:S(2)}) collective-permute-start(bf16[256,1024]{1,0:T(8,128)(2,1)} %get-tuple-element.97), channel_id=1, source_target_pairs={{0,24},{8,0},{16,8},{24,16},{1,25},{9,1},{17,9},{25,17},{2,26},{10... | collective-permute-start | bytes 1572872 | tf_op jit(solution)/shard_map/ppermute | solution.py:738
  660.6 9.6 %collective-permute-start.15 = (f32[20,128]{1,0:T(8,128)S(1)}, f32[20,128]{1,0:T(8,128)S(1)}, u32[]{:S(2)}, u32[]{:S(2)}) collective-permute-start(f32[20,128]{1,0:T(8,128)S(1)} %maximum_bitcast_fusion), channel_id=1, source_target_pairs={{0,1},{1,0},{2,3},{3,2},{4,5},{5,4},{6,7},{7,6},{8,9},{9,8},{10,11... | collective-permute-start | bytes 30728 | tf_op jit(solution)/shard_map/ppermute | solution.py:877
  665.1 51.1 %all-to-all-start.2 = ((bf16[8,4,32,768]{3,2,1,0:T(8,128)(2,1)}), bf16[8,4,32,768]{3,2,1,0:T(8,128)(2,1)}, u32[]{:S(2)}, u32[]{:S(2)}) async-start(bf16[8,4,32,768]{3,2,1,0:T(8,128)(2,1)} %bitcast.192), calls=%async_computation.2 | async-start | bytes 3145728 | tf_op jit(solution)/shard_map/all_to_all | solution.py:746
  670.2 21.5 %collective-permute-start.16 = (f32[20,128]{1,0:T(8,128)S(1)}, f32[20,128]{1,0:T(8,128)S(1)}, u32[]{:S(2)}, u32[]{:S(2)}) collective-permute-start(f32[20,128]{1,0:T(8,128)S(1)} %fusion.77), channel_id=1, source_target_pairs={{0,2},{1,3},{2,0},{3,1},{4,6},{5,7},{6,4},{7,5},{8,10},{9,11},{10,... | collective-permute-start | bytes 30728 | tf_op jit(solution)/shard_map/ppermute | solution.py:877
  695.4 18.2 %collective-permute-start.18 = (f32[20,128]{1,0:T(8,128)S(1)}, f32[20,128]{1,0:T(8,128)S(1)}, u32[]{:S(2)}, u32[]{:S(2)}) collective-permute-start(f32[20,128]{1,0:T(8,128)S(1)} %add.336), channel_id=1, source_target_pairs={{0,8},{8,16},{16,24},{24,0},{1,9},{9,17},{17,25},{25,1},{2,10},{10... | collective-permute-start | bytes 30728 | tf_op jit(solution)/shard_map/ppermute | solution.py:738
  (29 other events, 534.1 us)

commit v3 on v2

--- a/solution.py
+++ b/solution.py
@@ -176,88 +176,6 @@
     return v * half, slope
 
 
-def expert_kernel(
-    main, slots_ref, dout_ref, wgu_ref, wd_ref,
-    out_ref, dslot_ref, gwgu_ref, gwd_ref, gwgu_acc, gwd_acc,
-):
-    step = pl.program_id(0)
-
-    @pl.when(step == 0)
-    def _():
-        gwgu_acc[...] = jnp.zeros_like(gwgu_acc)
-        gwd_acc[...] = jnp.zeros_like(gwd_acc)
-
-    slots, d_out = slots_ref[0], dout_ref[0]
-    rows = slots.shape[0]
-    wgu, wd = wgu_ref[...], wd_ref[...]
-    pre = mm(slots, wgu)
-    d_hidden = mm(d_out, wd, NT)
-    low_lane = lax.broadcasted_iota(jnp.int32, (rows, 128), 1) < 64
-    gate, up = pre[:, :main], pre[:, main : 2 * main]
-    tail = pre[:, 2 * main :]
-    tail_up = pltpu.roll(tail, 64, 1)
-    act, slope = gelu_pair(gate)
-    act_t, slope_t = gelu_pair(tail)
-    hidden_t = jnp.where(low_lane, act_t * tail_up, 0.0)
-    hidden = jnp.concatenate([(act * up).astype(BF16), hidden_t.astype(BF16)], axis=1)
-    out_ref[0] = mm(hidden, wd).astype(BF16)
-    gwd_acc[...] += mm(hidden, d_out, TN)
-    dh, dh_t = d_hidden[:, :main], d_hidden[:, main:]
-    d_gate = dh * up * slope
-    d_up = dh * act
-    d_tail = jnp.where(low_lane, dh_t * tail_up * slope_t, pltpu.roll(dh_t * act_t, 64, 1))
-    d_pre = jnp.concatenate([d_gate.astype(BF16), d_up.astype(BF16), d_tail.astype(BF16)], axis=1)
-    dslot_ref[0] = mm(d_pre, wgu, NT).astype(BF16)
-    gwgu_acc[...] += mm(slots, d_pre, TN)
-
-    @pl.when(step == pl.num_programs(0) - 1)
-    def _():
-        gwgu_ref[...] = gwgu_acc[...].astype(BF16)
-        gwd_ref[...] = gwd_acc[...]
-
-
-def experts(slots, d_outs, wgu, wd, steps):
-    width, columns = wgu.shape
-    deep = wd.shape[0]
-    main = (columns - 128) // 2
-    slots = slots.reshape(steps, -1, width)
-    d_outs = d_outs.reshape(steps, -1, width)
-    half = slots.shape[1]
-    rows = half * steps
-    part = pl.BlockSpec((1, half, width), lambda i: (i, 0, 0))
-    return pl.pallas_call(
-        functools.partial(expert_kernel, main),
-        grid=(steps,),
-        in_specs=[
-            part, part,
-            pl.BlockSpec((width, columns), lambda i: (0, 0)),
-            pl.BlockSpec((deep, width), lambda i: (0, 0)),
-        ],
-        out_specs=[
-            part, part,
-            pl.BlockSpec((width, columns), lambda i: (0, 0)),
-            pl.BlockSpec((deep, width), lambda i: (0, 0)),
-        ],
-        out_shape=[
-            jax.ShapeDtypeStruct((steps, half, width), BF16),
-            jax.ShapeDtypeStruct((steps, half, width), BF16),
-            jax.ShapeDtypeStruct((width, columns), BF16),
-            jax.ShapeDtypeStruct((deep, width), F32),
-        ],
-        scratch_shapes=[
-            pltpu.VMEM((width, columns), F32),
-            pltpu.VMEM((deep, width), F32),
-        ],
-        compiler_params=pltpu.CompilerParams(vmem_limit_bytes=VMEM_LIMIT),
-        cost_estimate=pl.CostEstimate(
-            flops=6 * rows * width * (columns + deep),
-            bytes_accessed=8 * rows * width + 8 * width * columns,
-            transcendentals=rows * deep,
-        ),
-        name="experts",
-    )(slots, d_outs, wgu, wd)
-
-
 def unpack_kernel(n, piece, in_ref, gate_ref, up_ref):
     main = piece // 128 * 128
     rest = piece - main
@@ -734,6 +652,155 @@
     )(x_all, wq, wk, wv, wo, gain_one, gain_two, vectors, cot, meta_all, packed)
 
 
+def experts_kernel(
+    n, ne, cap_pad, deep, main,
+    slots, d_outs, wgu_ref, wd_ref, meta_all,
+    out_rows, d_two, gwgu, gwd,
+    s_buf, d_buf, back, part, landed, gwgu_acc,
+    load_sem, keep_sem, p_send, p_recv, z_send, z_recv,
+):
+    dp, ex = lax.axis_index("dp"), lax.axis_index("expert")
+    slots_n, width = s_buf.shape[1:]
+    tok = d_two.shape[0]
+    greet(n, ne, dp, ex)
+    toward = 2 * ((2 * dp) // n) - 1
+
+    def group_at(step):
+        return lax.rem(dp + n + toward * (1 + step), n)
+
+    def load(step, kind):
+        at = group_at(step)
+        src, dst = ((slots, s_buf), (d_outs, d_buf))[kind]
+        return pltpu.make_async_copy(src.at[at], dst.at[at], load_sem.at[kind, step])
+
+    for step in range(n):
+        for kind in range(2):
+            load(step, kind).start()
+    gwgu_acc[...] = jnp.zeros_like(gwgu_acc)
+    gwd[...] = jnp.zeros_like(gwd)
+
+    def rows_of(peer):
+        return pl.ds(pl.multiple_of(peer * cap_pad, 16), cap_pad)
+
+    def give(at, k):
+        peer = lax.rem(ex + k, ne)
+        return remote(
+            d_buf.at[at, rows_of(peer)], back.at[at, rows_of(ex)], p_send.at[at, k], p_recv.at[at, k], (dp, peer)
+        )
+
+    def take(at, k):
+        peer = lax.rem(ex + ne - k, ne)
+        return remote(
+            d_buf.at[at, rows_of(ex)], back.at[at, rows_of(peer)], p_send.at[at, k], p_recv.at[at, k], (dp, peer)
+        )
+
+    def keep(at):
+        return pltpu.make_async_copy(s_buf.at[at], out_rows.at[at], keep_sem.at[at])
+
+    def owed(at):
+        return remote(part.at[at], landed.at[dp], z_send.at[at], z_recv.at[dp], (at, ex))
+
+    def combine(at):
+        for k in range(1, ne):
+            take(at, k).wait_recv()
+        meta = meta_all[at]
+        ids = lax.broadcasted_iota(jnp.int32, (slots_n, tok), 0).astype(F32)
+        hit = (ids == meta[0:1, :]) | (ids == meta[1:2, :])
+        return mm(jnp.where(hit, 1.0, 0.0).astype(BF16), back[at], TN)
+
+    @pl.loop(0, n)
+    def _(step):
+        at = group_at(step)
+        for kind in range(2):
+            load(step, kind).wait()
+        wgu, wd = wgu_ref[...], wd_ref[...]
+        parts = -(-slots_n // 640)
+        size = slots_n // parts
+        low_lane = lax.broadcasted_iota(jnp.int32, (size, 128), 1) < 64
+        for p in range(parts):
+            here = slice(p * size, (p + 1) * size)
+            rows, d_out = s_buf[at, here, :], d_buf[at, here, :]
+            pre = mm(rows, wgu)
+            d_hidden = mm(d_out, wd, NT)
+            gate, up, tail = pre[:, :main], pre[:, main : 2 * main], pre[:, 2 * main :]
+            tail_up = pltpu.roll(tail, 64, 1)
+            act, slope = gelu_pair(gate)
+            act_t, slope_t = gelu_pair(tail)
+            hidden_t = jnp.where(low_lane, act_t * tail_up, 0.0)
+            hidden = jnp.concatenate([(act * up).astype(BF16), hidden_t.astype(BF16)], axis=1)
+            dh, dh_t = d_hidden[:, :main], d_hidden[:, main:]
+            d_gate = dh * up * slope
+            d_up = dh * act
+            d_tail = jnp.where(low_lane, dh_t * tail_up * slope_t, pltpu.roll(dh_t * act_t, 64, 1))
+            d_pre = jnp.concatenate([d_gate.astype(BF16), d_up.astype(BF16), d_tail.astype(BF16)], axis=1)
+            d_rows = mm(d_pre, wgu, NT).astype(BF16)
+            gwd[...] += mm(hidden, d_out, TN)[:deep]
+            d_buf[at, here, :] = d_rows
+            if p == parts - 1:
+                for k in range(1, ne):
+                    give(at, k).start()
+                back[at, rows_of(ex), :] = d_buf[at, rows_of(ex), :]
+            gwgu_acc[...] += mm(rows, d_pre, TN)
+            s_buf[at, here, :] = mm(hidden, wd).astype(BF16)
+        keep(at).start()
+
+        @pl.when(step > 0)
+        def _():
+            past = group_at(step - 1)
+            part[past] = combine(past).astype(BF16)
+            owed(past).start()
+
+    gwgu[...] = gwgu_acc[...].astype(BF16)
+    total = combine(dp)
+    for d in range(1, n):
+        src = lax.rem(dp + d, n)
+        remote(part.at[src], landed.at[src], z_send.at[src], z_recv.at[src], (src, ex)).wait_recv()
+        total = total + landed[src].astype(F32)
+    d_two[...] = total
+    for d in range(1, n):
+        owed(lax.rem(dp + d, n)).wait_send()
+
+    @pl.loop(0, n)
+    def _(at):
+        keep(at).wait()
+        for k in range(1, ne):
+            give(at, k).wait_send()
+
+
+def experts(n, ne, cap_pad, deep, slots, d_outs, wgu, wd, meta_all):
+    width, columns = wgu.shape
+    tok = meta_all.shape[2]
+    main = (columns - 128) // 2
+    slots_n = ne * cap_pad
+    slots = slots.reshape(n, slots_n, width)
+    d_outs = d_outs.reshape(n, slots_n, width)
+    sem = pltpu.SemaphoreType.DMA
+    return pl.pallas_call(
+        functools.partial(experts_kernel, n, ne, cap_pad, deep, main),
+        in_specs=[ANY, ANY, VM, VM, VM],
+        out_specs=[ANY, VM, VM, VM],
+        out_shape=[
+            jax.ShapeDtypeStruct((n, slots_n, width), BF16),
+            jax.ShapeDtypeStruct((tok, width), F32),
+            jax.ShapeDtypeStruct((width, columns), BF16),
+            jax.ShapeDtypeStruct((deep, width), F32),
+        ],
+        scratch_shapes=[
+            pltpu.VMEM((n, slots_n, width), BF16),
+            pltpu.VMEM((n, slots_n, width), BF16),
+            pltpu.VMEM((n, slots_n, width), BF16),
+            pltpu.VMEM((n, tok, width), BF16),
+            pltpu.VMEM((n, tok, width), BF16),
+            pltpu.VMEM((width, columns), F32),
+            sem((2, n)), sem((n,)), sem((n, ne)), sem((n, ne)), sem((n,)), sem((n,)),
+        ],
+        compiler_params=pltpu.CompilerParams(
+            collective_id=3, has_side_effects=True, vmem_limit_bytes=60 * 1024 * 1024
+        ),
+        name="experts",
+    )(slots, d_outs, wgu, wd, meta_all)
+
+
 def shift(value, distance, n):
     return lax.ppermute(value, "dp", [(i, (i + distance) % n) for i in range(n)])
 
@@ -803,9 +870,9 @@
     deep = w_down.shape[1]
     padded = -(-deep // 128) * 128
     wd = jnp.pad(w_down[0], ((0, padded - deep), (0, 0)))
-    steps = 2 * n
-    out_rows, dslot_rows, gwgu, gwd = experts(slots, d_outs, wgu, wd, steps)
-    grad_w_down = gwd[:deep]
+    out_rows, grad_normed_two, gwgu, grad_w_down = experts(
+        n, experts_n, cap_pad, deep, slots, d_outs, wgu, wd, meta_all
+    )
 
     dest = meta_all[:, :2].astype(jnp.int32)
     select = (dest[..., None] == jnp.arange(slots_n, dtype=jnp.int32)).astype(BF16)
@@ -818,10 +885,6 @@
         return jnp.swapaxes(exchange(rows), 0, 1).reshape(n, slots_n, width)
 
     got = trade(gwgu.reshape(n, width // n, gwgu.shape[1]), n, dp)
-    dslot_back = from_experts(dslot_rows)
-    dslot_back, got, out_rows = lax.optimization_barrier((dslot_back, got, out_rows))
-    partial = jnp.einsum("gts,gsd->gtd", both, dslot_back, preferred_element_type=F32)
-    grad_normed_two = to_owners(partial, n, dp)
     gain_one, gain_two = gain_one[0], gain_two[0]
     grad_top = cotangent[0].astype(F32)
     inverse_two = lax.rsqrt(jnp.mean(resid * resid, axis=-1, keepdims=True) + EPSILON)

time: 737 us -> 661 us (0.90)
  waiting for transfers between devices: 180 us -> 128 us
  starting transfers between devices: 114 us -> 71.5 us
  Pallas kernels: 344 us -> 368 us
    ppermute x24 -> x21, starting transfers between devices: 90.6 us -> 54.3 us  [shift(): lax.ppermute(value, 'dp', [(i, (i + distance) % n) for i in range(n)])]
    ppermute x24 -> x21, waiting for transfers between devices: 115 us -> 88.4 us  [shift(): lax.ppermute(value, 'dp', [(i, (i + distance) % n) for i in range(n)])]
    all_to_all x4 -> x3, waiting for transfers between devices: 45.7 us -> 21.3 us  [exchange(): lax.all_to_all(value, 'expert', split_axis=0, concat_axis=0, tiled=True)]
    pallas_call x1, Pallas kernels: 53.4 us -> 77.3 us  [experts(): pl.pallas_call(functools.partial(experts_kernel, n, ne, cap_pad, deep, ma...]
    all_to_all x4 -> x3, starting transfers between devices: 20.1 us -> 13.8 us  [exchange(): lax.all_to_all(value, 'expert', split_axis=0, concat_axis=0, tiled=True)]
  transfers between devices with their start and end apart: 31 -> 27, of which waited for: 19 -> 13; matrix products, arithmetic and copies ran while one was open for 7% -> 9% of each run, Pallas kernels for 4% -> 4%
where the time goes in v3:
time: 661 us; the launch traced here: 652 us
  Pallas kernels  368 us (56%)
  waiting for transfers between devices  128 us (19%)
  starting transfers between devices  71.5 us (11%)
  local copies, waits for them, and re-layouts  38.7 us (6%)
  other arithmetic  29.4 us (4%)
  matrix products  14.6 us (2%)
    pallas_call x1, Pallas kernels, forward(): pl.pallas_call(functools.partial(forward_kernel, n, ne, cap_pad), in_spec...  204 us
    ppermute x21, waiting for transfers between devices, shift(): lax.ppermute(value, 'dp', [(i, (i + distance) % n) for i in range(n)])  88.4 us
    pallas_call x1, Pallas kernels, experts(): pl.pallas_call(functools.partial(experts_kernel, n, ne, cap_pad, deep, ma...  77.3 us
    pallas_call x1, Pallas kernels, start(): pl.pallas_call(functools.partial(start_kernel, n, ne, cap, cap_pad, piece...  58.7 us
    ppermute x21, starting transfers between devices, shift(): lax.ppermute(value, 'dp', [(i, (i + distance) % n) for i in range(n)])  54.3 us
    pallas_call x1, Pallas kernels, attention_backward(): pl.pallas_call(functools.partial(attention_backward_kernel, n, block), gr...  23.6 us
    all_to_all x3, waiting for transfers between devices, exchange(): lax.all_to_all(value, 'expert', split_axis=0, concat_axis=0, tiled=True)  21.3 us
    ppermute x3, waiting for transfers between devices, local(): lax.ppermute(small, 'expert', [(i, i ^ step) for i in range(experts_n)])  18.3 us
  transfers between devices with their start and end apart: 27, of which 13 were waited for; matrix products, arithmetic and copies ran while one was open for 9% of the time, Pallas kernels for 4%

profile of v3, /device:TPU:0, one launch (start us, length us, event | category | flops | bytes accessed | tf_op | source)
XLA Modules:
  0.0 651.9 jit_solution(14826215767642971058)
XLA Ops:
  3.5 58.7 %start.1 = (bf16[4,256,1024]{2,1,0:T(8,128)(2,1)}, bf16[4,8,32,256]{3,2,1,0:T(8,128)(2,1)}, bf16[4,8,32,256]{3,2,1,0:T(8,128)(2,1)}, bf16[4,8,32,256]{3,2,1,0:T(...) custom-call(bf16[256,1024]{1,0:T(8,128)(2,1)} %bitcast.164, ...), custom_call_target="tpu_custom_call" | custom-call | tf_op jit(solution)/shard_map/start/pallas_call | solution.py:428
  67.6 203.7 %forward.1 = (bf16[1024,1024]{1,0:T(8,128)(2,1)}, bf16[1024,768]{1,0:T(8,128)(2,1)}, f32[1024,256]{1,0:T(8,128)}, bf16[256,1024]{1,0:T(8,128)(2,1)}, f32[256,102...) custom-call(bf16[4,256,1024]{2,1,0:T(8,128)(2,1)} %get-tuple-element, ...), custom_call_target="tpu_custom_call" | custom-call | tf_op jit(solution)/shard_map/forward/pallas_call | solution.py:620
  272.7 77.3 %experts.1 = (bf16[4,640,1024]{2,1,0:T(8,128)(2,1)}, f32[256,1024]{1,0:T(8,128)}, bf16[1024,1408]{1,0:T(8,128)(2,1)}, f32[704,1024]{1,0:T(8,128)}) custom-call(bf16[4,640,1024]{2,1,0:T(8,128)(2,1)} %bitcast.166, bf16[4,640,1024]{2,1,0:T(8,128)(2,1)} %bitcast.167, bf16[1024,1408]{1,0:T(8,128)(2,1)} %bitcast.170, bf16[768,1024]{1,0:T(8,128)(2,1)} %pad.9.wd_ref, ...), custom_call_target="tpu_custom_call" | custom-call | tf_op jit(solution)/shard_map/experts/pallas_call | solution.py:778
  355.4 4.8 all-to-all-start.2
  360.2 5.7 copy.80
  366.0 21.2 %all-to-all-done.2 = bf16[8,4,32,1024]{3,2,1,0:T(8,128)(2,1)} async-done(((bf16[8,4,32,1024]{3,2,1,0:T(8,128)(2,1)}), bf16[8,4,32,1024]{3,2,1,0:T(8,128)(2,1)}, u32[]{:S(2)}, u32[]{:S(2)}) %all-to-all-start.2) | async-done | bytes 2097184 | tf_op jit(solution)/shard_map/all_to_all | solution.py:813
  387.2 4.7 all-to-all-start
  391.9 3.6 constant_dynamic-slice_fusion.4
  395.5 7.6 %collective-permute-start.21 = (bf16[256,1408]{1,0:T(8,128)(2,1)}, bf16[256,1408]{1,0:T(8,128)(2,1)}, u32[]{:S(2)}, u32[]{:S(2)}) collective-permute-start(bf16[256,1408]{1,0:T(8,128)(2,1)} %get-tuple-element.102), channel_id=1, source_target_pairs={{0,8},{8,16},{16,24},{24,0},{1,9},{9,17},{17,25},{25,1},{2,10},{10... | collective-permute-start | bytes 2162696 | tf_op jit(solution)/shard_map/ppermute | solution.py:805
  419.4 34.3 %collective-permute-done = bf16[256,256]{1,0:T(8,128)(2,1)} collective-permute-done((bf16[256,256]{1,0:T(8,128)(2,1)}, bf16[256,256]{1,0:T(8,128)(2,1)}, u32[]{:S(2)}, u32[]{:S(2)}) %collective-permute-start) | collective-permute-done | bytes 131104 | tf_op jit(solution)/shard_map/ppermute | solution.py:805
  453.7 17.1 %collective-permute-done.1 = bf16[256,256]{1,0:T(8,128)(2,1)} collective-permute-done((bf16[256,256]{1,0:T(8,128)(2,1)}, bf16[256,256]{1,0:T(8,128)(2,1)}, u32[]{:S(2)}, u32[]{:S(2)}) %collective-permute-start.1) | collective-permute-done | bytes 131104 | tf_op jit(solution)/shard_map/ppermute | solution.py:805
  470.8 8.8 %collective-permute-done.2 = bf16[256,256]{1,0:T(8,128)(2,1)S(1)} collective-permute-done((bf16[256,256]{1,0:T(8,128)(2,1)}, bf16[256,256]{1,0:T(8,128)(2,1)S(1)}, u32[]{:S(2)}, u32[]{:S(2)}) %collective-permute-start.2) | collective-permute-done | bytes 131104 | tf_op jit(solution)/shard_map/ppermute | solution.py:805
  492.2 3.3 copy.51
  495.5 4.1 multiply_reduce_fusion
  505.2 23.6 %attention_backward.1 = (bf16[1024,256]{1,0:T(8,128)(2,1)}, bf16[1024,256]{1,0:T(8,128)(2,1)}, bf16[1024,256]{1,0:T(8,128)(2,1)}, f32[2,2,2048]{2,1,0:T(2,128)}) custom-call(bf16[1024,768]{1,0:T(8,128)(2,1)} %get-tuple-element.63.q_ref.k_ref.v_ref, bf16[1024,768]{1,0:T(8,128)(2,1)} %get-tuple-element.63.q_ref.k_ref.v_ref, ...), custom_call_target="tpu_custom_call" | custom-call | flops 10737418240 | bytes 3670016 | tf_op jit(solution)/shard_map/attention_backward/pallas_call | solution.py:134
  533.3 3.7 collective-permute-done.4
  540.9 11.7 %collective-permute-start.6 = (bf16[256,1024]{1,0:T(8,128)(2,1)}, bf16[256,1024]{1,0:T(8,128)(2,1)}, u32[]{:S(2)}, u32[]{:S(2)}) collective-permute-start(bf16[256,1024]{1,0:T(8,128)(2,1)} %get-tuple-element.89), channel_id=1, source_target_pairs={{0,8},{8,16},{16,24},{24,0},{1,9},{9,17},{17,25},{25,1},{2,10},{10... | collective-permute-start | bytes 1572872 | tf_op jit(solution)/shard_map/ppermute | solution.py:805
  556.8 4.9 unpack_columns.1
  567.1 18.3 %collective-permute-done.7 = bf16[256,1024]{1,0:T(8,128)(2,1)} collective-permute-done((bf16[256,1024]{1,0:T(8,128)(2,1)}, bf16[256,1024]{1,0:T(8,128)(2,1)}, u32[]{:S(2)}, u32[]{:S(2)}) %collective-permute-start.7) | collective-permute-done | bytes 524320 | tf_op jit(solution)/shard_map/ppermute | solution.py:805
  585.4 3.2 fusion.17
  591.8 4.3 all-to-all-start.1
  600.3 16.1 %collective-permute-done.10 = f32[20,128]{1,0:T(8,128)S(1)} collective-permute-done((f32[20,128]{1,0:T(8,128)S(1)}, f32[20,128]{1,0:T(8,128)S(1)}, u32[]{:S(2)}, u32[]{:S(2)}) %collective-permute-start.10) | collective-permute-done | bytes 10272 | tf_op jit(solution)/shard_map/ppermute | solution.py:940
  620.1 11.7 %collective-permute-start.12 = (f32[20,128]{1,0:T(8,128)S(1)}, f32[20,128]{1,0:T(8,128)S(1)}, u32[]{:S(2)}, u32[]{:S(2)}) collective-permute-start(f32[20,128]{1,0:T(8,128)S(1)} %add.309), channel_id=1, source_target_pairs={{0,8},{8,16},{16,24},{24,0},{1,9},{9,17},{17,25},{25,1},{2,10},{10... | collective-permute-start | bytes 30728 | tf_op jit(solution)/shard_map/ppermute | solution.py:805
  631.8 3.1 collective-permute-start.13
  (184 shorter events, 94.9 us)
Async XLA Ops:
  355.4 31.8 %all-to-all-start.2 = ((bf16[8,4,32,1024]{3,2,1,0:T(8,128)(2,1)}), bf16[8,4,32,1024]{3,2,1,0:T(8,128)(2,1)}, u32[]{:S(2)}, u32[]{:S(2)}) async-start(bf16[8,4,32,1024]{3,2,1,0:T(8,128)(2,1)} %bitcast.163), calls=%async_computation.2 | async-start | bytes 4194304 | tf_op jit(solution)/shard_map/all_to_all | solution.py:813
  387.2 105.0 %all-to-all-start = ((bf16[8,4,80,1024]{3,2,1,0:T(8,128)(2,1)}), bf16[8,4,80,1024]{3,2,1,0:T(8,128)(2,1)}, u32[]{:S(2)}, u32[]{:S(2)}) async-start(bf16[8,4,80,1024]{3,2,1,0:T(8,128)(2,1)} %bitcast.157), calls=%async_computation | async-start | bytes 10485760 | tf_op jit(solution)/shard_map/all_to_all | solution.py:813
  395.5 86.0 %collective-permute-start.21 = (bf16[256,1408]{1,0:T(8,128)(2,1)}, bf16[256,1408]{1,0:T(8,128)(2,1)}, u32[]{:S(2)}, u32[]{:S(2)}) collective-permute-start(bf16[256,1408]{1,0:T(8,128)(2,1)} %get-tuple-element.102), channel_id=1, source_target_pairs={{0,8},{8,16},{16,24},{24,0},{1,9},{9,17},{17,25},{25,1},{2,10},{10... | collective-permute-start | bytes 2162696 | tf_op jit(solution)/shard_map/ppermute | solution.py:805
  403.1 78.4 %collective-permute-start.22 = (bf16[256,1408]{1,0:T(8,128)(2,1)}, bf16[256,1408]{1,0:T(8,128)(2,1)}, u32[]{:S(2)}, u32[]{:S(2)}) collective-permute-start(bf16[256,1408]{1,0:T(8,128)(2,1)} %get-tuple-element.101), channel_id=1, source_target_pairs={{0,16},{8,24},{16,0},{24,8},{1,17},{9,25},{17,1},{25,9},{2,18},{10... | collective-permute-start | bytes 2162696 | tf_op jit(solution)/shard_map/ppermute | solution.py:805
  404.3 77.2 %collective-permute-start.23 = (bf16[256,1408]{1,0:T(8,128)(2,1)}, bf16[256,1408]{1,0:T(8,128)(2,1)}, u32[]{:S(2)}, u32[]{:S(2)}) collective-permute-start(bf16[256,1408]{1,0:T(8,128)(2,1)} %get-tuple-element.100), channel_id=1, source_target_pairs={{0,24},{8,0},{16,8},{24,16},{1,25},{9,1},{17,9},{25,17},{2,26},{10... | collective-permute-start | bytes 2162696 | tf_op jit(solution)/shard_map/ppermute | solution.py:805
  412.8 40.8 %collective-permute-start = (bf16[256,256]{1,0:T(8,128)(2,1)}, bf16[256,256]{1,0:T(8,128)(2,1)}, u32[]{:S(2)}, u32[]{:S(2)}) collective-permute-start(bf16[256,256]{1,0:T(8,128)(2,1)} %bitcast.154), channel_id=1, source_target_pairs={{0,8},{8,16},{16,24},{24,0},{1,9},{9,17},{17,25},{25,1},{2,10},{10... | collective-permute-start | bytes 393224 | tf_op jit(solution)/shard_map/ppermute | solution.py:805
  413.5 57.3 %collective-permute-start.1 = (bf16[256,256]{1,0:T(8,128)(2,1)}, bf16[256,256]{1,0:T(8,128)(2,1)}, u32[]{:S(2)}, u32[]{:S(2)}) collective-permute-start(bf16[256,256]{1,0:T(8,128)(2,1)} %bitcast.153), channel_id=1, source_target_pairs={{0,16},{8,24},{16,0},{24,8},{1,17},{9,25},{17,1},{25,9},{2,18},{10... | collective-permute-start | bytes 393224 | tf_op jit(solution)/shard_map/ppermute | solution.py:805
  453.6 25.9 %collective-permute-start.2 = (bf16[256,256]{1,0:T(8,128)(2,1)}, bf16[256,256]{1,0:T(8,128)(2,1)S(1)}, u32[]{:S(2)}, u32[]{:S(2)}) collective-permute-start(bf16[256,256]{1,0:T(8,128)(2,1)} %bitcast.189), channel_id=1, source_target_pairs={{0,24},{8,0},{16,8},{24,16},{1,25},{9,1},{17,9},{25,17},{2,26},{10... | collective-permute-start | bytes 393224 | tf_op jit(solution)/shard_map/ppermute | solution.py:805
  488.2 66.2 %collective-permute-start.18 = (bf16[32,1024]{1,0:T(8,128)(2,1)}, bf16[32,1024]{1,0:T(8,128)(2,1)S(1)}, u32[]{:S(2)}, u32[]{:S(2)}) collective-permute-start(bf16[32,1024]{1,0:T(8,128)(2,1)} %get-tuple-element.103), channel_id=1, source_target_pairs={{0,8},{8,16},{16,24},{24,0},{1,9},{9,17},{17,25},{25,1},{2,10},{10... | collective-permute-start | bytes 196616 | tf_op jit(solution)/shard_map/ppermute | solution.py:805
  490.7 71.0 %collective-permute-start.19 = (bf16[32,1024]{1,0:T(8,128)(2,1)}, bf16[32,1024]{1,0:T(8,128)(2,1)S(1)}, u32[]{:S(2)}, u32[]{:S(2)}) collective-permute-start(bf16[32,1024]{1,0:T(8,128)(2,1)} %get-tuple-element.105), channel_id=1, source_target_pairs={{0,16},{8,24},{16,0},{24,8},{1,17},{9,25},{17,1},{25,9},{2,18},{10... | collective-permute-start | bytes 196616 | tf_op jit(solution)/shard_map/ppermute | solution.py:805
  500.8 31.8 %collective-permute-start.3 = (bf16[256,1024]{1,0:T(8,128)(2,1)}, bf16[256,1024]{1,0:T(8,128)(2,1)}, u32[]{:S(2)}, u32[]{:S(2)}) collective-permute-start(bf16[256,1024]{1,0:T(8,128)(2,1)} %get-tuple-element.92), channel_id=1, source_target_pairs={{0,8},{8,16},{16,24},{24,0},{1,9},{9,17},{17,25},{25,1},{2,10},{10... | collective-permute-start | bytes 1572872 | tf_op jit(solution)/shard_map/ppermute | solution.py:805
  501.4 35.6 %collective-permute-start.4 = (bf16[256,1024]{1,0:T(8,128)(2,1)}, bf16[256,1024]{1,0:T(8,128)(2,1)}, u32[]{:S(2)}, u32[]{:S(2)}) collective-permute-start(bf16[256,1024]{1,0:T(8,128)(2,1)} %get-tuple-element.94), channel_id=1, source_target_pairs={{0,16},{8,24},{16,0},{24,8},{1,17},{9,25},{17,1},{25,9},{2,18},{10... | collective-permute-start | bytes 1572872 | tf_op jit(solution)/shard_map/ppermute | solution.py:805
  504.3 32.7 %collective-permute-start.5 = (bf16[256,1024]{1,0:T(8,128)(2,1)}, bf16[256,1024]{1,0:T(8,128)(2,1)}, u32[]{:S(2)}, u32[]{:S(2)}) collective-permute-start(bf16[256,1024]{1,0:T(8,128)(2,1)} %get-tuple-element.93), channel_id=1, source_target_pairs={{0,24},{8,0},{16,8},{24,16},{1,25},{9,1},{17,9},{25,17},{2,26},{10... | collective-permute-start | bytes 1572872 | tf_op jit(solution)/shard_map/ppermute | solution.py:805
  532.7 29.0 %collective-permute-start.20 = (bf16[32,1024]{1,0:T(8,128)(2,1)S(1)}, bf16[32,1024]{1,0:T(8,128)(2,1)S(1)}, u32[]{:S(2)}, u32[]{:S(2)}) collective-permute-start(bf16[32,1024]{1,0:T(8,128)(2,1)S(1)} %get-tuple-element.104), channel_id=1, source_target_pairs={{0,24},{8,0},{16,8},{24,16},{1,25},{9,1},{17,9},{25,17},{2,26},{10... | collective-permute-start | bytes 196616 | tf_op jit(solution)/shard_map/ppermute | solution.py:805
  540.9 26.3 %collective-permute-start.6 = (bf16[256,1024]{1,0:T(8,128)(2,1)}, bf16[256,1024]{1,0:T(8,128)(2,1)}, u32[]{:S(2)}, u32[]{:S(2)}) collective-permute-start(bf16[256,1024]{1,0:T(8,128)(2,1)} %get-tuple-element.89), channel_id=1, source_target_pairs={{0,8},{8,16},{16,24},{24,0},{1,9},{9,17},{17,25},{25,1},{2,10},{10... | collective-permute-start | bytes 1572872 | tf_op jit(solution)/shard_map/ppermute | solution.py:805
  552.6 32.9 %collective-permute-start.7 = (bf16[256,1024]{1,0:T(8,128)(2,1)}, bf16[256,1024]{1,0:T(8,128)(2,1)}, u32[]{:S(2)}, u32[]{:S(2)}) collective-permute-start(bf16[256,1024]{1,0:T(8,128)(2,1)} %get-tuple-element.91), channel_id=1, source_target_pairs={{0,16},{8,24},{16,0},{24,8},{1,17},{9,25},{17,1},{25,9},{2,18},{10... | collective-permute-start | bytes 1572872 | tf_op jit(solution)/shard_map/ppermute | solution.py:805
  554.4 31.1 %collective-permute-start.8 = (bf16[256,1024]{1,0:T(8,128)(2,1)}, bf16[256,1024]{1,0:T(8,128)(2,1)}, u32[]{:S(2)}, u32[]{:S(2)}) collective-permute-start(bf16[256,1024]{1,0:T(8,128)(2,1)} %get-tuple-element.90), channel_id=1, source_target_pairs={{0,24},{8,0},{16,8},{24,16},{1,25},{9,1},{17,9},{25,17},{2,26},{10... | collective-permute-start | bytes 1572872 | tf_op jit(solution)/shard_map/ppermute | solution.py:805
  588.6 7.5 %collective-permute-start.9 = (f32[20,128]{1,0:T(8,128)S(1)}, f32[20,128]{1,0:T(8,128)S(1)}, u32[]{:S(2)}, u32[]{:S(2)}) collective-permute-start(f32[20,128]{1,0:T(8,128)S(1)} %maximum_bitcast_fusion), channel_id=1, source_target_pairs={{0,1},{1,0},{2,3},{3,2},{4,5},{5,4},{6,7},{7,6},{8,9},{9,8},{10,11... | collective-permute-start | bytes 30728 | tf_op jit(solution)/shard_map/ppermute | solution.py:940
  591.8 46.8 %all-to-all-start.1 = ((bf16[8,4,32,768]{3,2,1,0:T(8,128)(2,1)}), bf16[8,4,32,768]{3,2,1,0:T(8,128)(2,1)}, u32[]{:S(2)}, u32[]{:S(2)}) async-start(bf16[8,4,32,768]{3,2,1,0:T(8,128)(2,1)} %bitcast.165), calls=%async_computation.1 | async-start | bytes 3145728 | tf_op jit(solution)/shard_map/all_to_all | solution.py:813
  596.2 20.2 %collective-permute-start.10 = (f32[20,128]{1,0:T(8,128)S(1)}, f32[20,128]{1,0:T(8,128)S(1)}, u32[]{:S(2)}, u32[]{:S(2)}) collective-permute-start(f32[20,128]{1,0:T(8,128)S(1)} %fusion.67), channel_id=1, source_target_pairs={{0,2},{1,3},{2,0},{3,1},{4,6},{5,7},{6,4},{7,5},{8,10},{9,11},{10,... | collective-permute-start | bytes 30728 | tf_op jit(solution)/shard_map/ppermute | solution.py:940
  620.1 16.0 %collective-permute-start.12 = (f32[20,128]{1,0:T(8,128)S(1)}, f32[20,128]{1,0:T(8,128)S(1)}, u32[]{:S(2)}, u32[]{:S(2)}) collective-permute-start(f32[20,128]{1,0:T(8,128)S(1)} %add.309), channel_id=1, source_target_pairs={{0,8},{8,16},{16,24},{24,0},{1,9},{9,17},{17,25},{25,1},{2,10},{10... | collective-permute-start | bytes 30728 | tf_op jit(solution)/shard_map/ppermute | solution.py:805
  631.8 4.8 collective-permute-start.13
  640.5 5.9 collective-permute-start.15
  640.5 5.9 collective-permute-start.16
  (33 other events, 740.7 us)

commit v4 on v3

--- a/solution.py
+++ b/solution.py
@@ -37,20 +37,6 @@
     return nearby + jnp.where(offset > 0, 16, 0).astype(jnp.int32)
 
 
-def norm_forward(values, gain):
-    inverse = lax.rsqrt(jnp.mean(values * values, axis=-1, keepdims=True) + EPSILON)
-    return (inverse, (values * inverse * gain).astype(BF16))
-
-
-def norm_backward(values, inverse, gain, grad_normed):
-    scaled = gain * grad_normed
-    grad_gain = jnp.sum(grad_normed * values * inverse, axis=0)
-    grad_values = inverse * scaled - values * inverse**3 * jnp.mean(
-        scaled * values, axis=-1, keepdims=True
-    )
-    return (grad_gain, grad_values)
-
-
 def bias_tile(vec_ref, head, tile_ref):
     block, wide = tile_ref.shape
     row = jnp.broadcast_to(vec_ref[pl.ds(head, 1), :], (block, wide))
@@ -77,95 +63,6 @@
         tile = tile[:half] + pltpu.roll(tile[half:], wide - half, 1)
         rows = half
     return tile
-
-
-def attention_backward_kernel(
-    n, block, q_ref, k_ref, v_ref, lse_ref, dm_ref, vec_ref,
-    dq_ref, dk_ref, dv_ref, diag_ref, tiles, sums, dk_acc, dv_acc,
-):
-    pair, query_block = pl.program_id(0), pl.program_id(1)
-
-    @pl.when(query_block == 0)
-    def _():
-        for side in range(2):
-            bias_tile(vec_ref, 2 * pair + side, tiles.at[side])
-        sums[...] = jnp.zeros_like(sums)
-        dk_acc[...] = jnp.zeros_like(dk_acc)
-        dv_acc[...] = jnp.zeros_like(dv_acc)
-
-    q_pair, k_pair, v_pair, dm_pair = q_ref[...], k_ref[...], v_ref[...], dm_ref[...]
-    rows = k_pair.shape[0]
-    lane = lax.broadcasted_iota(jnp.int32, (block, 128), 1)
-    dqs, dks, dvs = [], [], []
-    for side in range(2):
-        mask = (lane >= HEAD_DIM) if side else (lane < HEAD_DIM)
-        logits = logits_of(n, block, query_block, q_pair, k_pair, mask, tiles.at[side])
-        probs = jnp.exp(logits - lse_ref[:, side * HEAD_DIM : side * HEAD_DIM + 1])
-        masked = jnp.where(mask, dm_pair, jnp.zeros_like(dm_pair))
-        d_probs = mm(masked, v_pair, NT)
-        inner = jnp.sum(probs * d_probs, axis=-1, keepdims=True)
-        d_logits = (probs * (d_probs - inner)).astype(BF16)
-        dvs.append(mm(probs.astype(BF16), dm_pair, TN))
-        dqs.append(mm(d_logits, k_pair))
-        dks.append(mm(d_logits, q_pair, TN))
-        wide = d_logits.astype(F32)
-        for j in range(n):
-            here = pl.ds(tile_offset(n, block, query_block, j), block)
-            sums[side, :, here] += wide[:, j * block : (j + 1) * block]
-    dq_ref[...] = (jnp.where(lane < HEAD_DIM, dqs[0], dqs[1]) * SCALE).astype(BF16)
-    key_lane = lax.broadcasted_iota(jnp.int32, (rows, 128), 1)
-    dk_acc[...] += jnp.where(key_lane < HEAD_DIM, dks[0], dks[1])
-    dv_acc[...] += jnp.where(key_lane < HEAD_DIM, dvs[0], dvs[1])
-
-    @pl.when(query_block == n - 1)
-    def _():
-        dk_ref[...] = (dk_acc[...] * SCALE).astype(BF16)
-        dv_ref[...] = dv_acc[...].astype(BF16)
-        for side in range(2):
-            diag_ref[0, pl.ds(side, 1), :] = diagonal_sum(sums[side])
-
-
-def attention_backward(n, qkv, lse, d_mixed, vectors):
-    rows, triple = qkv.shape
-    own = triple // 3
-    block = rows // n
-    pairs = own // 128
-    wide = vectors.shape[1]
-    return pl.pallas_call(
-        functools.partial(attention_backward_kernel, n, block),
-        grid=(pairs, n),
-        in_specs=[
-            pl.BlockSpec((block, 128), lambda p, i: (i, p)),
-            pl.BlockSpec((rows, 128), lambda p, i: (0, pairs + p)),
-            pl.BlockSpec((rows, 128), lambda p, i: (0, 2 * pairs + p)),
-            pl.BlockSpec((block, 128), lambda p, i: (i, p)),
-            pl.BlockSpec((block, 128), lambda p, i: (i, p)),
-            pl.BlockSpec((2 * pairs, wide), lambda p, i: (0, 0)),
-        ],
-        out_specs=[
-            pl.BlockSpec((block, 128), lambda p, i: (i, p)),
-            pl.BlockSpec((rows, 128), lambda p, i: (0, p)),
-            pl.BlockSpec((rows, 128), lambda p, i: (0, p)),
-            pl.BlockSpec((1, 2, wide), lambda p, i: (p, 0, 0)),
-        ],
-        out_shape=[
-            jax.ShapeDtypeStruct((rows, own), BF16),
-            jax.ShapeDtypeStruct((rows, own), BF16),
-            jax.ShapeDtypeStruct((rows, own), BF16),
-            jax.ShapeDtypeStruct((pairs, 2, wide), F32),
-        ],
-        scratch_shapes=[
-            pltpu.VMEM((2, block, wide), F32),
-            pltpu.VMEM((2, block, wide), F32),
-            pltpu.VMEM((rows, 128), F32),
-            pltpu.VMEM((rows, 128), F32),
-        ],
-        compiler_params=pltpu.CompilerParams(vmem_limit_bytes=VMEM_LIMIT),
-        cost_estimate=pl.CostEstimate(
-            flops=40 * rows * rows * own, bytes_accessed=14 * rows * own, transcendentals=rows * rows * own // 64
-        ),
-        name="attention_backward",
-    )(qkv, qkv, qkv, lse, d_mixed, vectors)
 
 
 def gelu_pair(v):
@@ -801,28 +698,337 @@
     )(slots, d_outs, wgu, wd, meta_all)
 
 
-def shift(value, distance, n):
-    return lax.ppermute(value, "dp", [(i, (i + distance) % n) for i in range(n)])
-
-
-def pick(stacked, index):
-    return lax.dynamic_index_in_dim(stacked, index, 0, keepdims=False)
-
-
-def exchange(value):
-    return lax.all_to_all(value, "expert", split_axis=0, concat_axis=0, tiled=True)
-
-
-def trade(blocks, n, dp):
-    got = jnp.stack([pick(blocks, dp)] + [shift(pick(blocks, lax.rem(dp + d, n)), d, n) for d in range(1, n)])
-    return jnp.stack([pick(got, lax.rem(dp - j + n, n)) for j in range(n)])
-
-
-def to_owners(blocks, n, dp):
-    total = pick(blocks, dp).astype(F32)
-    for d in range(1, n):
-        total = total + shift(pick(blocks, lax.rem(dp + d, n)).astype(BF16), d, n).astype(F32)
-    return total
+def backward_kernel(
+    n, ne, cap_pad,
+    d_two, resid, cot, x, gain_one, gain_two, mixed, wo, qkv, lse, normed, vectors, wq, wk, wv, meta_all, in_bucket,
+    gwgu, out_rows,
+    block_out, grad_in, gq, gk, gv, go, small_all, gw_in, out_in,
+    dm, dm_in, tiles, sums, dq_s, dk_s, dv_s, dk_acc, dv_acc, diag, d_res,
+    dn_part, dn_land, moe_part, moe_land, out_one,
+    g_send, g_land, g2_send, g2_land, o_send, o_land, o2_send, o2_land,
+    small_own, small_land, small_sum,
+    out_s, out_r, w_s, w_r, dm_s, dm_r, dn_s, dn_r, moe_s, moe_r, g_s, g_r, o_s, o_r, g2_s, g2_r, o2_s, o2_r,
+    sp_s, sp_r, sz_s, sz_r, keep_sem,
+):
+    dp, ex = lax.axis_index("dp"), lax.axis_index("expert")
+    tok, width = cot.shape
+    own = dq_s.shape[1]
+    pairs_n = own // 128
+    slots_n = ne * cap_pad
+    wrows = go.shape[0]
+    greet(n, ne, dp, ex)
+    toward = 2 * ((2 * dp) // n) - 1
+
+    def group_at(step):
+        return lax.rem(dp + n + toward * (1 + step), n)
+
+    def rows_of(peer):
+        return pl.ds(pl.multiple_of(peer * cap_pad, 16), cap_pad)
+
+    def to_line(src, dst, send, recv, t):
+        return remote(src.at[t], dst.at[dp], send.at[t], recv.at[dp], (t, ex))
+
+    def from_line(src, dst, send, recv, t):
+        return remote(src.at[t], dst.at[t], send.at[t], recv.at[t], (t, ex))
+
+    def to_plane(src, dst, send, recv, k):
+        return remote(src, dst.at[ex], send.at[k], recv.at[k], (dp, lax.rem(ex + k, ne)))
+
+    def from_plane(src, dst, send, recv, k):
+        peer = lax.rem(ex + ne - k, ne)
+        return remote(src, dst.at[peer], send.at[k], recv.at[k], (dp, peer))
+
+    def out_give(at, k):
+        peer = lax.rem(ex + k, ne)
+        return remote(
+            out_rows.at[at, rows_of(peer)], out_in.at[at, rows_of(ex)], out_s.at[at, k], out_r.at[at, k], (dp, peer)
+        )
+
+    def out_take(at, k):
+        peer = lax.rem(ex + ne - k, ne)
+        return remote(
+            out_rows.at[at, rows_of(ex)], out_in.at[at, rows_of(peer)], out_s.at[at, k], out_r.at[at, k], (dp, peer)
+        )
+
+    def out_keep(at):
+        return pltpu.make_async_copy(out_rows.at[at, rows_of(ex)], out_in.at[at, rows_of(ex)], out_s.at[at, 0])
+
+    values = resid[...]
+    d_normed = d_two[...]
+    inverse = lax.rsqrt(jnp.mean(values * values, axis=-1, keepdims=True) + EPSILON)
+    scaled = gain_two[...] * d_normed
+    gain_rows_two = jnp.sum(d_normed * values * inverse, axis=0, keepdims=True)
+    mean = jnp.mean(scaled * values, axis=-1, keepdims=True)
+    d_resid = cot[...].astype(F32) + inverse * scaled - values * (inverse * inverse * inverse * mean)
+    d_res[...] = d_resid
+    d_attn = d_resid.astype(BF16)
+    d_mixed = mm(d_attn, wo[...], NT).astype(BF16)
+    for j in range(n):
+        dm[j] = d_mixed[:, j * own : (j + 1) * own]
+    for d in range(1, n):
+        to_line(dm, dm_in, dm_s, dm_r, lax.rem(dp + d, n)).start()
+    dm_in[dp] = dm[dp]
+    for d in range(1, n):
+        to_line(gwgu, gw_in, w_s, w_r, lax.rem(dp + d, n)).start()
+    keep_w = pltpu.make_async_copy(gwgu.at[dp], gw_in.at[dp], keep_sem.at[0])
+    keep_w.start()
+
+    @pl.loop(0, n)
+    def _(step):
+        at = group_at(step)
+        for k in range(1, ne):
+            out_give(at, k).start()
+        out_keep(at).start()
+
+    o_send[...] = mm(mixed[...], d_attn, TN).reshape(n, ne, wrows, width).astype(BF16)
+    for k in range(1, ne):
+        to_plane(o_send.at[:, lax.rem(ex + k, ne)], o_land, o_s, o_r, k).start()
+    o_land[ex] = o_send[:, ex]
+    for i in range(width // 128):
+        small_own[8 + i : 9 + i, :] = gain_rows_two[:, i * 128 : (i + 1) * 128]
+    for d in range(1, n):
+        from_line(dm, dm_in, dm_s, dm_r, lax.rem(dp + d, n)).wait_recv()
+
+    lane = lax.broadcasted_iota(jnp.int32, (tok, 128), 1)
+    low_half = lane < HEAD_DIM
+    key_low = lax.broadcasted_iota(jnp.int32, (n * tok, 128), 1) < HEAD_DIM
+    diag[...] = jnp.zeros_like(diag)
+    for pair in range(pairs_n):
+        cols = slice(pair * 128, (pair + 1) * 128)
+        for side in range(2):
+            bias_tile(vectors, 2 * pair + side, tiles.at[side])
+        sums[...] = jnp.zeros_like(sums)
+        dk_acc[...] = jnp.zeros_like(dk_acc)
+        dv_acc[...] = jnp.zeros_like(dv_acc)
+        k_pair = qkv[:, own + pair * 128 : own + (pair + 1) * 128]
+        v_pair = qkv[:, 2 * own + pair * 128 : 2 * own + (pair + 1) * 128]
+
+        @pl.loop(0, n)
+        def _(i):
+            at = pl.ds(pl.multiple_of(i * tok, tok), tok)
+            q_pair = qkv[at, cols]
+            dm_pair = dm_in[i, :, cols]
+            dqs, dks, dvs = [], [], []
+            for side in range(2):
+                mask = low_half if side == 0 else jnp.logical_not(low_half)
+                logits = logits_of(n, tok, i, q_pair, k_pair, mask, tiles.at[side])
+                first = pair * 128 + side * HEAD_DIM
+                probs = jnp.exp(logits - lse[at, first : first + 1])
+                d_probs = mm(jnp.where(mask, dm_pair, jnp.zeros_like(dm_pair)), v_pair, NT)
+                inner = jnp.sum(probs * d_probs, axis=-1, keepdims=True)
+                d_logits = (probs * (d_probs - inner)).astype(BF16)
+                dvs.append(mm(probs.astype(BF16), dm_pair, TN))
+                dqs.append(mm(d_logits, k_pair))
+                dks.append(mm(d_logits, q_pair, TN))
+                wide = d_logits.astype(F32)
+                for j in range(n):
+                    here = pl.ds(tile_offset(n, tok, i, j), tok)
+                    sums[side, :, here] += wide[:, j * tok : (j + 1) * tok]
+            dq_s[at, cols] = (jnp.where(low_half, dqs[0], dqs[1]) * SCALE).astype(BF16)
+            dk_acc[...] += jnp.where(key_low, dks[0], dks[1])
+            dv_acc[...] += jnp.where(key_low, dvs[0], dvs[1])
+
+        dk_s[:, cols] = (dk_acc[...] * SCALE).astype(BF16)
+        dv_s[:, cols] = dv_acc[...].astype(BF16)
+        for side in range(2):
+            diag[2 * pair + side : 2 * pair + side + 1, :] = diagonal_sum(sums[side])
+
+    def d_norm(t):
+        at = pl.ds(pl.multiple_of(t * tok, tok), tok)
+        return mm(dq_s[at, :], wq[...], NT) + mm(dk_s[at, :], wk[...], NT) + mm(dv_s[at, :], wv[...], NT)
+
+    @pl.loop(0, n - 1)
+    def _(step):
+        t = group_at(step)
+        dn_part[t] = d_norm(t).astype(BF16)
+        to_line(dn_part, dn_land, dn_s, dn_r, t).start()
+
+    for w, ref in enumerate((dq_s, dk_s, dv_s)):
+        g_send[:, :, w] = mm(normed[...], ref[...], TN).reshape(n, ne, wrows, own).astype(BF16)
+    for k in range(1, ne):
+        to_plane(g_send.at[:, lax.rem(ex + k, ne)], g_land, g_s, g_r, k).start()
+    g_land[ex] = g_send[:, ex]
+
+    rest = diag[...]
+    table = jnp.zeros((8, 128), F32)
+    for _ in range(3):
+        piece = rest.astype(BF16)
+        table = table + mm(piece, in_bucket[...])
+        rest = rest - piece.astype(F32)
+    small_own[16:24, :] = table
+
+    for k in range(1, ne):
+        from_plane(o_send.at[:, ex], o_land, o_s, o_r, k).wait_recv()
+    total = o_land[0].astype(F32)
+    for e in range(1, ne):
+        total = total + o_land[e].astype(F32)
+    o2_send[...] = total.astype(BF16)
+    for d in range(1, n):
+        to_line(o2_send, o2_land, o2_s, o2_r, lax.rem(dp + d, n)).start()
+    o2_land[dp] = o2_send[dp]
+
+    def moe(at):
+        for k in range(1, ne):
+            out_take(at, k).wait_recv()
+        out_keep(at).wait()
+        load = pltpu.make_async_copy(out_in.at[at], out_one, keep_sem.at[1])
+        load.start()
+        meta = meta_all[at]
+        ids = lax.broadcasted_iota(jnp.int32, (slots_n, tok), 0).astype(F32)
+        gate = meta[2:3, :]
+        weight = jnp.where(ids == meta[0:1, :], gate, 0.0) + jnp.where(ids == meta[1:2, :], 1.0 - gate, 0.0)
+        load.wait()
+        return mm(weight.astype(BF16), out_one[...], TN)
+
+    @pl.loop(0, n - 1)
+    def _(step):
+        t = group_at(step)
+        moe_part[t] = moe(t).astype(BF16)
+        to_line(moe_part, moe_land, moe_s, moe_r, t).start()
+
+    for k in range(1, ne):
+        from_plane(g_send.at[:, ex], g_land, g_s, g_r, k).wait_recv()
+    total = g_land[0].astype(F32)
+    for e in range(1, ne):
+        total = total + g_land[e].astype(F32)
+    g2_send[...] = total.astype(BF16)
+    for d in range(1, n):
+        to_line(g2_send, g2_land, g2_s, g2_r, lax.rem(dp + d, n)).start()
+    g2_land[dp] = g2_send[dp]
+
+    total = d_norm(dp)
+    for d in range(1, n):
+        t = lax.rem(dp + d, n)
+        from_line(dn_part, dn_land, dn_s, dn_r, t).wait_recv()
+        total = total + dn_land[t].astype(F32)
+    values = x[...].astype(F32)
+    inverse = lax.rsqrt(jnp.mean(values * values, axis=-1, keepdims=True) + EPSILON)
+    scaled = gain_one[...] * total
+    gain_rows_one = jnp.sum(total * values * inverse, axis=0, keepdims=True)
+    mean = jnp.mean(scaled * values, axis=-1, keepdims=True)
+    grad_in[...] = (d_res[...] + inverse * scaled - values * (inverse * inverse * inverse * mean)).astype(BF16)
+    for i in range(width // 128):
+        small_own[i : i + 1, :] = gain_rows_one[:, i * 128 : (i + 1) * 128]
+    for k in range(1, ne):
+        to_plane(small_own, small_land, sp_s, sp_r, k).start()
+    small_land[ex] = small_own[...]
+    for k in range(1, ne):
+        from_plane(small_own, small_land, sp_s, sp_r, k).wait_recv()
+    total = small_land[0]
+    for e in range(1, ne):
+        total = total + small_land[e]
+    small_sum[...] = total
+    for d in range(1, n):
+        t = lax.rem(dp + d, n)
+        remote(small_sum, small_all.at[dp], sz_s.at[t], sz_r.at[dp], (t, ex)).start()
+    small_all[dp] = total
+
+    total = resid[...] + moe(dp)
+    for d in range(1, n):
+        t = lax.rem(dp + d, n)
+        from_line(moe_part, moe_land, moe_s, moe_r, t).wait_recv()
+        total = total + moe_land[t].astype(F32)
+    block_out[...] = total.astype(BF16)
+
+    for d in range(1, n):
+        t = lax.rem(dp + d, n)
+        from_line(o2_send, o2_land, o2_s, o2_r, t).wait_recv()
+        from_line(g2_send, g2_land, g2_s, g2_r, t).wait_recv()
+        remote(small_sum, small_all.at[t], sz_s.at[t], sz_r.at[t], (t, ex)).wait_recv()
+    total = o2_land[0].astype(F32)
+    for j in range(1, n):
+        total = total + o2_land[j].astype(F32)
+    go[...] = total
+    for w, ref in enumerate((gq, gk, gv)):
+        ref[...] = jnp.concatenate([g2_land[j, w] for j in range(n)], axis=1).astype(F32)
+    for d in range(1, n):
+        t = lax.rem(dp + d, n)
+        from_line(gwgu, gw_in, w_s, w_r, t).wait_recv()
+        for src, dst, send, recv in (
+            (gwgu, gw_in, w_s, w_r), (dm, dm_in, dm_s, dm_r), (dn_part, dn_land, dn_s, dn_r),
+            (moe_part, moe_land, moe_s, moe_r), (o2_send, o2_land, o2_s, o2_r), (g2_send, g2_land, g2_s, g2_r),
+        ):
+            to_line(src, dst, send, recv, t).wait_send()
+        remote(small_sum, small_all.at[dp], sz_s.at[t], sz_r.at[dp], (t, ex)).wait_send()
+    keep_w.wait()
+    for k in range(1, ne):
+        to_plane(o_send.at[:, ex], o_land, o_s, o_r, k).wait_send()
+        to_plane(g_send.at[:, ex], g_land, g_s, g_r, k).wait_send()
+        to_plane(small_own, small_land, sp_s, sp_r, k).wait_send()
+
+    @pl.loop(0, n)
+    def _(at):
+        for k in range(1, ne):
+            out_give(at, k).wait_send()
+
+
+def backward(
+    n, ne, cap_pad, wrows, d_two, resid, cot, x, gain_one, gain_two, mixed, wo, qkv, lse, normed, vectors,
+    wq, wk, wv, meta_all, in_bucket, gwgu, out_rows,
+):
+    tok, width = cot.shape
+    own = wq.shape[1]
+    wide = vectors.shape[1]
+    both = gwgu.shape[2]
+    slots_n = ne * cap_pad
+    length = n * tok
+    sem = pltpu.SemaphoreType.DMA
+    shape = jax.ShapeDtypeStruct
+    return pl.pallas_call(
+        functools.partial(backward_kernel, n, ne, cap_pad),
+        in_specs=[VM] * 17 + [ANY] * 2,
+        out_specs=[VM] * 7 + [ANY] * 2,
+        out_shape=[
+            shape((tok, width), BF16),
+            shape((tok, width), BF16),
+            shape((wrows, width), F32),
+            shape((wrows, width), F32),
+            shape((wrows, width), F32),
+            shape((wrows, width), F32),
+            shape((n, 24, 128), F32),
+            shape((n, tok, both), BF16),
+            shape((n, slots_n, width), BF16),
+        ],
+        scratch_shapes=[
+            pltpu.VMEM((n, tok, own), BF16),
+            pltpu.VMEM((n, tok, own), BF16),
+            pltpu.VMEM((2, tok, wide), F32),
+            pltpu.VMEM((2, tok, wide), F32),
+            pltpu.VMEM((length, own), BF16),
+            pltpu.VMEM((length, own), BF16),
+            pltpu.VMEM((length, own), BF16),
+            pltpu.VMEM((length, 128), F32),
+            pltpu.VMEM((length, 128), F32),
+            pltpu.VMEM((8, wide), F32),
+            pltpu.VMEM((tok, width), F32),
+            pltpu.VMEM((n, tok, width), BF16),
+            pltpu.VMEM((n, tok, width), BF16),
+            pltpu.VMEM((n, tok, width), BF16),
+            pltpu.VMEM((n, tok, width), BF16),
+            pltpu.VMEM((slots_n, width), BF16),
+            pltpu.VMEM((n, ne, 3, wrows, own), BF16),
+            pltpu.VMEM((ne, n, 3, wrows, own), BF16),
+            pltpu.VMEM((n, 3, wrows, own), BF16),
+            pltpu.VMEM((n, 3, wrows, own), BF16),
+            pltpu.VMEM((n, ne, wrows, width), BF16),
+            pltpu.VMEM((ne, n, wrows, width), BF16),
+            pltpu.VMEM((n, wrows, width), BF16),
+            pltpu.VMEM((n, wrows, width), BF16),
+            pltpu.VMEM((24, 128), F32),
+            pltpu.VMEM((ne, 24, 128), F32),
+            pltpu.VMEM((24, 128), F32),
+            sem((n, ne)), sem((n, ne)), sem((n,)), sem((n,)), sem((n,)), sem((n,)), sem((n,)), sem((n,)),
+            sem((n,)), sem((n,)), sem((ne,)), sem((ne,)), sem((ne,)), sem((ne,)), sem((n,)), sem((n,)),
+            sem((n,)), sem((n,)), sem((ne,)), sem((ne,)), sem((n,)), sem((n,)), sem((2,)),
+        ],
+        compiler_params=pltpu.CompilerParams(
+            collective_id=4, has_side_effects=True, vmem_limit_bytes=60 * 1024 * 1024
+        ),
+        name="backward",
+    )(
+        d_two, resid, cot, x, gain_one, gain_two, mixed, wo, qkv, lse, normed, vectors, wq, wk, wv, meta_all,
+        in_bucket, gwgu, out_rows,
+    )
 
 
 def local(
@@ -874,87 +1080,29 @@
         n, experts_n, cap_pad, deep, slots, d_outs, wgu, wd, meta_all
     )
 
-    dest = meta_all[:, :2].astype(jnp.int32)
-    select = (dest[..., None] == jnp.arange(slots_n, dtype=jnp.int32)).astype(BF16)
-    both = select[:, 0] + select[:, 1]
-    first_gate = meta_all[:, 2]
-    gates = jnp.stack([first_gate, 1.0 - first_gate], axis=1)
-
-    def from_experts(rows):
-        rows = jnp.swapaxes(rows.reshape(n, experts_n, cap_pad, width), 0, 1)
-        return jnp.swapaxes(exchange(rows), 0, 1).reshape(n, slots_n, width)
-
-    got = trade(gwgu.reshape(n, width // n, gwgu.shape[1]), n, dp)
-    gain_one, gain_two = gain_one[0], gain_two[0]
-    grad_top = cotangent[0].astype(F32)
-    inverse_two = lax.rsqrt(jnp.mean(resid * resid, axis=-1, keepdims=True) + EPSILON)
-    grad_gain_two, grad_resid_norm = norm_backward(resid, inverse_two, gain_two, grad_normed_two)
-    grad_resid = grad_top + grad_resid_norm
-    grad_attn_low = grad_resid.astype(BF16)
-    d_mixed = mm(grad_attn_low, wo, NT).astype(BF16)
-    d_mixed_heads = trade(jnp.swapaxes(d_mixed.reshape(tok, n, own), 0, 1), n, dp).reshape(length, own)
-    grad_w_out_part = mm(mixed, grad_attn_low, TN)
-
-    out_back = from_experts(out_rows)
-    out_back, d_mixed_heads = lax.optimization_barrier((out_back, d_mixed_heads))
-    picked = jnp.einsum("gcts,gsd->gctd", select, out_back, preferred_element_type=F32)
-    moe_sum = to_owners(jnp.sum(picked * gates[..., None], axis=1), n, dp)
-
-    dq, dk, dv, diagonals = attention_backward(n, qkv, lse, d_mixed_heads, vectors)
-    d_normed_part = mm(dq, wq, NT) + mm(dk, wk, NT) + mm(dv, wv, NT)
-    d_normed_part, moe_sum = lax.optimization_barrier((d_normed_part, moe_sum))
-    grad_normed = to_owners(d_normed_part.reshape(n, tok, width), n, dp)
-    d_qkv = jnp.concatenate([dq, dk, dv], axis=1)
-    grad_wqkv_part = mm(normed, d_qkv, TN)
-    tokens = inputs[0].astype(F32)
-    inverse_one = lax.rsqrt(jnp.mean(tokens * tokens, axis=-1, keepdims=True) + EPSILON)
-    grad_gain_one, grad_tok_norm = norm_backward(tokens, inverse_one, gain_one, grad_normed)
-    grad_inputs = (grad_resid + grad_tok_norm).astype(BF16)
-    block_out = (resid + moe_sum).astype(BF16)
-
+    by_diagonal = jnp.pad(jnp.roll(in_bucket, -tok, axis=0), ((0, 0), (0, 128 - BUCKETS)))
+    block_out, grad_inputs, gq, gk, gv, go, small, got, _ = backward(
+        n, experts_n, cap_pad, wrows, grad_normed_two, resid, cotangent[0], inputs[0], gain_one, gain_two, mixed, wo,
+        qkv, lse, normed, vectors, wq, wk, wv, meta_all, by_diagonal, gwgu.reshape(n, width // n, -1), out_rows,
+    )
     grad_w_gate, grad_w_up = unpack_columns(got)
 
-    def plane_sum(parts):
-        return jnp.sum(exchange(parts.astype(BF16)).astype(F32), axis=0)
-
-    go = grad_w_out_part.reshape(n, experts_n, wrows, width)
-    go = plane_sum(jnp.swapaxes(go, 0, 1))
-    grad_w_out = to_owners(go, n, dp)
-
-    gq = grad_wqkv_part.reshape(n, experts_n, wrows, 3 * own)
-    gq = plane_sum(jnp.swapaxes(gq, 0, 1)).astype(BF16)
-    gq_all = trade(gq, n, dp).astype(F32)
-    gq_all = gq_all.reshape(n, wrows, 3, own).transpose(2, 1, 0, 3).reshape(3, wrows, width)
-
-    diag_rows = jnp.roll(diagonals.reshape(heads_own, wide), tok, axis=1)
-    grad_table = lax.dot_general(
-        in_bucket.astype(F32), diag_rows, (((0,), (1,)), ((), ())), precision=lax.Precision.HIGHEST,
-        preferred_element_type=F32,
-    )
-    grad_table = lax.dynamic_update_slice_in_dim(
-        jnp.zeros((BUCKETS, HEADS), F32), grad_table, dp * heads_own, 1
-    )
-    small = jnp.concatenate([grad_gain_one, grad_gain_two, grad_table.reshape(-1)]).reshape(-1, 128)
-    step = 1
-    while step < experts_n:
-        small = small + lax.ppermute(small, "expert", [(i, i ^ step) for i in range(experts_n)])
-        step *= 2
-    small = (small + sum(shift(small, d, n) for d in range(1, n))).reshape(-1)
     me = dp * experts_n + ex
-    grad_gain_attn = lax.dynamic_slice_in_dim(small, me * n_gain, n_gain)
-    grad_gain_moe = lax.dynamic_slice_in_dim(small, width + me * n_gain, n_gain)
-    grad_bias = lax.dynamic_slice_in_dim(small, 2 * width + me * n_bias, n_bias)
+    gains = jnp.sum(small[:, :16], axis=0).reshape(2, width)
+    mine = lax.dynamic_slice_in_dim(gains, me * n_gain, n_gain, 1)
+    grad_table = small[:, 16 : 16 + heads_own, :BUCKETS].reshape(HEADS, BUCKETS).T.reshape(-1)
+    grad_bias = lax.dynamic_slice_in_dim(grad_table, me * n_bias, n_bias)
 
     return (
         block_out[None],
         grad_inputs[None],
-        grad_gain_attn,
-        gq_all[0],
-        gq_all[1],
-        gq_all[2],
-        grad_w_out,
+        mine[0],
+        gq,
+        gk,
+        gv,
+        go,
         grad_bias,
-        grad_gain_moe,
+        mine[1],
         grad_w_gate[None],
         grad_w_up[None],
         grad_w_down[None],

time: 661 us -> 572 us (0.87)
  Pallas kernels: 368 us -> 539 us
  waiting for transfers between devices: 128 us -> 0 us
  starting transfers between devices: 71.5 us -> 0 us
  other arithmetic: 29.4 us -> 2.97 us
  local copies, waits for them, and re-layouts: 38.7 us -> 19.7 us
  matrix products: 14.6 us -> 0.89 us
    pallas_call x1, Pallas kernels: 23.6 us -> 195 us  [backward(): pl.pallas_call(functools.partial(backward_kernel, n, ne, cap_pad), in_spe...]
    ppermute x24 -> x0, waiting for transfers between devices: 107 us -> none  [the longest x21 88.4 us: shift(): lax.ppermute(value, 'dp', [(i, (i + distance) % n) for i in range(n)])]
    ppermute x24 -> x0, starting transfers between devices: 57.8 us -> none  [the longest x21 54.3 us: shift(): lax.ppermute(value, 'dp', [(i, (i + distance) % n) for i in range(n)])]
    all_to_all x3 -> x0, waiting for transfers between devices: 21.3 us -> none  [exchange(): lax.all_to_all(value, 'expert', split_axis=0, concat_axis=0, tiled=True)]
    all_to_all x3 -> x0, starting transfers between devices: 13.8 us -> none  [exchange(): lax.all_to_all(value, 'expert', split_axis=0, concat_axis=0, tiled=True)]
    reduce_sum x6 -> x1, other arithmetic: 10.1 us -> 0.76 us  [local(): gains = jnp.sum(small[:, :16], axis=0).reshape(2, width)]
    dot_general x7 -> x1, matrix products: 9.2 us -> 0.89 us  [mm(): return lax.dot_general(a, b, dims, preferred_element_type=F32)]
    another operation x7 -> x1, other arithmetic: 7.74 us -> 0.76 us  [the longest x3 2.83 us: trade(): jnp.stack([pick(blocks, dp)] + [shift(pick(blocks, lax.rem(dp + d, n)), d...]
  transfers between devices with their start and end apart: 27 -> 0, of which waited for: 13 -> 0; matrix products, arithmetic and copies ran while one was open for 9% -> 0% of each run, Pallas kernels for 4% -> 0%
where the time goes in v4:
time: 572 us; the launch traced here: 564 us
  Pallas kernels  539 us (94%)
  local copies, waits for them, and re-layouts  19.7 us (3%)
    pallas_call x1, Pallas kernels, forward(): pl.pallas_call(functools.partial(forward_kernel, n, ne, cap_pad), in_spec...  204 us
    pallas_call x1, Pallas kernels, backward(): pl.pallas_call(functools.partial(backward_kernel, n, ne, cap_pad), in_spe...  195 us
    pallas_call x1, Pallas kernels, experts(): pl.pallas_call(functools.partial(experts_kernel, n, ne, cap_pad, deep, ma...  76.9 us
    pallas_call x1, Pallas kernels, start(): pl.pallas_call(functools.partial(start_kernel, n, ne, cap, cap_pad, piece...  58.7 us

profile of v4, /device:TPU:0, one launch (start us, length us, event | category | flops | bytes accessed | tf_op | source)
XLA Modules:
  0.0 563.7 jit_solution(6160521006568727528)
XLA Ops:
  0.6 0.8 maximum_bitcast_fusion
  2.0 1.3 pad_add_fusion.meta_in
  3.3 58.7 %start.1 = (bf16[4,256,1024]{2,1,0:T(8,128)(2,1)}, bf16[4,8,32,256]{3,2,1,0:T(8,128)(2,1)}, bf16[4,8,32,256]{3,2,1,0:T(8,128)(2,1)}, bf16[4,8,32,256]{3,2,1,0:T(...) custom-call(bf16[256,1024]{1,0:T(8,128)(2,1)} %bitcast.41, ...), custom_call_target="tpu_custom_call" | custom-call | tf_op jit(solution)/shard_map/start/pallas_call | solution.py:325
  62.0 0.9 slice.48
  63.0 0.9 fusion.2.vectors
  64.0 0.7 reshape.168.gain_one
  64.7 0.7 reshape.169.gain_two
  65.3 203.8 %forward.1 = (bf16[1024,1024]{1,0:T(8,128)(2,1)}, bf16[1024,768]{1,0:T(8,128)(2,1)}, f32[1024,256]{1,0:T(8,128)}, bf16[256,1024]{1,0:T(8,128)(2,1)}, f32[256,102...) custom-call(bf16[4,256,1024]{2,1,0:T(8,128)(2,1)} %get-tuple-element, ...), custom_call_target="tpu_custom_call" | custom-call | tf_op jit(solution)/shard_map/forward/pallas_call | solution.py:517
  269.1 1.3 pad.13.wd_ref
  270.4 76.9 %experts.1 = (bf16[4,640,1024]{2,1,0:T(8,128)(2,1)}, f32[256,1024]{1,0:T(8,128)}, bf16[1024,1408]{1,0:T(8,128)(2,1)}, f32[704,1024]{1,0:T(8,128)}) custom-call(bf16[4,640,1024]{2,1,0:T(8,128)(2,1)} %bitcast.36, bf16[4,640,1024]{2,1,0:T(8,128)(2,1)} %bitcast.37, bf16[1024,1408]{1,0:T(8,128)(2,1)} %bitcast.39, bf16[768,1024]{1,0:T(8,128)(2,1)} %pad.13.wd_ref, ...), custom_call_target="tpu_custom_call" | custom-call | tf_op jit(solution)/shard_map/experts/pallas_call | solution.py:675
  347.7 0.9 pad.14.in_bucket
  348.6 194.6 %backward.1 = (bf16[256,1024]{1,0:T(8,128)(2,1)}, bf16[256,1024]{1,0:T(8,128)(2,1)}, f32[32,1024]{1,0:T(8,128)}, f32[32,1024]{1,0:T(8,128)}, f32[32,1024]{1,0:T(...) custom-call(f32[256,1024]{1,0:T(8,128)} %get-tuple-element.65.d_two,, ...), custom_call_target="tpu_custom_call" | custom-call | tf_op jit(solution)/shard_map/backward/pallas_call | solution.py:977
  543.2 5.1 unpack_columns.1
  548.3 1.3 slice.56
  549.6 0.8 copy.28
  550.4 0.7 reshape.167
  551.1 1.3 dynamic_slice.11
  552.3 0.8 slice_reduce_fusion
  553.7 1.9 copy.39
  555.6 0.8 copy.40
  556.4 1.6 copy.41
  557.9 1.6 copy.42
  559.5 1.6 copy.43
  561.7 1.6 copy.45
  (23 shorter events, 2.4 us)
Async XLA Ops:
  65.3 203.8 %copy-start.1 = (bf16[1,704,1024]{2,1,0:T(8,128)(2,1)S(1)}, bf16[1,704,1024]{2,1,0:T(8,128)(2,1)}, u32[]{:S(2)}) copy-start(bf16[1,704,1024]{2,1,0:T(8,128)(2,1)} %param.27) | copy-start | bytes 4325380
  543.2 12.4 %copy-start.2 = (bf16[256,1024]{1,0:T(8,128)(2,1)S(1)}, bf16[256,1024]{1,0:T(8,128)(2,1)}, u32[]{:S(2)}) copy-start(bf16[256,1024]{1,0:T(8,128)(2,1)} %get-tuple-element.74) | copy-start | bytes 1572868
  543.2 17.9 %copy-start.3 = (f32[32,1024]{1,0:T(8,128)S(1)}, f32[32,1024]{1,0:T(8,128)}, u32[]{:S(2)}) copy-start(f32[32,1024]{1,0:T(8,128)} %get-tuple-element.106) | copy-start | bytes 393220
  543.2 18.5 %copy-start = (f32[704,1024]{1,0:T(8,128)S(1)}, f32[704,1024]{1,0:T(8,128)}, u32[]{:S(2)}) copy-start(f32[704,1024]{1,0:T(8,128)} %get-tuple-element.83) | copy-start | bytes 8650756

commit v5 on v4

--- a/solution.py
+++ b/solution.py
@@ -71,35 +71,6 @@
     half = 0.5 * (1.0 + t)
     slope = half + (0.5 * GELU_C) * v * (1.0 - t * t) * (1.0 + (3.0 * GELU_A) * square)
     return v * half, slope
-
-
-def unpack_kernel(n, piece, in_ref, gate_ref, up_ref):
-    main = piece // 128 * 128
-    rest = piece - main
-    gates, ups = [], []
-    for j in range(n):
-        block = in_ref[j].astype(F32)
-        gates += [block[:, :main], block[:, 2 * main : 2 * main + rest]]
-        ups += [block[:, main : 2 * main], block[:, 2 * main + rest :]]
-    gate_ref[...] = jnp.concatenate(gates, axis=1)
-    up_ref[...] = jnp.concatenate(ups, axis=1)
-
-
-def unpack_columns(blocks):
-    n, rows, both = blocks.shape
-    piece = both // 2
-    step = min(rows, 64)
-    total = n * piece
-    return pl.pallas_call(
-        functools.partial(unpack_kernel, n, piece),
-        grid=(rows // step,),
-        in_specs=[pl.BlockSpec((n, step, both), lambda i: (0, i, 0))],
-        out_specs=[pl.BlockSpec((step, total), lambda i: (i, 0))] * 2,
-        out_shape=[jax.ShapeDtypeStruct((rows, total), F32)] * 2,
-        compiler_params=pltpu.CompilerParams(vmem_limit_bytes=VMEM_LIMIT),
-        cost_estimate=pl.CostEstimate(flops=0, bytes_accessed=12 * rows * total, transcendentals=0),
-        name="unpack_columns",
-    )(blocks)
 
 
 MESH = pl.DeviceIdType.MESH
@@ -414,6 +385,11 @@
             to_plane(rows, land, send, recv, group, k).start()
         kept(rows, land, group, send).start()
 
+    def send_cot(group, tokens):
+        dispatch(group, tokens, cot_rows, d_outs, pc_send, pc_recv, True)
+
+    send_cot(dp, cot[...])
+
     @pl.loop(0, n)
     def _(j):
         at = pl.ds(pl.multiple_of(j * block, block), block)
@@ -455,10 +431,15 @@
             def _():
                 then(chain.arrive(h, side))
 
+    def cot_hop(h):
+        hop(cots, h, lambda group: send_cot(group, cot_all[group]))
+
+    cot_hop(0)
+    for d in range(1, n):
+        weights(d).start()
     attend(0)
-    hop(cots, 0, lambda at: None)
-    for d in range(1, n):
-        weights(d).start()
+    if n > 2:
+        cot_hop(1)
     for pair in range(1, pairs_n):
         attend(pair)
 
@@ -472,10 +453,8 @@
     for d in range(1, n):
         give(d).start()
     mixed_in[dp] = heads[pl.ds(pl.multiple_of(dp * block, block), block), :]
-    dispatch(dp, cot[...], cot_rows, d_outs, pc_send, pc_recv, True)
-    for h in range(1, n - 1):
-        hop(cots, h, lambda at: None)
-    cots.finish()
+    for h in range(2, n - 1):
+        cot_hop(h)
     for d in range(1, n):
         give(d).wait()
     mixed[...] = jnp.concatenate([mixed_in[j] for j in range(n)], axis=1)
@@ -489,10 +468,9 @@
         dispatch(group, tokens, two_rows, slots, pt_send, pt_recv, False)
 
     send_two(dp, two_own[...])
-    for j in range(1, n):
-        at = lax.rem(dp + j, n)
-        dispatch(at, cot_all[at], cot_rows, d_outs, pc_send, pc_recv, True)
-        hop(twos, j - 1, lambda group: send_two(group, two_all[group]))
+    for h in range(n - 1):
+        hop(twos, h, lambda group: send_two(group, two_all[group]))
+    cots.finish()
     twos.finish()
     keep_w.wait()
     for d in range(1, n):
@@ -702,7 +680,7 @@
     n, ne, cap_pad,
     d_two, resid, cot, x, gain_one, gain_two, mixed, wo, qkv, lse, normed, vectors, wq, wk, wv, meta_all, in_bucket,
     gwgu, out_rows,
-    block_out, grad_in, gq, gk, gv, go, small_all, gw_in, out_in,
+    block_out, grad_in, g_all, small_all, gw_in, out_in,
     dm, dm_in, tiles, sums, dq_s, dk_s, dv_s, dk_acc, dv_acc, diag, d_res,
     dn_part, dn_land, moe_part, moe_land, out_one,
     g_send, g_land, g2_send, g2_land, o_send, o_land, o2_send, o2_land,
@@ -715,7 +693,7 @@
     own = dq_s.shape[1]
     pairs_n = own // 128
     slots_n = ne * cap_pad
-    wrows = go.shape[0]
+    wrows = g_all.shape[1]
     greet(n, ne, dp, ex)
     toward = 2 * ((2 * dp) // n) - 1
 
@@ -837,17 +815,73 @@
         at = pl.ds(pl.multiple_of(t * tok, tok), tok)
         return mm(dq_s[at, :], wq[...], NT) + mm(dk_s[at, :], wk[...], NT) + mm(dv_s[at, :], wv[...], NT)
 
-    @pl.loop(0, n - 1)
-    def _(step):
-        t = group_at(step)
-        dn_part[t] = d_norm(t).astype(BF16)
-        to_line(dn_part, dn_land, dn_s, dn_r, t).start()
+    def sum_copy(part, land, send, recv, r, side):
+        t = lax.rem(dp + n + (n - r) * (1 - 2 * side), n)
+        target = lax.rem(dp + n + 1 - 2 * side, n)
+        return t, remote(part.at[t], land.at[r - 1, side], send.at[r - 1, side], recv.at[r - 1, side], (target, ex))
+
+    def takes_part(r, side):
+        return ((side == 0) & (dp < r) & (dp + 1 < n)) | ((side == 1) & (dp + r >= n) & (dp > 0))
+
+    def is_fed(r, side):
+        return ((side == 0) & (dp > 0) & (r > 1)) | ((side == 1) & (dp + 1 < n) & (r > 1))
+
+    def fed(part, land, send, recv, r, side):
+        remote(
+            part.at[dp], land.at[r - 1, side], send.at[r - 1, side], recv.at[r - 1, side], (dp, ex)
+        ).wait_recv()
+
+    def sum_round(part, land, send, recv, term, r):
+        @pl.loop(0, 2)
+        def _(side):
+            @pl.when(takes_part(r, side))
+            def _():
+                t, copy = sum_copy(part, land, send, recv, r, side)
+                mine = term(t)
+
+                @pl.when(is_fed(r, side))
+                def _():
+                    fed(part, land, send, recv, r - 1, side)
+                    part[t] = (mine + land[max(r - 2, 0), side].astype(F32)).astype(BF16)
+
+                @pl.when(jnp.logical_not(is_fed(r, side)))
+                def _():
+                    part[t] = mine.astype(BF16)
+
+                copy.start()
+
+    def sum_end(part, land, send, recv, mine):
+        @pl.when(dp > 0)
+        def _():
+            fed(part, land, send, recv, n - 1, 0)
+
+        @pl.when(dp + 1 < n)
+        def _():
+            fed(part, land, send, recv, n - 1, 1)
+
+        left = jnp.where(dp > 0, land[n - 2, 0].astype(F32), 0.0)
+        right = jnp.where(dp + 1 < n, land[n - 2, 1].astype(F32), 0.0)
+        return mine + left + right
+
+    def sum_sent(part, land, send, recv):
+        for r in range(1, n):
+            for side in range(2):
+                @pl.when(takes_part(r, side))
+                def _():
+                    sum_copy(part, land, send, recv, r, side)[1].wait_send()
+
+    dn = (dn_part, dn_land, dn_s, dn_r)
+    moes = (moe_part, moe_land, moe_s, moe_r)
+    sum_round(*dn, d_norm, 1)
 
     for w, ref in enumerate((dq_s, dk_s, dv_s)):
         g_send[:, :, w] = mm(normed[...], ref[...], TN).reshape(n, ne, wrows, own).astype(BF16)
     for k in range(1, ne):
         to_plane(g_send.at[:, lax.rem(ex + k, ne)], g_land, g_s, g_r, k).start()
     g_land[ex] = g_send[:, ex]
+
+    for r in range(2, n):
+        sum_round(*dn, d_norm, r)
 
     rest = diag[...]
     table = jnp.zeros((8, 128), F32)
@@ -880,11 +914,8 @@
         load.wait()
         return mm(weight.astype(BF16), out_one[...], TN)
 
-    @pl.loop(0, n - 1)
-    def _(step):
-        t = group_at(step)
-        moe_part[t] = moe(t).astype(BF16)
-        to_line(moe_part, moe_land, moe_s, moe_r, t).start()
+    for r in range(1, n):
+        sum_round(*moes, moe, r)
 
     for k in range(1, ne):
         from_plane(g_send.at[:, ex], g_land, g_s, g_r, k).wait_recv()
@@ -896,11 +927,7 @@
         to_line(g2_send, g2_land, g2_s, g2_r, lax.rem(dp + d, n)).start()
     g2_land[dp] = g2_send[dp]
 
-    total = d_norm(dp)
-    for d in range(1, n):
-        t = lax.rem(dp + d, n)
-        from_line(dn_part, dn_land, dn_s, dn_r, t).wait_recv()
-        total = total + dn_land[t].astype(F32)
+    total = sum_end(*dn, d_norm(dp))
     values = x[...].astype(F32)
     inverse = lax.rsqrt(jnp.mean(values * values, axis=-1, keepdims=True) + EPSILON)
     scaled = gain_one[...] * total
@@ -923,12 +950,7 @@
         remote(small_sum, small_all.at[dp], sz_s.at[t], sz_r.at[dp], (t, ex)).start()
     small_all[dp] = total
 
-    total = resid[...] + moe(dp)
-    for d in range(1, n):
-        t = lax.rem(dp + d, n)
-        from_line(moe_part, moe_land, moe_s, moe_r, t).wait_recv()
-        total = total + moe_land[t].astype(F32)
-    block_out[...] = total.astype(BF16)
+    block_out[...] = sum_end(*moes, resid[...] + moe(dp)).astype(BF16)
 
     for d in range(1, n):
         t = lax.rem(dp + d, n)
@@ -938,19 +960,21 @@
     total = o2_land[0].astype(F32)
     for j in range(1, n):
         total = total + o2_land[j].astype(F32)
-    go[...] = total
-    for w, ref in enumerate((gq, gk, gv)):
-        ref[...] = jnp.concatenate([g2_land[j, w] for j in range(n)], axis=1).astype(F32)
+    g_all[3] = total
+    for w in range(3):
+        g_all[w] = jnp.concatenate([g2_land[j, w] for j in range(n)], axis=1).astype(F32)
     for d in range(1, n):
         t = lax.rem(dp + d, n)
         from_line(gwgu, gw_in, w_s, w_r, t).wait_recv()
         for src, dst, send, recv in (
-            (gwgu, gw_in, w_s, w_r), (dm, dm_in, dm_s, dm_r), (dn_part, dn_land, dn_s, dn_r),
-            (moe_part, moe_land, moe_s, moe_r), (o2_send, o2_land, o2_s, o2_r), (g2_send, g2_land, g2_s, g2_r),
+            (gwgu, gw_in, w_s, w_r), (dm, dm_in, dm_s, dm_r),
+            (o2_send, o2_land, o2_s, o2_r), (g2_send, g2_land, g2_s, g2_r),
         ):
             to_line(src, dst, send, recv, t).wait_send()
         remote(small_sum, small_all.at[dp], sz_s.at[t], sz_r.at[dp], (t, ex)).wait_send()
     keep_w.wait()
+    sum_sent(*dn)
+    sum_sent(*moes)
     for k in range(1, ne):
         to_plane(o_send.at[:, ex], o_land, o_s, o_r, k).wait_send()
         to_plane(g_send.at[:, ex], g_land, g_s, g_r, k).wait_send()
@@ -977,14 +1001,11 @@
     return pl.pallas_call(
         functools.partial(backward_kernel, n, ne, cap_pad),
         in_specs=[VM] * 17 + [ANY] * 2,
-        out_specs=[VM] * 7 + [ANY] * 2,
+        out_specs=[VM] * 4 + [ANY] * 2,
         out_shape=[
             shape((tok, width), BF16),
             shape((tok, width), BF16),
-            shape((wrows, width), F32),
-            shape((wrows, width), F32),
-            shape((wrows, width), F32),
-            shape((wrows, width), F32),
+            shape((4, wrows, width), F32),
             shape((n, 24, 128), F32),
             shape((n, tok, both), BF16),
             shape((n, slots_n, width), BF16),
@@ -1002,9 +1023,9 @@
             pltpu.VMEM((8, wide), F32),
             pltpu.VMEM((tok, width), F32),
             pltpu.VMEM((n, tok, width), BF16),
+            pltpu.VMEM((n - 1, 2, tok, width), BF16),
             pltpu.VMEM((n, tok, width), BF16),
-            pltpu.VMEM((n, tok, width), BF16),
-            pltpu.VMEM((n, tok, width), BF16),
+            pltpu.VMEM((n - 1, 2, tok, width), BF16),
             pltpu.VMEM((slots_n, width), BF16),
             pltpu.VMEM((n, ne, 3, wrows, own), BF16),
             pltpu.VMEM((ne, n, 3, wrows, own), BF16),
@@ -1017,8 +1038,8 @@
             pltpu.VMEM((24, 128), F32),
             pltpu.VMEM((ne, 24, 128), F32),
             pltpu.VMEM((24, 128), F32),
-            sem((n, ne)), sem((n, ne)), sem((n,)), sem((n,)), sem((n,)), sem((n,)), sem((n,)), sem((n,)),
-            sem((n,)), sem((n,)), sem((ne,)), sem((ne,)), sem((ne,)), sem((ne,)), sem((n,)), sem((n,)),
+            sem((n, ne)), sem((n, ne)), sem((n,)), sem((n,)), sem((n,)), sem((n,)), sem((n, 2)), sem((n, 2)),
+            sem((n, 2)), sem((n, 2)), sem((ne,)), sem((ne,)), sem((ne,)), sem((ne,)), sem((n,)), sem((n,)),
             sem((n,)), sem((n,)), sem((ne,)), sem((ne,)), sem((n,)), sem((n,)), sem((2,)),
         ],
         compiler_params=pltpu.CompilerParams(
@@ -1029,6 +1050,98 @@
         d_two, resid, cot, x, gain_one, gain_two, mixed, wo, qkv, lse, normed, vectors, wq, wk, wv, meta_all,
         in_bucket, gwgu, out_rows,
     )
+
+
+def split_pieces(value):
+    pieces = []
+    for _ in range(3):
+        piece = value.astype(BF16)
+        pieces.append(piece)
+        value = value - piece.astype(F32)
+    return pieces
+
+
+def finish_kernel(
+    n, ne, heads_own, piece, blocks, g_all, small, out_in, grad_in, gwd_in,
+    gate_ref, up_ref, gq, gk, gv, go, gain_one, gain_two, bias, block_out, grad_out, gwd,
+):
+    main = piece // 128 * 128
+    rest = piece - main
+    gates, ups = [], []
+    for j in range(n):
+        block = blocks[j].astype(F32)
+        gates += [block[:, :main], block[:, 2 * main : 2 * main + rest]]
+        ups += [block[:, main : 2 * main], block[:, 2 * main + rest :]]
+    gate_ref[...] = jnp.concatenate(gates, axis=1)
+    up_ref[...] = jnp.concatenate(ups, axis=1)
+    block_out[...] = out_in[...]
+    grad_out[...] = grad_in[...]
+    gwd[...] = gwd_in[...]
+
+    @pl.when(pl.program_id(0) == 0)
+    def _():
+        for i, ref in enumerate((gq, gk, gv, go)):
+            ref[...] = g_all[i]
+        me = lax.axis_index("dp") * ne + lax.axis_index("expert")
+        total = small[0, :16]
+        for j in range(1, n):
+            total = total + small[j, :16]
+        rows = lax.broadcasted_iota(jnp.int32, (8, 128), 0)
+        lanes = lax.broadcasted_iota(jnp.int32, (8, 128), 1)
+        for i, ref in enumerate((gain_one, gain_two)):
+            count = ref.shape[1]
+            at = me * count
+            row = jnp.sum(jnp.where(rows == at // 128, total[8 * i : 8 * i + 8], 0.0), axis=0, keepdims=True)
+            row = jnp.broadcast_to(row, (8, 128))
+            ref[...] = pltpu.roll(row, lax.rem(128 - lax.rem(at, 128), 128), 1)[:1, :count]
+        table = jnp.concatenate([small[j, 16 : 16 + heads_own] for j in range(n)], axis=0)
+        heads = n * heads_own
+        count = bias.shape[1]
+        at = me * count
+        table = jnp.concatenate([table, jnp.zeros((128 - heads, 128), F32)], axis=0)
+        hot = jnp.where(lanes == at // heads, 1.0, 0.0).astype(BF16)
+        row = sum(mm(hot, part, NT) for part in split_pieces(table))
+        bias[...] = pltpu.roll(row, lax.rem(128 - lax.rem(at, heads), 128), 1)[:1, :count]
+
+
+def finish(n, ne, heads_own, n_gain, n_bias, blocks, g_all, small, block_out, grad_in, gwd):
+    tok, both = blocks.shape[1:]
+    wrows, width = g_all.shape[1:]
+    deep = gwd.shape[0]
+    piece = both // 2
+    steps = 4
+    step, part = tok // steps, deep // steps
+    total = n * piece
+    shape = jax.ShapeDtypeStruct
+    fixed2 = lambda i: (0, 0)
+    fixed3 = lambda i: (0, 0, 0)
+    move = lambda i: (i, 0)
+    return pl.pallas_call(
+        functools.partial(finish_kernel, n, ne, heads_own, piece),
+        grid=(steps,),
+        in_specs=[
+            pl.BlockSpec((n, step, both), lambda i: (0, i, 0)),
+            pl.BlockSpec((4, wrows, width), fixed3),
+            pl.BlockSpec(small.shape, fixed3),
+            pl.BlockSpec((step, width), move),
+            pl.BlockSpec((step, width), move),
+            pl.BlockSpec((part, width), move),
+        ],
+        out_specs=[pl.BlockSpec((step, total), move)] * 2
+        + [pl.BlockSpec((wrows, width), fixed2)] * 4
+        + [pl.BlockSpec((1, n_gain), fixed2)] * 2
+        + [pl.BlockSpec((1, n_bias), fixed2)]
+        + [pl.BlockSpec((step, width), move)] * 2
+        + [pl.BlockSpec((part, width), move)],
+        out_shape=[shape((tok, total), F32)] * 2
+        + [shape((wrows, width), F32)] * 4
+        + [shape((1, n_gain), F32)] * 2
+        + [shape((1, n_bias), F32)]
+        + [shape((tok, width), BF16)] * 2
+        + [shape((deep, width), F32)],
+        compiler_params=pltpu.CompilerParams(vmem_limit_bytes=VMEM_LIMIT),
+        name="finish",
+    )(blocks, g_all, small, block_out, grad_in, gwd)
 
 
 def local(
@@ -1081,28 +1194,25 @@
     )
 
     by_diagonal = jnp.pad(jnp.roll(in_bucket, -tok, axis=0), ((0, 0), (0, 128 - BUCKETS)))
-    block_out, grad_inputs, gq, gk, gv, go, small, got, _ = backward(
+    block_out, grad_inputs, g_all, small, got, _ = backward(
         n, experts_n, cap_pad, wrows, grad_normed_two, resid, cotangent[0], inputs[0], gain_one, gain_two, mixed, wo,
         qkv, lse, normed, vectors, wq, wk, wv, meta_all, by_diagonal, gwgu.reshape(n, width // n, -1), out_rows,
     )
-    grad_w_gate, grad_w_up = unpack_columns(got)
-
-    me = dp * experts_n + ex
-    gains = jnp.sum(small[:, :16], axis=0).reshape(2, width)
-    mine = lax.dynamic_slice_in_dim(gains, me * n_gain, n_gain, 1)
-    grad_table = small[:, 16 : 16 + heads_own, :BUCKETS].reshape(HEADS, BUCKETS).T.reshape(-1)
-    grad_bias = lax.dynamic_slice_in_dim(grad_table, me * n_bias, n_bias)
+    (
+        grad_w_gate, grad_w_up, gq, gk, gv, go, grad_gain_one, grad_gain_two, grad_bias, block_out, grad_inputs,
+        grad_w_down,
+    ) = finish(n, experts_n, heads_own, n_gain, n_bias, got, g_all, small, block_out, grad_inputs, grad_w_down)
 
     return (
         block_out[None],
         grad_inputs[None],
-        mine[0],
+        grad_gain_one[0],
         gq,
         gk,
         gv,
         go,
-        grad_bias,
-        mine[1],
+        grad_bias[0],
+        grad_gain_two[0],
         grad_w_gate[None],
         grad_w_up[None],
         grad_w_down[None],

time: 572 us -> 482 us (0.84)
  Pallas kernels: 539 us -> 464 us
  local copies, waits for them, and re-layouts: 19.7 us -> 5.43 us
    pallas_call x1, Pallas kernels: 204 us -> 165 us  [forward(): pl.pallas_call(functools.partial(forward_kernel, n, ne, cap_pad), in_spec...]
    pallas_call x1, Pallas kernels: 195 us -> 156 us  [backward(): pl.pallas_call(functools.partial(backward_kernel, n, ne, cap_pad), in_spe...]
    unnamed x16 -> x3, local copies, waits for them, and re-layouts: 9.62 us -> 0.01 us
where the time goes in v5:
time: 482 us; the launch traced here: 474 us
  Pallas kernels  464 us (96%)
  local copies, waits for them, and re-layouts  5.43 us (1%)
    pallas_call x1, Pallas kernels, forward(): pl.pallas_call(functools.partial(forward_kernel, n, ne, cap_pad), in_spec...  165 us
    pallas_call x1, Pallas kernels, backward(): pl.pallas_call(functools.partial(backward_kernel, n, ne, cap_pad), in_spe...  156 us
    pallas_call x1, Pallas kernels, experts(): pl.pallas_call(functools.partial(experts_kernel, n, ne, cap_pad, deep, ma...  76.2 us
    pallas_call x1, Pallas kernels, start(): pl.pallas_call(functools.partial(start_kernel, n, ne, cap, cap_pad, piece...  58.6 us

profile of v5, /device:TPU:0, one launch (start us, length us, event | category | flops | bytes accessed | tf_op | source)
XLA Modules:
  0.0 473.6 jit_solution(5568381932388707198)
XLA Ops:
  0.6 0.8 maximum_bitcast_fusion
  1.4 0.6 scatter.4.extra
  2.0 1.3 pad_add_fusion.meta_in
  3.3 58.6 %start.1 = (bf16[4,256,1024]{2,1,0:T(8,128)(2,1)}, bf16[4,8,32,256]{3,2,1,0:T(8,128)(2,1)}, bf16[4,8,32,256]{3,2,1,0:T(8,128)(2,1)}, bf16[4,8,32,256]{3,2,1,0:T(...) custom-call(bf16[256,1024]{1,0:T(8,128)(2,1)} %bitcast.37, ...), custom_call_target="tpu_custom_call" | custom-call | tf_op jit(solution)/shard_map/start/pallas_call | solution.py:296
  62.0 0.9 slice.36
  62.9 0.1 slice_bitcast_fusion
  63.0 0.9 fusion.2.vectors
  63.9 0.1 slice_convert_fusion
  64.0 0.7 reshape.156.gain_one
  64.7 0.7 reshape.157.gain_two
  65.3 0.0 copy-start
  65.3 164.9 %forward.1 = (bf16[1024,1024]{1,0:T(8,128)(2,1)}, bf16[1024,768]{1,0:T(8,128)(2,1)}, f32[1024,256]{1,0:T(8,128)}, bf16[256,1024]{1,0:T(8,128)(2,1)}, f32[256,102...) custom-call(bf16[4,256,1024]{2,1,0:T(8,128)(2,1)} %get-tuple-element, ...), custom_call_target="tpu_custom_call" | custom-call | tf_op jit(solution)/shard_map/forward/pallas_call | solution.py:495
  230.2 0.0 copy-done
  230.2 1.3 pad.13.wd_ref
  231.5 76.2 %experts.1 = (bf16[4,640,1024]{2,1,0:T(8,128)(2,1)}, f32[256,1024]{1,0:T(8,128)}, bf16[1024,1408]{1,0:T(8,128)(2,1)}, f32[704,1024]{1,0:T(8,128)}) custom-call(bf16[4,640,1024]{2,1,0:T(8,128)(2,1)} %bitcast.33, bf16[4,640,1024]{2,1,0:T(8,128)(2,1)} %bitcast.34, bf16[1024,1408]{1,0:T(8,128)(2,1)} %bitcast.36, bf16[768,1024]{1,0:T(8,128)(2,1)} %pad.13.wd_ref, ...), custom_call_target="tpu_custom_call" | custom-call | tf_op jit(solution)/shard_map/experts/pallas_call | solution.py:653
  307.8 0.3 copy.26
  308.1 0.9 pad.14.in_bucket
  309.0 156.4 %backward.1 = (bf16[256,1024]{1,0:T(8,128)(2,1)}, bf16[256,1024]{1,0:T(8,128)(2,1)}, f32[4,32,1024]{2,1,0:T(8,128)}, f32[4,24,128]{2,1,0:T(8,128)}, bf16[4,256,1...) custom-call(f32[256,1024]{1,0:T(8,128)} %get-tuple-element.72.d_two, f32[256,1024]{1,0:T(8,128)} %get-tuple-element.73.resid, ...), custom_call_target="tpu_custom_call" | custom-call | tf_op jit(solution)/shard_map/backward/pallas_call | solution.py:1001
  465.4 7.7 %finish.1 = (f32[256,2816]{1,0:T(8,128)}, f32[256,2816]{1,0:T(8,128)}, f32[32,1024]{1,0:T(8,128)}, f32[32,1024]{1,0:T(8,128)}, f32[32,1024]{1,0:T(8,128)}, /*ind...) custom-call(bf16[4,256,1408]{2,1,0:T(8,128)(2,1)} %get-tuple-element, ...), custom_call_target="tpu_custom_call" | custom-call | tf_op jit(solution)/shard_map/finish/pallas_call | solution.py:1119
  (7 shorter events, 0.1 us)
Async XLA Ops:
  65.3 164.9 %copy-start = (bf16[1,704,1024]{2,1,0:T(8,128)(2,1)S(1)}, bf16[1,704,1024]{2,1,0:T(8,128)(2,1)}, u32[]{:S(2)}) copy-start(bf16[1,704,1024]{2,1,0:T(8,128)(2,1)} %param.27) | copy-start | bytes 4325380

commit v6 on v5

--- a/solution.py
+++ b/solution.py
@@ -88,7 +88,23 @@
         pl.semaphore_signal(barrier, inc=1, device_id=(lax.rem(dp + d, n), ex), device_id_type=MESH)
     for k in range(1, ne):
         pl.semaphore_signal(barrier, inc=1, device_id=(dp, lax.rem(ex + k, ne)), device_id_type=MESH)
-    pl.semaphore_wait(barrier, n + ne - 2)
+
+
+def meet(n, ne):
+    pl.semaphore_wait(pltpu.get_barrier_semaphore(), n + ne - 2)
+
+
+class Copies:
+    def __init__(self, sem, pairs):
+        self.copies = [pltpu.make_async_copy(src, dst, sem.at[i]) for i, (src, dst) in enumerate(pairs)]
+
+    def start(self, *which):
+        for i in which:
+            self.copies[i].start()
+
+    def wait(self, *which):
+        for i in which:
+            self.copies[i].wait()
 
 
 class Chain:
@@ -144,17 +160,65 @@
                     self.copy(hop, side, hop == 0).wait_send()
 
 
-def start_kernel(
+ANY = pl.BlockSpec(memory_space=pl.ANY)
+VM = pl.BlockSpec(memory_space=pltpu.VMEM)
+
+
+def bucket_hot(wide, turn, length):
+    at = lax.broadcasted_iota(jnp.int32, (wide, 128), 0) + turn
+    offset = jnp.where(at >= wide, at - wide, at) - length
+    hit = bucket_of(offset) == lax.broadcasted_iota(jnp.int32, (wide, 128), 1)
+    return jnp.where(hit & (jnp.abs(offset) < length), 1.0, 0.0).astype(BF16)
+
+
+def rows_flat(ref):
+    n, ne, rows, columns = ref.shape
+    if rows % 16 == 0:
+        return ref[...].reshape(n * ne * rows, columns)
+    return ref[...].astype(F32).reshape(n * ne * rows, columns).astype(BF16)
+
+
+def front_kernel(
     n, ne, cap, cap_pad, piece,
-    x, wq, wk, wv, extra, wo, meta_in, wg, wu,
-    x_all, lq, lk, lv, lext, lwo, meta_all, packed,
-    sq, sk, sv, sext, swo, smeta,
+    x_in, wq, wk, wv, wo, gain_attn, gain_moe, position_bias, meta_in, wg_in, wu_in, cot_in,
+    normed_out, qkv_out, lse_out, mixed_out, resid_out, lq_out, lk_out, lv_out, lwo_out, meta_all, vectors, gains,
+    slots, d_outs, wgu,
+    x, wg, wu, cot, normed, qkv, lse, mixed, resid, lq, lk, lv, lwo,
+    extra, sq, sk, sv, sext, swo, smeta, lext, packed,
+    x_all, heads, mixed_in, tiles, cot_all, two_all, two_own, two_rows, cot_rows,
     line_send, line_recv, plane_send, plane_recv, core_send, core_recv, chain_send, chain_recv, own_sem,
+    w_send, w_recv, m_send, m_recv, c_send, c_recv, t_send, t_recv,
+    pc_send, pc_recv, pt_send, pt_recv, in_sem, out_sem,
 ):
     dp, ex = lax.axis_index("dp"), lax.axis_index("expert")
+    greet(n, ne, dp, ex)
+    loads = Copies(in_sem, [(x_in, x), (cot_in, cot), (wg_in, wg), (wu_in, wu)])
+    loads.start(0, 1, 2, 3)
+    stores = Copies(
+        out_sem,
+        [
+            (normed, normed_out), (qkv, qkv_out), (lse, lse_out), (mixed, mixed_out), (resid, resid_out),
+            (lq, lq_out), (lk, lk_out), (lv, lv_out), (lwo, lwo_out),
+        ],
+    )
     own = sq.shape[2]
-    greet(n, ne, dp, ex)
+    block, width = cot.shape
+    pairs_n = own // 128
+    slots_n = ne * cap_pad
+    n_gain, n_bias = gain_attn.shape[1], position_bias.shape[1]
+    line_of = jnp.concatenate(
+        [
+            gain_attn[...].astype(F32), gain_moe[...].astype(F32), position_bias[...].astype(F32),
+            jnp.zeros((1, own - 2 * n_gain - n_bias), F32),
+        ],
+        axis=1,
+    )
+    extra[...] = jnp.broadcast_to(line_of, (16, own)).astype(BF16)
+    loads.wait(0)
+    meet(n, ne)
     chain = Chain(n, dp, ex, x, x_all, chain_send, chain_recv)
+    cots = Chain(n, dp, ex, cot, cot_all, c_send, c_recv)
+    twos = Chain(n, dp, ex, two_own, two_all, t_send, t_recv)
 
     def column(ref, t):
         return ref.at[:, pl.ds(pl.multiple_of(t * own, 128), own)]
@@ -173,13 +237,13 @@
     chain.start()
     for d in range(1, n):
         line(4, d).start()
-    keep = pltpu.make_async_copy(x, x_all.at[dp], own_sem.at[0])
-    keep.start()
-    sq[dp] = wq[:, pl.ds(pl.multiple_of(dp * own, 128), own)]
-    sk[dp] = wk[:, pl.ds(pl.multiple_of(dp * own, 128), own)]
-    sv[dp] = wv[:, pl.ds(pl.multiple_of(dp * own, 128), own)]
+    here = pl.ds(pl.multiple_of(dp * own, 128), own)
+    sq[dp] = wq[:, here]
+    sk[dp] = wk[:, here]
+    sv[dp] = wv[:, here]
     sext[dp] = extra[...]
     swo[dp] = wo[...]
+    x_all[dp] = x[...]
 
     tok = meta_in.shape[1]
     routes = meta_in[...]
@@ -192,15 +256,14 @@
     counts = mm((first + second).astype(BF16), before)
     slot_a = jnp.sum(counts * first, axis=0, keepdims=True)
     slot_b = jnp.sum((counts + first) * second, axis=0, keepdims=True)
-    wide = routes.astype(F32)
-    dest_a = jnp.where(slot_a < cap, wide[0:1, :] * cap_pad + slot_a, -1.0)
-    dest_b = jnp.where(slot_b < cap, wide[1:2, :] * cap_pad + slot_b, -1.0)
-    gate = wide[2:3, :] * (1.0 / 65536.0)
+    asked = routes.astype(F32)
+    dest_a = jnp.where(slot_a < cap, asked[0:1, :] * cap_pad + slot_a, -1.0)
+    dest_b = jnp.where(slot_b < cap, asked[1:2, :] * cap_pad + slot_b, -1.0)
+    gate = asked[2:3, :] * (1.0 / 65536.0)
     smeta[...] = jnp.concatenate([dest_a, dest_b, gate, jnp.zeros((5, tok), F32)], axis=0)
+    meta_all[dp] = smeta[...]
     for d in range(1, n):
         line(5, d).start()
-    keep_meta = pltpu.make_async_copy(smeta, meta_all.at[dp], own_sem.at[1])
-    keep_meta.start()
 
     pairs = [(sq, lq), (sk, lk), (sv, lv), (sext, lext), (swo, lwo)]
     partner = ex + 1 - 2 * lax.rem(ex, 2)
@@ -220,22 +283,89 @@
             core_send.at[kind, k], core_recv.at[kind, k], (dp, partner),
         )
 
+    def keep_own(kind):
+        return pltpu.make_async_copy(pairs[kind][0], pairs[kind][1].at[:, ex], own_sem.at[kind])
+
     def spread(kind):
         for d in range(1, n):
             line(kind, d).wait_recv()
         for k in range(1, ne // 2):
             plane(kind, k).start()
         core(kind, 0).start()
-        pltpu.make_async_copy(pairs[kind][0], pairs[kind][1].at[:, ex], own_sem.at[2 + kind]).start()
+        keep_own(kind).start()
+
+    def pass_on(kind):
+        for k in range(1, ne // 2):
+            plane(kind, k).wait_recv()
+            core(kind, k).start()
+
+    def settle(kind):
+        keep_own(kind).wait()
+        for k in range(ne // 2):
+            core(kind, k).wait()
+        for k in range(1, ne // 2):
+            plane(kind, k).wait_send()
 
     for kind in range(4):
         spread(kind)
 
+    def to_plane(rows, land, send, recv, group, k):
+        peer = lax.rem(ex + k, ne)
+        return remote(
+            rows.at[group, pl.ds(pl.multiple_of(peer * cap_pad, 16), cap_pad)], land.at[group, ex],
+            send.at[group, k], recv.at[group, k], (dp, peer),
+        )
+
+    def kept(rows, land, group, sem):
+        return pltpu.make_async_copy(
+            rows.at[group, pl.ds(pl.multiple_of(ex * cap_pad, 16), cap_pad)], land.at[group, ex], sem.at[group, 0]
+        )
+
+    def dispatch(group, tokens, rows, land, send, recv, weigh):
+        meta = meta_all[group]
+        slot_ids = lax.broadcasted_iota(jnp.int32, (slots_n, block), 0).astype(F32)
+        hit_a, hit_b = slot_ids == meta[0:1, :], slot_ids == meta[1:2, :]
+        chosen = jnp.where(hit_a | hit_b, 1.0, 0.0).astype(BF16)
+        found = mm(chosen, tokens)
+        if weigh:
+            share = meta[2:3, :]
+            factor = jnp.sum(
+                jnp.where(hit_a, share, 0.0) + jnp.where(hit_b, 1.0 - share, 0.0), axis=1, keepdims=True
+            )
+            found = found * factor
+        rows[group] = found.astype(BF16)
+        for k in range(1, ne):
+            to_plane(rows, land, send, recv, group, k).start()
+        kept(rows, land, group, send).start()
+
+    def send_cot(group, tokens):
+        dispatch(group, tokens, cot_rows, d_outs, pc_send, pc_recv, True)
+
+    def send_two(group, tokens):
+        dispatch(group, tokens, two_rows, slots, pt_send, pt_recv, False)
+
+    loads.wait(1)
+    send_cot(dp, cot[...])
+
+    def weights(d):
+        t = lax.rem(dp + d, n)
+        return remote(packed.at[t], wgu.at[dp], w_send.at[d], w_recv.at[d], (t, ex))
+
+    keep_w = pltpu.make_async_copy(packed.at[dp], wgu.at[dp], own_sem.at[5])
+
+    def hop(line_chain, h, then):
+        for side in range(2):
+            @pl.when(line_chain.held(h, side))
+            def _():
+                then(line_chain.arrive(h, side))
+
+    def x_hop(h):
+        hop(chain, h, lambda at: None)
+
     main = piece // 128 * 128
     step = min(wg.shape[0], 64)
 
-    @pl.loop(0, wg.shape[0] // step)
-    def _(i):
+    def pack(i):
         rows = pl.ds(pl.multiple_of(i * step, step), step)
         gate_w, up_w = wg[rows, :], wu[rows, :]
         for j in range(n):
@@ -243,162 +373,83 @@
             u = up_w[:, j * piece : (j + 1) * piece]
             packed[j, rows, :] = jnp.concatenate([g[:, :main], u[:, :main], g[:, main:], u[:, main:]], axis=1)
 
+    loads.wait(2, 3)
+    pl.loop(0, wg.shape[0] // step)(pack)
+    x_hop(0)
     spread(4)
-
-    def pass_on(kind):
-        for k in range(1, ne // 2):
-            plane(kind, k).wait_recv()
-            core(kind, k).start()
-
-    def hop(h):
-        for side in range(2):
-            @pl.when(chain.held(h, side))
-            def _():
-                chain.arrive(h, side)
-
-    hop(0)
     for kind in range(4):
         pass_on(kind)
-    for h in range(1, n - 1):
-        hop(h)
-        if h == 1:
-            pass_on(4)
-    if n < 3:
-        pass_on(4)
-    for kind in range(5):
-        for k in range(ne // 2):
-            core(kind, k).wait()
-        for k in range(1, ne // 2):
-            plane(kind, k).wait_send()
-        pltpu.make_async_copy(pairs[kind][0], pairs[kind][1].at[:, ex], own_sem.at[2 + kind]).wait()
-    for d in range(1, n):
-        for kind in range(6):
-            line(kind, d).wait_send()
-        line(5, d).wait_recv()
-    chain.finish()
-    keep.wait()
-    keep_meta.wait()
-
-
-def whole(array):
-    return pl.BlockSpec(memory_space=pltpu.VMEM)
-
-
-ANY = pl.BlockSpec(memory_space=pl.ANY)
-VM = pl.BlockSpec(memory_space=pltpu.VMEM)
-
-
-def start(n, ne, cap, cap_pad, x, wq, wk, wv, extra, wo, meta_in, wg, wu):
-    tok, width = x.shape
-    wrows = wq.shape[0]
-    own = width // n
-    piece = wg.shape[1] // n
-    return pl.pallas_call(
-        functools.partial(start_kernel, n, ne, cap, cap_pad, piece),
-        in_specs=[VM] * 9,
-        out_specs=[ANY] * 7 + [VM],
-        out_shape=[
-            jax.ShapeDtypeStruct((n, tok, width), BF16),
-            jax.ShapeDtypeStruct((n, ne, wrows, own), BF16),
-            jax.ShapeDtypeStruct((n, ne, wrows, own), BF16),
-            jax.ShapeDtypeStruct((n, ne, wrows, own), BF16),
-            jax.ShapeDtypeStruct((n, ne, 16, own), BF16),
-            jax.ShapeDtypeStruct((n, ne, wrows, width), BF16),
-            jax.ShapeDtypeStruct((n, 8, tok), F32),
-            jax.ShapeDtypeStruct((n, tok, 2 * piece), BF16),
-        ],
-        scratch_shapes=[
-            pltpu.VMEM((n, wrows, own), BF16),
-            pltpu.VMEM((n, wrows, own), BF16),
-            pltpu.VMEM((n, wrows, own), BF16),
-            pltpu.VMEM((n, 16, own), BF16),
-            pltpu.VMEM((n, wrows, width), BF16),
-            pltpu.VMEM((8, tok), F32),
-            pltpu.SemaphoreType.DMA((6, n)),
-            pltpu.SemaphoreType.DMA((6, n)),
-            pltpu.SemaphoreType.DMA((5, ne // 2)),
-            pltpu.SemaphoreType.DMA((5, ne // 2)),
-            pltpu.SemaphoreType.DMA((5, ne // 2)),
-            pltpu.SemaphoreType.DMA((5, ne // 2)),
-            pltpu.SemaphoreType.DMA((n, 2)),
-            pltpu.SemaphoreType.DMA((n, 2)),
-            pltpu.SemaphoreType.DMA((7,)),
-        ],
-        compiler_params=pltpu.CompilerParams(
-            collective_id=1, has_side_effects=True, vmem_limit_bytes=VMEM_LIMIT
-        ),
-        name="start",
-    )(x, wq, wk, wv, extra, wo, meta_in, wg, wu)
-
-
-def forward_kernel(
-    n, ne, cap_pad,
-    x_all, wq, wk, wv, wo, gain_one, gain_two, vectors, cot, meta_all, packed,
-    normed, qkv, lse, mixed, resid, slots, d_outs, wgu,
-    heads, mixed_in, tiles, cot_all, two_all, two_own, two_rows, cot_rows,
-    w_send, w_recv, m_send, m_recv, c_send, c_recv, t_send, t_recv,
-    pc_send, pc_recv, pt_send, pt_recv, own_sem,
-):
-    dp, ex = lax.axis_index("dp"), lax.axis_index("expert")
-    block, width = cot.shape
-    own = heads.shape[1]
-    pairs_n = own // 128
-    slots_n = ne * cap_pad
-    greet(n, ne, dp, ex)
-
-    def weights(d):
-        t = lax.rem(dp + d, n)
-        return remote(packed.at[t], wgu.at[dp], w_send.at[d], w_recv.at[d], (t, ex))
-
-    cots = Chain(n, dp, ex, cot, cot_all, c_send, c_recv)
-    twos = Chain(n, dp, ex, two_own, two_all, t_send, t_recv)
-    cots.start()
-    keep_w = pltpu.make_async_copy(packed.at[dp], wgu.at[dp], own_sem.at[0])
-    keep_w.start()
-
-    def to_plane(rows, land, send, recv, group, k):
-        peer = lax.rem(ex + k, ne)
-        return remote(
-            rows.at[group, pl.ds(pl.multiple_of(peer * cap_pad, 16), cap_pad)], land.at[group, ex],
-            send.at[group, k], recv.at[group, k], (dp, peer),
-        )
-
-    def kept(rows, land, group, sem):
-        return pltpu.make_async_copy(
-            rows.at[group, pl.ds(pl.multiple_of(ex * cap_pad, 16), cap_pad)], land.at[group, ex], sem.at[group, 0]
-        )
-
-    def dispatch(group, tokens, rows, land, send, recv, weigh):
-        meta = meta_all[group]
-        ids = lax.broadcasted_iota(jnp.int32, (slots_n, block), 0).astype(F32)
-        hit_a, hit_b = ids == meta[0:1, :], ids == meta[1:2, :]
-        chosen = jnp.where(hit_a | hit_b, 1.0, 0.0).astype(BF16)
-        found = mm(chosen, tokens)
-        if weigh:
-            gate = meta[2:3, :]
-            factor = jnp.sum(
-                jnp.where(hit_a, gate, 0.0) + jnp.where(hit_b, 1.0 - gate, 0.0), axis=1, keepdims=True
-            )
-            found = found * factor
-        rows[group] = found.astype(BF16)
-        for k in range(1, ne):
-            to_plane(rows, land, send, recv, group, k).start()
-        kept(rows, land, group, send).start()
-
-    def send_cot(group, tokens):
-        dispatch(group, tokens, cot_rows, d_outs, pc_send, pc_recv, True)
-
-    send_cot(dp, cot[...])
-
-    @pl.loop(0, n)
-    def _(j):
+    if n > 2:
+        x_hop(1)
+    for kind in range(4):
+        settle(kind)
+    stores.start(5, 6, 7)
+
+    devices = n * ne
+    shared = jnp.max(lext[...].astype(F32), axis=2).reshape(devices, own).astype(BF16)
+
+    def laid_out(first_lane, count, total):
+        lanes = lax.broadcasted_iota(jnp.int32, (own, total), 1)
+        rows = lax.broadcasted_iota(jnp.int32, (own, total), 0)
+        spreading = jnp.where(lax.rem(lanes, count) + first_lane == rows, 1.0, 0.0).astype(BF16)
+        everywhere = mm(shared, spreading)
+        owner = lax.broadcasted_iota(jnp.int32, (devices, total), 0)
+        lane_owner = lax.broadcasted_iota(jnp.int32, (devices, total), 1) // count
+        return jnp.sum(jnp.where(owner == lane_owner, everywhere, 0.0), axis=0, keepdims=True)
+
+    gain_one = laid_out(0, n_gain, width)
+    gain_two = laid_out(n_gain, n_gain, width)
+    gains[...] = jnp.concatenate([gain_one, gain_two, jnp.zeros((6, width), F32)], axis=0)
+    entries = HEADS * BUCKETS
+    flat = laid_out(2 * n_gain, n_bias, entries)
+    lanes = lax.broadcasted_iota(jnp.int32, (8, entries), 1)
+    head_of = lax.broadcasted_iota(jnp.int32, (8, entries), 0) + dp * (HEADS // n)
+    by_head = jnp.where(lax.rem(lanes, HEADS) == head_of, jnp.broadcast_to(flat, (8, entries)), 0.0).astype(BF16)
+    bucket_rows = lax.broadcasted_iota(jnp.int32, (entries, 128), 0) // HEADS
+    to_bucket = jnp.where(
+        bucket_rows == lax.broadcasted_iota(jnp.int32, (entries, 128), 1), 1.0, 0.0
+    ).astype(BF16)
+    table = mm(by_head, to_bucket).astype(BF16)
+    wide = vectors.shape[1]
+    vectors[...] = mm(table, bucket_hot(wide, 0, wide // 2), NT)
+
+    def project(j):
         at = pl.ds(pl.multiple_of(j * block, block), block)
         xf = x_all[j].astype(F32)
         inverse = lax.rsqrt(jnp.mean(xf * xf, axis=-1, keepdims=True) + EPSILON)
-        low = (xf * inverse * gain_one[...]).astype(BF16)
+        low = (xf * inverse * gains[0:1, :]).astype(BF16)
         normed[at, :] = low
-        for w, ref in enumerate((wq, wk, wv)):
-            qkv[at, w * own : (w + 1) * own] = mm(low, ref[...]).astype(BF16)
+        for w, ref in enumerate((lq, lk, lv)):
+            qkv[at, w * own : (w + 1) * own] = mm(low, rows_flat(ref)).astype(BF16)
+
+    project(dp)
+
+    def project_hop(h):
+        @pl.loop(0, 2)
+        def _(side):
+            @pl.when(((side == 0) & (dp > h)) | ((side == 1) & (dp + 1 + h < n)))
+            def _():
+                project(chain.block(h + 1, side))
+
+    for h in range(n - 2):
+        project_hop(h)
+    pass_on(4)
+    x_hop(n - 2)
+    cots.start()
+    keep_w.start()
+
+    def send_weights(to_ends):
+        for d in range(1, n):
+            t = lax.rem(dp + d, n)
+            at_end = (t == 0) | (t == n - 1)
+
+            @pl.when(at_end if to_ends else jnp.logical_not(at_end))
+            def _():
+                weights(d).start()
+
+    send_weights(False)
+    project_hop(n - 2)
+    stores.start(0, 1)
 
     def attend(pair):
         for side in range(2):
@@ -425,24 +476,11 @@
             heads[at, pair * 128 : (pair + 1) * 128] = jnp.where(low_half, outs[0], outs[1]).astype(BF16)
             lse[at, pair * 128 : (pair + 1) * 128] = jnp.where(low_half, logs[0], logs[1])
 
-    def hop(chain, h, then):
-        for side in range(2):
-            @pl.when(chain.held(h, side))
-            def _():
-                then(chain.arrive(h, side))
-
     def cot_hop(h):
         hop(cots, h, lambda group: send_cot(group, cot_all[group]))
 
-    cot_hop(0)
-    for d in range(1, n):
-        weights(d).start()
-    attend(0)
-    if n > 2:
-        cot_hop(1)
-    for pair in range(1, pairs_n):
-        attend(pair)
-
+    for d in range(1, n):
+        line(5, d).wait_recv()
     def give(d):
         t = lax.rem(dp + d, n)
         return remote(
@@ -450,28 +488,39 @@
             (t, ex),
         )
 
-    for d in range(1, n):
-        give(d).start()
+    for pair in range(pairs_n):
+        attend(pair)
+        if pair == pairs_n - 1:
+            for d in range(1, n):
+                give(d).start()
+        if pair < n - 1:
+            cot_hop(pair)
     mixed_in[dp] = heads[pl.ds(pl.multiple_of(dp * block, block), block), :]
-    for h in range(2, n - 1):
-        cot_hop(h)
+    settle(4)
+    stores.start(8, 2)
     for d in range(1, n):
         give(d).wait()
     mixed[...] = jnp.concatenate([mixed_in[j] for j in range(n)], axis=1)
-    total = x_all[dp].astype(F32) + mm(mixed[...], wo[...])
+    total = x[...].astype(F32) + mm(mixed[...], rows_flat(lwo))
     resid[...] = total
     inverse = lax.rsqrt(jnp.mean(total * total, axis=-1, keepdims=True) + EPSILON)
-    two_own[...] = (total * inverse * gain_two[...]).astype(BF16)
+    two_own[...] = (total * inverse * gains[1:2, :]).astype(BF16)
     twos.start()
-
-    def send_two(group, tokens):
-        dispatch(group, tokens, two_rows, slots, pt_send, pt_recv, False)
+    stores.start(3, 4)
 
     send_two(dp, two_own[...])
+    for h in range(pairs_n, n - 1):
+        cot_hop(h)
     for h in range(n - 1):
         hop(twos, h, lambda group: send_two(group, two_all[group]))
+    send_weights(True)
+    stores.wait(*range(9))
+    chain.finish()
     cots.finish()
     twos.finish()
+    for d in range(1, n):
+        for kind in range(6):
+            line(kind, d).wait_send()
     keep_w.wait()
     for d in range(1, n):
         weights(d).wait()
@@ -485,28 +534,60 @@
                 to_plane(rows, land, send, recv, group, k).wait()
 
 
-def forward(n, ne, cap_pad, x_all, wq, wk, wv, wo, gain_one, gain_two, vectors, cot, meta_all, packed):
-    tok, width = cot.shape
-    own = wq.shape[1]
-    wide = vectors.shape[1]
-    both = packed.shape[2]
+def front(n, ne, cap, cap_pad, x, wq, wk, wv, wo, gain_attn, gain_moe, position_bias, meta_in, wg, wu, cot):
+    tok, width = x.shape
+    wrows = wq.shape[0]
+    own = width // n
+    piece = wg.shape[1] // n
+    wide = 2 * n * tok
     slots_n = ne * cap_pad
     sem = pltpu.SemaphoreType.DMA
+    shape = jax.ShapeDtypeStruct
     return pl.pallas_call(
-        functools.partial(forward_kernel, n, ne, cap_pad),
-        in_specs=[VM] * 10 + [ANY],
-        out_specs=[VM] * 5 + [ANY] * 3,
+        functools.partial(front_kernel, n, ne, cap, cap_pad, piece),
+        in_specs=[ANY] + [VM] * 8 + [ANY] * 3,
+        out_specs=[ANY] * 9 + [VM] * 3 + [ANY] * 3,
         out_shape=[
-            jax.ShapeDtypeStruct((n * tok, width), BF16),
-            jax.ShapeDtypeStruct((n * tok, 3 * own), BF16),
-            jax.ShapeDtypeStruct((n * tok, own), F32),
-            jax.ShapeDtypeStruct((tok, width), BF16),
-            jax.ShapeDtypeStruct((tok, width), F32),
-            jax.ShapeDtypeStruct((n, ne, cap_pad, width), BF16),
-            jax.ShapeDtypeStruct((n, ne, cap_pad, width), BF16),
-            jax.ShapeDtypeStruct((n, tok, both), BF16),
+            shape((n * tok, width), BF16),
+            shape((n * tok, 3 * own), BF16),
+            shape((n * tok, own), F32),
+            shape((tok, width), BF16),
+            shape((tok, width), F32),
+            shape((n, ne, wrows, own), BF16),
+            shape((n, ne, wrows, own), BF16),
+            shape((n, ne, wrows, own), BF16),
+            shape((n, ne, wrows, width), BF16),
+            shape((n, 8, tok), F32),
+            shape((8, wide), F32),
+            shape((8, width), F32),
+            shape((n, ne, cap_pad, width), BF16),
+            shape((n, ne, cap_pad, width), BF16),
+            shape((n, tok, 2 * piece), BF16),
         ],
         scratch_shapes=[
+            pltpu.VMEM((tok, width), BF16),
+            pltpu.VMEM(wg.shape, BF16),
+            pltpu.VMEM(wu.shape, BF16),
+            pltpu.VMEM((tok, width), BF16),
+            pltpu.VMEM((n * tok, width), BF16),
+            pltpu.VMEM((n * tok, 3 * own), BF16),
+            pltpu.VMEM((n * tok, own), F32),
+            pltpu.VMEM((tok, width), BF16),
+            pltpu.VMEM((tok, width), F32),
+            pltpu.VMEM((n, ne, wrows, own), BF16),
+            pltpu.VMEM((n, ne, wrows, own), BF16),
+            pltpu.VMEM((n, ne, wrows, own), BF16),
+            pltpu.VMEM((n, ne, wrows, width), BF16),
+            pltpu.VMEM((16, own), BF16),
+            pltpu.VMEM((n, wrows, own), BF16),
+            pltpu.VMEM((n, wrows, own), BF16),
+            pltpu.VMEM((n, wrows, own), BF16),
+            pltpu.VMEM((n, 16, own), BF16),
+            pltpu.VMEM((n, wrows, width), BF16),
+            pltpu.VMEM((8, tok), F32),
+            pltpu.VMEM((n, ne, 16, own), BF16),
+            pltpu.VMEM((n, tok, 2 * piece), BF16),
+            pltpu.VMEM((n, tok, width), BF16),
             pltpu.VMEM((n * tok, own), BF16),
             pltpu.VMEM((n, tok, own), BF16),
             pltpu.VMEM((2, tok, wide), F32),
@@ -515,24 +596,26 @@
             pltpu.VMEM((tok, width), BF16),
             pltpu.VMEM((n, slots_n, width), BF16),
             pltpu.VMEM((n, slots_n, width), BF16),
+            sem((6, n)), sem((6, n)),
+            sem((5, ne // 2)), sem((5, ne // 2)), sem((5, ne // 2)), sem((5, ne // 2)),
+            sem((n, 2)), sem((n, 2)), sem((6,)),
             sem((n,)), sem((n,)), sem((n,)), sem((n,)),
             sem((n, 2)), sem((n, 2)), sem((n, 2)), sem((n, 2)),
-            sem((n, ne)), sem((n, ne)), sem((n, ne)), sem((n, ne)),
-            sem((1,)),
+            sem((n, ne)), sem((n, ne)), sem((n, ne)), sem((n, ne)), sem((4,)), sem((9,)),
         ],
         compiler_params=pltpu.CompilerParams(
-            collective_id=2, has_side_effects=True, vmem_limit_bytes=VMEM_LIMIT
+            collective_id=1, has_side_effects=True, vmem_limit_bytes=60 * 1024 * 1024
         ),
-        name="forward",
-    )(x_all, wq, wk, wv, wo, gain_one, gain_two, vectors, cot, meta_all, packed)
+        name="front",
+    )(x, wq, wk, wv, wo, gain_attn, gain_moe, position_bias, meta_in, wg, wu, cot)
 
 
 def experts_kernel(
     n, ne, cap_pad, deep, main,
-    slots, d_outs, wgu_ref, wd_ref, meta_all,
-    out_rows, d_two, gwgu, gwd,
-    s_buf, d_buf, back, part, landed, gwgu_acc,
-    load_sem, keep_sem, p_send, p_recv, z_send, z_recv,
+    slots, d_outs, wgu_in, wd_in, meta_all,
+    out_rows, d_two, gwgu_out, gwd_out,
+    wgu_ref, gwgu, gwd, wd_ref, s_buf, d_buf, back, part, landed, gwgu_acc,
+    load_sem, keep_sem, p_send, p_recv, z_send, z_recv, wd_sem,
 ):
     dp, ex = lax.axis_index("dp"), lax.axis_index("expert")
     slots_n, width = s_buf.shape[1:]
@@ -548,11 +631,19 @@
         src, dst = ((slots, s_buf), (d_outs, d_buf))[kind]
         return pltpu.make_async_copy(src.at[at], dst.at[at], load_sem.at[kind, step])
 
+    whole = Copies(
+        wd_sem,
+        [(wgu_in, wgu_ref), (wd_in, wd_ref.at[pl.ds(0, deep)]), (gwgu, gwgu_out), (gwd, gwd_out)],
+    )
+    whole.start(0, 1)
     for step in range(n):
         for kind in range(2):
             load(step, kind).start()
+    wd_ref[deep:, :] = jnp.zeros((wd_ref.shape[0] - deep, width), BF16)
     gwgu_acc[...] = jnp.zeros_like(gwgu_acc)
     gwd[...] = jnp.zeros_like(gwd)
+    whole.wait(0, 1)
+    meet(n, ne)
 
     def rows_of(peer):
         return pl.ds(pl.multiple_of(peer * cap_pad, 16), cap_pad)
@@ -626,12 +717,14 @@
             owed(past).start()
 
     gwgu[...] = gwgu_acc[...].astype(BF16)
+    whole.start(2, 3)
     total = combine(dp)
     for d in range(1, n):
         src = lax.rem(dp + d, n)
         remote(part.at[src], landed.at[src], z_send.at[src], z_recv.at[src], (src, ex)).wait_recv()
         total = total + landed[src].astype(F32)
     d_two[...] = total
+    whole.wait(2, 3)
     for d in range(1, n):
         owed(lax.rem(dp + d, n)).wait_send()
 
@@ -652,8 +745,8 @@
     sem = pltpu.SemaphoreType.DMA
     return pl.pallas_call(
         functools.partial(experts_kernel, n, ne, cap_pad, deep, main),
-        in_specs=[ANY, ANY, VM, VM, VM],
-        out_specs=[ANY, VM, VM, VM],
+        in_specs=[ANY, ANY, ANY, ANY, VM],
+        out_specs=[ANY, VM, ANY, ANY],
         out_shape=[
             jax.ShapeDtypeStruct((n, slots_n, width), BF16),
             jax.ShapeDtypeStruct((tok, width), F32),
@@ -661,13 +754,17 @@
             jax.ShapeDtypeStruct((deep, width), F32),
         ],
         scratch_shapes=[
+            pltpu.VMEM((width, columns), BF16),
+            pltpu.VMEM((width, columns), BF16),
+            pltpu.VMEM((deep, width), F32),
+            pltpu.VMEM((-(-deep // 128) * 128, width), BF16),
             pltpu.VMEM((n, slots_n, width), BF16),
             pltpu.VMEM((n, slots_n, width), BF16),
             pltpu.VMEM((n, slots_n, width), BF16),
             pltpu.VMEM((n, tok, width), BF16),
             pltpu.VMEM((n, tok, width), BF16),
             pltpu.VMEM((width, columns), F32),
-            sem((2, n)), sem((n,)), sem((n, ne)), sem((n, ne)), sem((n,)), sem((n,)),
+            sem((2, n)), sem((n,)), sem((n, ne)), sem((n, ne)), sem((n,)), sem((n,)), sem((4,)),
         ],
         compiler_params=pltpu.CompilerParams(
             collective_id=3, has_side_effects=True, vmem_limit_bytes=60 * 1024 * 1024
@@ -678,15 +775,17 @@
 
 def backward_kernel(
     n, ne, cap_pad,
-    d_two, resid, cot, x, gain_one, gain_two, mixed, wo, qkv, lse, normed, vectors, wq, wk, wv, meta_all, in_bucket,
+    gains, vectors, meta_all,
+    d_two_in, resid_in, cot_in, wo_in, x_in, mixed_in, qkv_in, lse_in, normed_in, wq_in, wk_in, wv_in,
     gwgu, out_rows,
     block_out, grad_in, g_all, small_all, gw_in, out_in,
+    d_two, resid, cot, wo, x, mixed, qkv, lse, normed, wq, wk, wv,
     dm, dm_in, tiles, sums, dq_s, dk_s, dv_s, dk_acc, dv_acc, diag, d_res,
     dn_part, dn_land, moe_part, moe_land, out_one,
     g_send, g_land, g2_send, g2_land, o_send, o_land, o2_send, o2_land,
     small_own, small_land, small_sum,
     out_s, out_r, w_s, w_r, dm_s, dm_r, dn_s, dn_r, moe_s, moe_r, g_s, g_r, o_s, o_r, g2_s, g2_r, o2_s, o2_r,
-    sp_s, sp_r, sz_s, sz_r, keep_sem,
+    sp_s, sp_r, sz_s, sz_r, keep_sem, in_sem,
 ):
     dp, ex = lax.axis_index("dp"), lax.axis_index("expert")
     tok, width = cot.shape
@@ -695,6 +794,14 @@
     slots_n = ne * cap_pad
     wrows = g_all.shape[1]
     greet(n, ne, dp, ex)
+    loads = Copies(
+        in_sem,
+        [
+            (d_two_in, d_two), (resid_in, resid), (cot_in, cot), (wo_in, wo), (x_in, x), (mixed_in, mixed),
+            (qkv_in, qkv), (lse_in, lse), (normed_in, normed), (wq_in, wq), (wk_in, wk), (wv_in, wv),
+        ],
+    )
+    loads.start(0, 1, 2, 3, 5, 6, 7, 9, 10, 11, 8, 4)
     toward = 2 * ((2 * dp) // n) - 1
 
     def group_at(step):
@@ -731,16 +838,19 @@
     def out_keep(at):
         return pltpu.make_async_copy(out_rows.at[at, rows_of(ex)], out_in.at[at, rows_of(ex)], out_s.at[at, 0])
 
+    loads.wait(0, 1, 2)
     values = resid[...]
     d_normed = d_two[...]
     inverse = lax.rsqrt(jnp.mean(values * values, axis=-1, keepdims=True) + EPSILON)
-    scaled = gain_two[...] * d_normed
+    scaled = gains[1:2, :] * d_normed
     gain_rows_two = jnp.sum(d_normed * values * inverse, axis=0, keepdims=True)
     mean = jnp.mean(scaled * values, axis=-1, keepdims=True)
     d_resid = cot[...].astype(F32) + inverse * scaled - values * (inverse * inverse * inverse * mean)
     d_res[...] = d_resid
     d_attn = d_resid.astype(BF16)
+    loads.wait(3)
     d_mixed = mm(d_attn, wo[...], NT).astype(BF16)
+    meet(n, ne)
     for j in range(n):
         dm[j] = d_mixed[:, j * own : (j + 1) * own]
     for d in range(1, n):
@@ -758,6 +868,7 @@
             out_give(at, k).start()
         out_keep(at).start()
 
+    loads.wait(5)
     o_send[...] = mm(mixed[...], d_attn, TN).reshape(n, ne, wrows, width).astype(BF16)
     for k in range(1, ne):
         to_plane(o_send.at[:, lax.rem(ex + k, ne)], o_land, o_s, o_r, k).start()
@@ -767,6 +878,7 @@
     for d in range(1, n):
         from_line(dm, dm_in, dm_s, dm_r, lax.rem(dp + d, n)).wait_recv()
 
+    loads.wait(6, 7, 9, 10, 11)
     lane = lax.broadcasted_iota(jnp.int32, (tok, 128), 1)
     low_half = lane < HEAD_DIM
     key_low = lax.broadcasted_iota(jnp.int32, (n * tok, 128), 1) < HEAD_DIM
@@ -874,6 +986,7 @@
     moes = (moe_part, moe_land, moe_s, moe_r)
     sum_round(*dn, d_norm, 1)
 
+    loads.wait(8, 4)
     for w, ref in enumerate((dq_s, dk_s, dv_s)):
         g_send[:, :, w] = mm(normed[...], ref[...], TN).reshape(n, ne, wrows, own).astype(BF16)
     for k in range(1, ne):
@@ -885,9 +998,11 @@
 
     rest = diag[...]
     table = jnp.zeros((8, 128), F32)
+    wide = vectors.shape[1]
+    hot = bucket_hot(wide, tok, wide // 2)
     for _ in range(3):
         piece = rest.astype(BF16)
-        table = table + mm(piece, in_bucket[...])
+        table = table + mm(piece, hot)
         rest = rest - piece.astype(F32)
     small_own[16:24, :] = table
 
@@ -930,7 +1045,7 @@
     total = sum_end(*dn, d_norm(dp))
     values = x[...].astype(F32)
     inverse = lax.rsqrt(jnp.mean(values * values, axis=-1, keepdims=True) + EPSILON)
-    scaled = gain_one[...] * total
+    scaled = gains[0:1, :] * total
     gain_rows_one = jnp.sum(total * values * inverse, axis=0, keepdims=True)
     mean = jnp.mean(scaled * values, axis=-1, keepdims=True)
     grad_in[...] = (d_res[...] + inverse * scaled - values * (inverse * inverse * inverse * mean)).astype(BF16)
@@ -987,8 +1102,8 @@
 
 
 def backward(
-    n, ne, cap_pad, wrows, d_two, resid, cot, x, gain_one, gain_two, mixed, wo, qkv, lse, normed, vectors,
-    wq, wk, wv, meta_all, in_bucket, gwgu, out_rows,
+    n, ne, cap_pad, wrows, d_two, resid, cot, x, gains, mixed, wo, qkv, lse, normed, vectors,
+    wq, wk, wv, meta_all, gwgu, out_rows,
 ):
     tok, width = cot.shape
     own = wq.shape[1]
@@ -1000,7 +1115,7 @@
     shape = jax.ShapeDtypeStruct
     return pl.pallas_call(
         functools.partial(backward_kernel, n, ne, cap_pad),
-        in_specs=[VM] * 17 + [ANY] * 2,
+        in_specs=[VM] * 3 + [ANY] * 14,
         out_specs=[VM] * 4 + [ANY] * 2,
         out_shape=[
             shape((tok, width), BF16),
@@ -1011,6 +1126,18 @@
             shape((n, slots_n, width), BF16),
         ],
         scratch_shapes=[
+            pltpu.VMEM((tok, width), F32),
+            pltpu.VMEM((tok, width), F32),
+            pltpu.VMEM((tok, width), BF16),
+            pltpu.VMEM((width, width), BF16),
+            pltpu.VMEM((tok, width), BF16),
+            pltpu.VMEM((tok, width), BF16),
+            pltpu.VMEM((length, 3 * own), BF16),
+            pltpu.VMEM((length, own), F32),
+            pltpu.VMEM((length, width), BF16),
+            pltpu.VMEM((width, own), BF16),
+            pltpu.VMEM((width, own), BF16),
+            pltpu.VMEM((width, own), BF16),
             pltpu.VMEM((n, tok, own), BF16),
             pltpu.VMEM((n, tok, own), BF16),
             pltpu.VMEM((2, tok, wide), F32),
@@ -1040,15 +1167,14 @@
             pltpu.VMEM((24, 128), F32),
             sem((n, ne)), sem((n, ne)), sem((n,)), sem((n,)), sem((n,)), sem((n,)), sem((n, 2)), sem((n, 2)),
             sem((n, 2)), sem((n, 2)), sem((ne,)), sem((ne,)), sem((ne,)), sem((ne,)), sem((n,)), sem((n,)),
-            sem((n,)), sem((n,)), sem((ne,)), sem((ne,)), sem((n,)), sem((n,)), sem((2,)),
+            sem((n,)), sem((n,)), sem((ne,)), sem((ne,)), sem((n,)), sem((n,)), sem((2,)), sem((12,)),
         ],
         compiler_params=pltpu.CompilerParams(
             collective_id=4, has_side_effects=True, vmem_limit_bytes=60 * 1024 * 1024
         ),
         name="backward",
     )(
-        d_two, resid, cot, x, gain_one, gain_two, mixed, wo, qkv, lse, normed, vectors, wq, wk, wv, meta_all,
-        in_bucket, gwgu, out_rows,
+        gains, vectors, meta_all, d_two, resid, cot, wo, x, mixed, qkv, lse, normed, wq, wk, wv, gwgu, out_rows
     )
 
 
@@ -1162,41 +1288,23 @@
     slots_n = experts_n * cap_pad
 
     n_gain, n_bias = gain_attn.shape[0], position_bias.shape[0]
-    extra = jnp.concatenate([gain_attn, gain_moe, position_bias])
-    extra = jnp.zeros((16, own), BF16).at[0, : 2 * n_gain + n_bias].set(extra)
     meta_in = jnp.concatenate([routes[0].T, gate_fixed], axis=0)
-    x_all, wq, wk, wv, extras, wo, meta_all, packed = start(
-        n, experts_n, capacity, cap_pad,
-        inputs[0], w_query, w_key, w_value, extra, w_out, meta_in, w_gate[0], w_up[0],
+    normed, qkv, lse, mixed, resid, wq, wk, wv, wo, meta_all, vectors, gains, slots, d_outs, wgu = front(
+        n, experts_n, capacity, cap_pad, inputs[0], w_query, w_key, w_value, w_out,
+        gain_attn.reshape(1, -1), gain_moe.reshape(1, -1), position_bias.reshape(1, -1),
+        meta_in, w_gate[0], w_up[0], cotangent[0],
     )
     wq, wk, wv = (w.reshape(width, own) for w in (wq, wk, wv))
     wo = wo.reshape(width, width)
-    extras = extras[:, :, 0]
-    gain_one = extras[:, :, :n_gain].reshape(1, -1).astype(F32)
-    gain_two = extras[:, :, n_gain : 2 * n_gain].reshape(1, -1).astype(F32)
-    table = extras[:, :, 2 * n_gain : 2 * n_gain + n_bias].reshape(BUCKETS, HEADS)
-    table = lax.dynamic_slice_in_dim(table, dp * heads_own, heads_own, 1)
-    wide = 2 * length
-    offsets = jnp.arange(wide, dtype=jnp.int32) - length
-    in_bucket = (bucket_of(offsets)[:, None] == jnp.arange(BUCKETS, dtype=jnp.int32)).astype(BF16)
-    in_bucket = jnp.where(jnp.abs(offsets)[:, None] < length, in_bucket, jnp.zeros_like(in_bucket))
-    vectors = mm(table, in_bucket, (((0,), (1,)), ((), ())))
-
-    normed, qkv, lse, mixed, resid, slots, d_outs, wgu = forward(
-        n, experts_n, cap_pad, x_all, wq, wk, wv, wo, gain_one, gain_two, vectors, cotangent[0], meta_all, packed
-    )
     wgu = wgu.reshape(width, -1)
     deep = w_down.shape[1]
-    padded = -(-deep // 128) * 128
-    wd = jnp.pad(w_down[0], ((0, padded - deep), (0, 0)))
     out_rows, grad_normed_two, gwgu, grad_w_down = experts(
-        n, experts_n, cap_pad, deep, slots, d_outs, wgu, wd, meta_all
+        n, experts_n, cap_pad, deep, slots, d_outs, wgu, w_down[0], meta_all
     )
 
-    by_diagonal = jnp.pad(jnp.roll(in_bucket, -tok, axis=0), ((0, 0), (0, 128 - BUCKETS)))
     block_out, grad_inputs, g_all, small, got, _ = backward(
-        n, experts_n, cap_pad, wrows, grad_normed_two, resid, cotangent[0], inputs[0], gain_one, gain_two, mixed, wo,
-        qkv, lse, normed, vectors, wq, wk, wv, meta_all, by_diagonal, gwgu.reshape(n, width // n, -1), out_rows,
+        n, experts_n, cap_pad, wrows, grad_normed_two, resid, cotangent[0], inputs[0], gains, mixed, wo,
+        qkv, lse, normed, vectors, wq, wk, wv, meta_all, gwgu.reshape(n, width // n, -1), out_rows,
     )
     (
         grad_w_gate, grad_w_up, gq, gk, gv, go, grad_gain_one, grad_gain_two, grad_bias, block_out, grad_inputs,

time: 482 us -> 448 us (0.929)
  Pallas kernels: 464 us -> 441 us
  local copies, waits for them, and re-layouts: 5.43 us -> 0 us
    pallas_call x2 -> x1, Pallas kernels: 224 us -> 205 us  [front(): pl.pallas_call(functools.partial(front_kernel, n, ne, cap, cap_pad, piece...]
    pallas_call x1, Pallas kernels: 156 us -> 151 us  [backward(): pl.pallas_call(functools.partial(backward_kernel, n, ne, cap_pad), in_spe...]
where the time goes in v6:
time: 448 us; the launch traced here: 443 us
  Pallas kernels  441 us (98%)
    pallas_call x1, Pallas kernels, front(): pl.pallas_call(functools.partial(front_kernel, n, ne, cap, cap_pad, piece...  205 us
    pallas_call x1, Pallas kernels, backward(): pl.pallas_call(functools.partial(backward_kernel, n, ne, cap_pad), in_spe...  151 us
    pallas_call x1, Pallas kernels, experts(): pl.pallas_call(functools.partial(experts_kernel, n, ne, cap_pad, deep, ma...  77.5 us

profile of v6, /device:TPU:0, one launch (start us, length us, event | category | flops | bytes accessed | tf_op | source)
XLA Modules:
  0.0 443.2 jit_solution(2838046660349648617)
XLA Ops:
  0.6 1.3 pad_add_fusion.meta_in
  1.9 204.9 %front.1 = (bf16[1024,1024]{1,0:T(8,128)(2,1)}, bf16[1024,768]{1,0:T(8,128)(2,1)}, f32[1024,256]{1,0:T(8,128)}, bf16[256,1024]{1,0:T(8,128)(2,1)}, f32[256,1024]...) custom-call(bf16[256,1024]{1,0:T(8,128)(2,1)} %bitcast.32, ...), custom_call_target="tpu_custom_call" | custom-call | tf_op jit(solution)/shard_map/front/pallas_call | solution.py:546
  206.9 77.5 %experts.1 = (bf16[4,640,1024]{2,1,0:T(8,128)(2,1)}, f32[256,1024]{1,0:T(8,128)}, bf16[1024,1408]{1,0:T(8,128)(2,1)}, f32[704,1024]{1,0:T(8,128)}) custom-call(bf16[4,640,1024]{2,1,0:T(8,128)(2,1)} %bitcast.27, bf16[4,640,1024]{2,1,0:T(8,128)(2,1)} %bitcast.28, bf16[1024,1408]{1,0:T(8,128)(2,1)} %bitcast.30, bf16[704,1024]{1,0:T(8,128)(2,1)} %bitcast.36, ...), custom_call_target="tpu_custom_call" | custom-call | tf_op jit(solution)/shard_map/experts/pallas_call | solution.py:746
  284.4 150.8 %backward.1 = (bf16[256,1024]{1,0:T(8,128)(2,1)}, bf16[256,1024]{1,0:T(8,128)(2,1)}, f32[4,32,1024]{2,1,0:T(8,128)}, f32[4,24,128]{2,1,0:T(8,128)}, bf16[4,256,1...) custom-call(f32[8,1024]{1,0:T(8,128)} %get-tuple-element.48.gains, f32[8,2048]{1,0:T(8,128)} %get-tuple-element.49.vectors, ...), custom_call_target="tpu_custom_call" | custom-call | tf_op jit(solution)/shard_map/backward/pallas_call | solution.py:1116
  435.2 7.7 %finish.1 = (f32[256,2816]{1,0:T(8,128)}, f32[256,2816]{1,0:T(8,128)}, f32[32,1024]{1,0:T(8,128)}, f32[32,1024]{1,0:T(8,128)}, f32[32,1024]{1,0:T(8,128)}, /*ind...) custom-call(bf16[4,256,1408]{2,1,0:T(8,128)(2,1)} %get-tuple-element, ...), custom_call_target="tpu_custom_call" | custom-call | tf_op jit(solution)/shard_map/finish/pallas_call | solution.py:1245
